TPU v7x, 32 devices: a whole 2x2x4 slice. The times are simulated.
32 devices in a mesh: grp: 2 (over y), row: 4 (over z), col: 4 (over x, core).
Axes of the slice: x: 2, y: 2, z: 4, core: 2. Of those that a mesh axis runs over, the one named last changes fastest.
Arguments:
- inputs: bfloat16 [256, 16384], P(('grp', 'row'), 'col'), parts along dimension 0, may hold values from -6 to 6
- output_gradient: bfloat16 [256, 16384], P(('grp', 'row'), 'col'), parts along dimension 0, may hold values from -6 to 6
- gate_preactivation: bfloat16 [256, 8192], P('grp', 'row'), parts along dimension 0, may hold values from -6 to 6
- up_preactivation: bfloat16 [256, 8192], P('grp', 'row'), parts along dimension 0, may hold values from -6 to 6
- gate_weight: bfloat16 [16384, 8192], P('col', 'row'), may hold values from -0.046875 to 0.046875
- up_weight: bfloat16 [16384, 8192], P('col', 'row'), may hold values from -0.046875 to 0.046875
- down_weight: bfloat16 [8192, 16384], P('row', 'col'), may hold values from -0.0625 to 0.0625
- up_adapter_entry: bfloat16 [16, 16384], P(None, 'col'), may hold values from -6 to 6
- up_adapter_exit: bfloat16 [16, 8192], P(None, 'row'), may hold values from -0.0032958984 to 0.0032958984
- down_adapter_entry: bfloat16 [16, 8192], P(None, 'row'), may hold values from -6 to 6
- down_adapter_exit: bfloat16 [16, 16384], P(None, 'col'), may hold values from -0.0023956299 to 0.0023956299
- up_adapter_activations: bfloat16 [16, 256], P(None, 'grp'), parts along dimension 1, may hold values from -0.29882812 to 0.29882812
- down_adapter_activations: bfloat16 [16, 256], P(None, 'grp'), parts along dimension 1, may hold values from -0.29882812 to 0.29882812
Outputs:
- grad_inputs: bfloat16 [256, 16384], P(('grp', 'row'), 'col'), parts along dimension 0
- up_entry_gradient: float32 [32, 16384], P('grp', 'col'), parts along dimension 0
- up_exit_gradient: float32 [32, 8192], P('grp', 'row'), parts along dimension 0
- down_entry_gradient: float32 [32, 8192], P('grp', 'row'), parts along dimension 0
- down_exit_gradient: float32 [32, 16384], P('grp', 'col'), parts along dimension 0
There are 2 independent parts, one for each index of `grp`. A program takes and returns all parts, laid end to end along the dimension named above; an argument that names none is the same for every part. Nothing has to cross between parts.
All inputs are finite; a program needn't handle non-finite values.
Results may differ from a plain program's by a relative error of at most 0.005.
Values may be sent and summed in bfloat16 or wider, within the bound.
No kernel may reach another device: no remote copies, remote signals or barrier semaphores. Data moves between devices by JAX's collectives and lax.ppermute only.
A program may use at most 128 MiB of HBM per device.

v0:
```python
import jax
import jax.numpy as jnp
from jax import lax
from jax.sharding import PartitionSpec as P

adapter_scale = 2.0


def contract_trailing(left, right):
    return lax.dot_general(
        left, right, (((1,), (1,)), ((), ())), preferred_element_type=jnp.float32
    )


def contract_leading(left, right, matmul_accuracy=None):
    return lax.dot_general(
        left,
        right,
        (((0,), (0,)), ((), ())),
        precision=matmul_accuracy,
        preferred_element_type=jnp.float32,
    )


def body(
    inputs,
    output_gradient,
    gate_preactivation,
    up_preactivation,
    gate_weight,
    up_weight,
    down_weight,
    up_adapter_entry,
    up_adapter_exit,
    down_adapter_entry,
    down_adapter_exit,
    up_adapter_activations,
    down_adapter_activations,
):
    highest_setting = lax.Precision.HIGHEST
    complete_gradient = lax.all_gather(output_gradient, "row", axis=0, tiled=True)
    down_piece = contract_trailing(complete_gradient, down_adapter_exit)
    hidden_piece = contract_trailing(complete_gradient, down_weight)
    hidden_piece = hidden_piece + adapter_scale * jnp.dot(
        down_piece, down_adapter_entry.astype(jnp.float32), precision=highest_setting
    )
    hidden_gradient, down_full = lax.psum((hidden_piece, down_piece), "col")
    gate_f = gate_preactivation.astype(jnp.float32)
    up_f = up_preactivation.astype(jnp.float32)
    sigmoid_gate = jax.nn.sigmoid(gate_f)
    hidden_state = (gate_f * sigmoid_gate * up_f).astype(jnp.bfloat16)
    gate_grad = (
        hidden_gradient * up_f * sigmoid_gate * (1.0 + gate_f * (1.0 - sigmoid_gate))
    ).astype(jnp.bfloat16)
    up_gradient = (hidden_gradient * gate_f * sigmoid_gate).astype(jnp.bfloat16)
    down_rounded_value = down_full.astype(jnp.bfloat16)
    upper_piece = contract_trailing(up_gradient, up_adapter_exit)
    input_piece = contract_trailing(gate_grad, gate_weight) + contract_trailing(
        up_gradient, up_weight
    )
    input_piece = input_piece + adapter_scale * jnp.dot(
        upper_piece, up_adapter_entry.astype(jnp.float32), precision=highest_setting
    )
    input_grad, upper_full = (
        lax.psum_scatter(input_piece, "row", scatter_dimension=0, tiled=True),
        lax.psum_scatter(upper_piece, "row", scatter_dimension=0, tiled=True),
    )
    up_entry_term = adapter_scale * contract_leading(
        upper_full, inputs.astype(jnp.float32), matmul_accuracy=highest_setting
    )
    up_entry_gradient = lax.psum(up_entry_term, "row")
    up_exit_gradient = adapter_scale * jnp.dot(
        up_adapter_activations, up_gradient, preferred_element_type=jnp.float32
    )
    down_entry_gradient = adapter_scale * contract_leading(down_rounded_value, hidden_state)
    down_exit_gradient = adapter_scale * jnp.dot(
        down_adapter_activations, complete_gradient, preferred_element_type=jnp.float32
    )
    return (
        input_grad.astype(jnp.bfloat16),
        up_entry_gradient,
        up_exit_gradient,
        down_entry_gradient,
        down_exit_gradient,
    )


def solution(mesh):
    placed = (
        P(("grp", "row"), "col"),
        P(("grp", "row"), "col"),
        P("grp", "row"),
        P("grp", "row"),
        P("col", "row"),
        P("col", "row"),
        P("row", "col"),
        P(None, "col"),
        P(None, "row"),
        P(None, "row"),
        P(None, "col"),
        P(None, "grp"),
        P(None, "grp"),
    )
    return jax.shard_map(
        body,
        mesh=mesh,
        in_specs=placed,
        out_specs=(
            P(("grp", "row"), "col"),
            P("grp", "col"),
            P("grp", "row"),
            P("grp", "row"),
            P("grp", "col"),
        ),
        check_vma=False,
    )
```

profile of v0, /device:TPU:0, one launch (start us, length us, event | category | flops | bytes accessed | tf_op | source)
XLA Modules:
  0.0 212.7 jit_solution(2744428697788110122)
XLA Ops:
  7.2 0.0 copy-start
  7.2 0.0 all-gather.2.cloned.1.call-start
  7.3 0.7 all-gather.2.cloned.1.call-update
  8.0 0.0 all-reduce.3.cloned.1.call-start
  8.0 32.3 %all-gather.2.cloned.1.call-done = bf16[128,4096]{1,0:T(8,128)(2,1)} async-done(((bf16[32,4096]{1,0:T(8,128)(2,1)}), bf16[128,4096]{1,0:T(8,128)(2,1)}) %all-gather.2.cloned.1.call-update) | async-done | bytes 1048592 | tf_op jit(solution)/shard_map/all_gather | solution.py:41
  40.3 1.6 fusion.21
  41.9 11.8 %fusion.20 = f32[128,2048]{1,0:T(8,128)S(1)} fusion(bf16[128,4096]{1,0:T(8,128)(2,1)} %all-gather.2.cloned.1.call-done, bf16[2048,4096]{1,0:T(8,128)(2,1)} %param.19), kind=kOutput, calls=%fused_computation.31 | convolution fusion | flops 2147483648 | bytes 18874368 | tf_op jit(solution)/shard_map/dot_general | solution.py:10
  53.7 1.6 fusion.1
  55.3 0.0 all-reduce.3.cloned.1.call-update
  55.3 0.0 reduce-scatter.7.cloned.1.call-start
  55.3 35.7 %all-reduce.3.cloned.1.call-done = f32[128,2048]{1,0:T(8,128)} async-done(((f32[128,2048]{1,0:T(8,128)}), f32[128,2048]{1,0:T(8,128)}) %all-reduce.3.cloned.1.call-update) | async-done | bytes 1048592 | tf_op jit(solution)/shard_map/psum | solution.py:47
  91.0 1.5 fusion.12
  92.5 0.8 copy-done.2
  93.3 0.2 fusion.22
  93.6 0.8 copy.18
  94.3 0.0 reduce-scatter.7.cloned.1.call-update
  94.4 0.2 reduce-scatter.5.cloned.1.call-start
  94.6 13.2 %fusion.13 = f32[128,4096]{1,0:T(8,128)} fusion(bf16[4096,2048]{1,0:T(8,128)(2,1)} %param.17, f32[128,2048]{1,0:T(8,128)} %all-reduce.3.cloned.1.call-done, bf16[128,2048]{1,0:T(8,128)(2,1)S(1)} %copy-done.7, bf16[128,2048]{1,0:T(8,128)(2,1)S(1)} %copy-done.3), kind=kOutput, calls=%fused_computation.26 | convolution fusion | flops 2150629376 | bytes 20971520 | tf_op jit(solution)/shard_map/dot_general | solution.py:10
  107.8 12.3 %convolution_add_fusion = f32[128,4096]{1,0:T(8,128)S(1)} fusion(f32[128,4096]{1,0:T(8,128)} %fusion.13, bf16[128,2048]{1,0:T(8,128)(2,1)} %copy-done.2, bf16[4096,2048]{1,0:T(8,128)(2,1)} %param.18), kind=kOutput, calls=%fused_computation.2 | convolution fusion | flops 2148007936 | bytes 21495808 | tf_op jit(solution)/shard_map/dot_general | solution.py:10
  120.1 2.4 %fusion = f32[128,4096]{1,0:T(8,128)} fusion(f32[128,4096]{1,0:T(8,128)S(1)} %convolution_add_fusion, f32[128,16]{0,1:T(8,128)S(1)} %fusion.22, bf16[16,4096]{1,0:T(8,128)(2,1)S(1)} %copy-done.4), kind=kOutput, calls=%fused_computation.1 | convolution fusion | flops 101711872 | bytes 4333568 | tf_op jit(solution)/shard_map/dot_general | solution.py:61
  122.5 0.0 reduce-scatter.5.cloned.1.call-update
  122.5 0.0 all-reduce.5.cloned.1.call-start
  122.6 6.0 %psum.23 = bf16[128,16]{0,1:T(8,128)(2,1)S(1)} all-reduce(f32[128,16]{0,1:T(8,128)S(1)} %fusion.21), channel_id=1, replica_groups=mesh['grp'=2,'row'=4,'col'=4] {'col'}, use_global_device_ids=true, to_apply=%region_4.0 | all-reduce | flops 2048 | bytes 12288 | tf_op jit(solution)/shard_map/psum | solution.py:47
  128.6 2.4 %convolution_multiply_fusion.5 = f32[16,2048]{1,0:T(8,128)} fusion(bf16[128,2048]{1,0:T(8,128)(2,1)} %param.16, bf16[128,2048]{1,0:T(8,128)(2,1)} %param.15, bf16[128,16]{0,1:T(8,128)(2,1)S(1)} %psum.23), kind=kOutput, calls=%fused_computation.9 | convolution fusion | flops 10518528 | bytes 1183744 | tf_op jit(solution)/shard_map/dot_general | solution.py:16
  131.0 1.7 convolution_multiply_fusion.2
  132.7 0.0 all-reduce.5.cloned.1.call-update
  132.8 1.6 convolution_multiply_fusion.1
  134.4 1.9 fusion.2
  136.3 30.6 %reduce-scatter.5.cloned.1.call-done = f32[32,4096]{1,0:T(8,128)} async-done(((f32[128,4096]{1,0:T(8,128)}), f32[32,4096]{1,0:T(8,128)}) %reduce-scatter.5.cloned.1.call-update) | async-done | bytes 524304 | tf_op jit(solution)/shard_map/reduce_scatter | solution.py:65
  166.9 1.8 convert_element_type.28
  168.7 35.8 %all-reduce.5.cloned.1.call-done = f32[16,4096]{1,0:T(8,128)} async-done(((f32[16,4096]{1,0:T(8,128)}), f32[16,4096]{1,0:T(8,128)}) %all-reduce.5.cloned.1.call-update) | async-done | bytes 262160 | tf_op jit(solution)/shard_map/psum | solution.py:71
  204.5 1.7 copy.22
  (15 shorter events, 0.0 us)
Async XLA Ops:
  7.2 123.8 %copy-start = (bf16[32,4096]{1,0:T(8,128)(2,1)S(1)}, bf16[32,4096]{1,0:T(8,128)(2,1)}, u32[]{:S(2)}) copy-start(bf16[32,4096]{1,0:T(8,128)(2,1)} %param.13) | copy-start | bytes 786436
  7.2 46.5 %copy-start.5 = (bf16[16,2048]{1,0:T(8,128)(2,1)S(1)}, bf16[16,2048]{1,0:T(8,128)(2,1)}, u32[]{:S(2)}) copy-start(bf16[16,2048]{1,0:T(8,128)(2,1)} %param.22) | copy-start | bytes 196612
  7.2 83.8 %copy-start.3 = (bf16[128,2048]{1,0:T(8,128)(2,1)S(1)}, bf16[128,2048]{1,0:T(8,128)(2,1)}, u32[]{:S(2)}) copy-start(bf16[128,2048]{1,0:T(8,128)(2,1)} %param.15) | copy-start | bytes 1572868
  7.2 86.1 %copy-start.6 = (bf16[16,2048]{1,0:T(8,128)(2,1)S(1)}, bf16[16,2048]{1,0:T(8,128)(2,1)}, u32[]{:S(2)}) copy-start(bf16[16,2048]{1,0:T(8,128)(2,1)} %param.21) | copy-start | bytes 196612
  7.2 87.4 %copy-start.7 = (bf16[128,2048]{1,0:T(8,128)(2,1)S(1)}, bf16[128,2048]{1,0:T(8,128)(2,1)}, u32[]{:S(2)}) copy-start(bf16[128,2048]{1,0:T(8,128)(2,1)} %param.16) | copy-start | bytes 1572868
  7.2 33.1 %all-gather.2.cloned.1.call-start = ((), (), s32[]{:S(2)}) async-start(), calls=%async_computation.2 | async-start | bytes 1310720 | tf_op jit(solution)/shard_map/all_gather | solution.py:41
  8.0 83.1 %all-reduce.3.cloned.1.call-start = ((), (), s32[]{:S(2)}) async-start(), calls=%async_computation.3 | async-start | bytes 2097152 | tf_op jit(solution)/shard_map/psum | solution.py:47
  55.3 75.7 %reduce-scatter.7.cloned.1.call-start = ((), (), s32[]{:S(2)}) async-start(), calls=%async_computation.6 | async-start | bytes 81920
  92.5 0.8 copy-start.2
  94.4 25.7 %copy-start.4 = (bf16[16,4096]{1,0:T(8,128)(2,1)S(1)}, bf16[16,4096]{1,0:T(8,128)(2,1)}, u32[]{:S(2)}) copy-start(bf16[16,4096]{1,0:T(8,128)(2,1)} %param.20) | copy-start | bytes 393220
  94.4 72.5 %reduce-scatter.5.cloned.1.call-start = ((), (), s32[]{:S(2)}) async-start(), calls=%async_computation.4 | async-start | bytes 2621440 | tf_op jit(solution)/shard_map/reduce_scatter | solution.py:65
  107.8 25.0 %copy-start.1 = (bf16[128,4096]{1,0:T(8,128)(2,1)S(1)}, bf16[128,4096]{1,0:T(8,128)(2,1)}, u32[]{:S(2)}) copy-start(bf16[128,4096]{1,0:T(8,128)(2,1)} %all-gather.2.cloned.1.call-done) | copy-start | bytes 3145732
  122.5 82.0 %all-reduce.5.cloned.1.call-start = ((), (), s32[]{:S(2)}) async-start(), calls=%async_computation.5 | async-start | bytes 524288 | tf_op jit(solution)/shard_map/psum | solution.py:71
Sparse Core Ops, SparseCore 0:
  9.6 30.6 all-gather.1
  55.4 35.5 all-reduce.2
  94.5 19.4 reduce-scatter.6
  122.6 44.2 reduce-scatter.4
  169.8 34.6 all-reduce.4
where the time goes:
time: 213 us
  waiting for transfers between devices  135 us (63%)
  matrix products  50.8 us (24%)
  between operations  13.9 us (7%)
  blocking collectives  6 us (3%)
  other arithmetic  3.28 us (2%)
  local copies, waits for them, and re-layouts  3.27 us (2%)
    dot_general x5, matrix products, contract_trailing(): lax.dot_general(left, right, (((1,), (1,)), ((), ())), preferred_element_...  39 us
    psum x1, waiting for transfers between devices, body(): up_entry_gradient = lax.psum(up_entry_term, 'row')  35.8 us
    psum x1, waiting for transfers between devices, body(): hidden_gradient, down_full = lax.psum((hidden_piece, down_piece), 'col')  35.7 us
    all_gather x1, waiting for transfers between devices, body(): lax.all_gather(output_gradient, 'row', axis=0, tiled=True)  32.3 us
    reduce_scatter x1, waiting for transfers between devices, body(): lax.psum_scatter(input_piece, 'row', scatter_dimension=0, tiled=True)  30.6 us
    psum x1, blocking collectives, body(): hidden_gradient, down_full = lax.psum((hidden_piece, down_piece), 'col')  6 us
  transfers between devices with their start and end apart: 5, of which 4 were waited for; matrix products, arithmetic and copies ran while one was open for 18% of the time, Pallas kernels for 0%

commit v1 on v0

v1 whole, which is shorter than its diff:
```python
import functools

import jax
import jax.numpy as jnp
from jax import lax
from jax.experimental import pallas as pl
from jax.experimental.pallas import tpu as pltpu
from jax.sharding import PartitionSpec as P

adapter_scale = 2.0
HIGHEST = lax.Precision.HIGHEST
LANES = 128
VMEM_SPEC = pl.BlockSpec(memory_space=pltpu.VMEM)
ANY_SPEC = pl.BlockSpec(memory_space=pl.ANY)
f32 = jnp.float32
bf16 = jnp.bfloat16


def contract_trailing(left, right):
    return lax.dot_general(
        left, right, (((1,), (1,)), ((), ())), preferred_element_type=f32
    )


def contract_leading(left, right, matmul_accuracy=None):
    return lax.dot_general(
        left,
        right,
        (((0,), (0,)), ((), ())),
        precision=matmul_accuracy,
        preferred_element_type=f32,
    )


def in_vmem(x):
    return pltpu.with_memory_space_constraint(x, pltpu.VMEM)


def call(kernel, out_shape, *args, scratch=(), specs=None, vmem=16 << 20, cost=None):
    outs = out_shape if isinstance(out_shape, (tuple, list)) else (out_shape,)
    out_specs = tuple(VMEM_SPEC for _ in outs)
    result = pl.pallas_call(
        kernel,
        out_shape=tuple(outs),
        in_specs=specs if specs is not None else [VMEM_SPEC] * len(args),
        out_specs=out_specs,
        scratch_shapes=list(scratch),
        compiler_params=pltpu.CompilerParams(vmem_limit_bytes=vmem),
        cost_estimate=cost,
    )(*args)
    return result if isinstance(out_shape, (tuple, list)) else result[0]


def shape(dims, dtype):
    return jax.ShapeDtypeStruct(dims, dtype)


def fetch_kernel(pieces, src, dst, sems):
    rows = src.shape[0] // pieces
    copies = [
        pltpu.make_async_copy(
            src.at[pl.ds(i * rows, rows)], dst.at[pl.ds(i * rows, rows)], sems.at[i]
        )
        for i in range(pieces)
    ]
    for c in copies:
        c.start()
    for c in copies:
        c.wait()


def fetch(weight, pieces=8):
    cost = pl.CostEstimate(flops=0, transcendentals=0, bytes_accessed=2 * weight.size * 2)
    return call(
        functools.partial(fetch_kernel, pieces),
        pltpu.VMEM(weight.shape, weight.dtype),
        weight,
        scratch=[pltpu.SemaphoreType.DMA((pieces,))],
        specs=[ANY_SPEC],
        cost=cost,
    )


def factors_kernel(g_ref, u_ref, a_ref, b_ref, h_ref):
    g = g_ref[...].astype(f32)
    u = u_ref[...].astype(f32)
    q = 1.0 / (1.0 + jnp.exp(-g))
    b = g * q
    a_ref[...] = u * q * (1.0 + g * (1.0 - q))
    b_ref[...] = b
    h_ref[...] = (b * u).astype(bf16)


def split_terms(x):
    hi = x.astype(bf16)
    rest = x - hi.astype(f32)
    mid = rest.astype(bf16)
    low = (rest - mid.astype(f32)).astype(bf16)
    return hi, mid, low


def join_terms(hi, mid, low):
    return hi.astype(f32) + (mid.astype(f32) + low.astype(f32))


def store_terms(ref, start, x):
    n = x.shape[0]
    for i, term in enumerate(split_terms(x)):
        ref[start + i * n : start + (i + 1) * n, :] = term


def load_terms(ref, start, n):
    return join_terms(*(ref[start + i * n : start + (i + 1) * n, :] for i in range(3)))


def place_rows(full, pieces, position):
    n = pieces[0].shape[0]
    for k, piece in enumerate(pieces):
        full[pl.ds(pl.multiple_of((position ^ k) * n, n), n), :] = piece[...]


def hidden_kernel(flip, block, o0, o1, o2, o3, w, exit_ref, entry, out, low_ref, full):
    place_rows(full, (o0, o1, o2, o3), lax.axis_index("row"))
    half = out.shape[1]
    which = lax.rem(lax.axis_index("col"), 2) ^ flip
    low = contract_trailing(exit_ref[...], full[...])
    low_ref[...] = low
    for i in range(half // block):
        rows = pl.ds(pl.multiple_of(which * half + i * block, block), block)
        out[:, i * block : (i + 1) * block] = contract_trailing(
            full[...], w[rows, :]
        ) + adapter_scale * contract_leading(
            low, entry[:, rows].astype(f32), HIGHEST
        )


def payload_kernel(keep, got, low, low_got, out):
    total = keep[...] + got[...]
    rows, half = total.shape
    for i in range(half // LANES):
        out[i * rows : (i + 1) * rows, :] = total[:, i * LANES : (i + 1) * LANES].astype(bf16)
    store_terms(out, half // LANES * rows, low[...] + low_got[...])


def gradient_kernel(mine, other, a, b, out, low_ref):
    rows = a.shape[0]
    half = out.shape[2]
    rank = low_ref.shape[0]
    blocks = half // LANES
    start = pl.multiple_of(lax.rem(lax.axis_index("col"), 2) * half, half)
    for i in range(blocks):
        here = slice(i * rows, (i + 1) * rows)
        grad = mine[here, :].astype(f32) + other[here, :].astype(f32)
        lanes = pl.ds(pl.multiple_of(start + i * LANES, LANES), LANES)
        out[0, :, i * LANES : (i + 1) * LANES] = (grad * a[:, lanes]).astype(bf16)
        out[1, :, i * LANES : (i + 1) * LANES] = (grad * b[:, lanes]).astype(bf16)
    low_ref[...] = load_terms(mine, blocks * rows, rank) + load_terms(other, blocks * rows, rank)


def inputs_kernel(first, with_low, block, own, mate, wg, wu, exit_ref, entry, *rest):
    own_out, s1, s2, s3 = rest[:4]
    low_ref = rest[4] if with_low else None
    gg, ug, acc = rest[-3:]
    half = own.shape[2]
    width = acc.shape[1]
    rank = exit_ref.shape[0]
    par = lax.rem(lax.axis_index("col"), 2)
    mine = pl.ds(pl.multiple_of(par * half, half), half)
    theirs = pl.ds(pl.multiple_of((1 - par) * half, half), half)
    gg[:, mine] = own[0]
    ug[:, mine] = own[1]
    gg[:, theirs] = mate[0]
    ug[:, theirs] = mate[1]
    low = contract_trailing(exit_ref[...], ug[...])
    for i in range(width // block):
        rows = slice(first + i * block, first + (i + 1) * block)
        acc[:, i * block : (i + 1) * block] = (
            contract_trailing(gg[...], wg[rows, :])
            + contract_trailing(ug[...], wu[rows, :])
            + adapter_scale * contract_leading(low, entry[:, rows].astype(f32), HIGHEST)
        )
    row = lax.axis_index("row")
    n = own_out.shape[0]
    own_out[...] = acc[pl.ds(pl.multiple_of(row * n, n), n), :]
    for k, out in ((1, s1), (2, s2), (3, s3)):
        dest = pl.ds(pl.multiple_of((row ^ k) * n, n), n)
        for i in range(width // LANES):
            out[i * n : (i + 1) * n, :] = acc[dest, i * LANES : (i + 1) * LANES].astype(bf16)
        if with_low:
            store_terms(out, width // LANES * n, low)
    if with_low:
        low_ref[...] = low


def finish_kernel(own, r1, r2, r3, out):
    n, width = own.shape
    for i in range(width // LANES):
        here = slice(i * n, (i + 1) * n)
        lanes = slice(i * LANES, (i + 1) * LANES)
        out[:, lanes] = (
            own[:, lanes]
            + r1[here, :].astype(f32)
            + r2[here, :].astype(f32)
            + r3[here, :].astype(f32)
        ).astype(bf16)


def entry_kernel(offset, i0, i1, i2, i3, low, r1, r2, r3, out, full, lows):
    row = lax.axis_index("row")
    rank = low.shape[0]
    place_rows(full, (i0, i1, i2, i3), row)
    lows[row] = low[...]
    for k, ref in ((1, r1), (2, r2), (3, r3)):
        lows[row ^ k] = load_terms(ref, offset, rank)
    total = (lows[0] + lows[1]) + (lows[2] + lows[3])
    parts = split_terms(total)
    full_inputs = full[...]
    out[...] = adapter_scale * sum(
        jnp.dot(part, full_inputs, preferred_element_type=f32) for part in parts
    )


def small_kernel(own, mate, low, hidden, up_act, down_act, o0, o1, o2, o3, up_exit, down_entry, down_exit, full, ug):
    half = own.shape[2]
    par = lax.rem(lax.axis_index("col"), 2)
    ug[:, pl.ds(pl.multiple_of(par * half, half), half)] = own[1]
    ug[:, pl.ds(pl.multiple_of((1 - par) * half, half), half)] = mate[1]
    place_rows(full, (o0, o1, o2, o3), lax.axis_index("row"))
    up_exit[...] = adapter_scale * jnp.dot(up_act[...], ug[...], preferred_element_type=f32)
    down_entry[...] = adapter_scale * jnp.dot(
        low[...].astype(bf16), hidden[...], preferred_element_type=f32
    )
    down_exit[...] = adapter_scale * jnp.dot(down_act[...], full[...], preferred_element_type=f32)


def swap(x, axis, distance, n):
    return lax.ppermute(x, axis, [(i, i ^ distance) for i in range(n)])


CHUNKS = 2


def exchange_body(
    inputs,
    output_gradient,
    gate_preactivation,
    up_preactivation,
    gate_weight,
    up_weight,
    down_weight,
    up_adapter_entry,
    up_adapter_exit,
    down_adapter_entry,
    down_adapter_exit,
    up_adapter_activations,
    down_adapter_activations,
):
    tokens, hidden = gate_preactivation.shape
    share, width = output_gradient.shape
    rank = up_adapter_exit.shape[0]
    half = hidden // 2
    own_gradient = output_gradient
    gathered = [swap(own_gradient, "row", k, 4) for k in (1, 2, 3)]
    down_v = fetch(down_weight)
    gate_v = fetch(gate_weight)
    up_v = fetch(up_weight)
    a, b, hidden_state = call(
        factors_kernel,
        (shape((tokens, hidden), f32), shape((tokens, hidden), f32), shape((tokens, hidden), bf16)),
        gate_preactivation,
        up_preactivation,
    )
    gathered_inputs = [swap(inputs, "row", k, 4) for k in (1, 2, 3)]

    def hidden_half(flip):
        return call(
            functools.partial(hidden_kernel, flip, 512),
            (shape((tokens, half), f32), shape((rank, tokens), f32)),
            own_gradient,
            *gathered,
            in_vmem(down_v),
            down_adapter_exit,
            down_adapter_entry,
            scratch=[pltpu.VMEM((tokens, width), bf16)],
        )

    send, low_piece = hidden_half(1)
    got = swap(send, "col", 1, 4)
    low_got = swap(low_piece, "col", 1, 4)
    keep, low_piece2 = hidden_half(0)
    blocks = half // LANES
    payload = call(
        payload_kernel,
        shape((blocks * tokens + 3 * rank, LANES), bf16),
        keep,
        got,
        low_piece2,
        low_got,
    )
    other = swap(payload, "col", 2, 4)
    grads, low_full = call(
        gradient_kernel,
        (shape((2, tokens, half), bf16), shape((rank, tokens), f32)),
        payload,
        other,
        a,
        b,
    )
    mate_grads = swap(grads, "col", 1, 4)

    part = width // CHUNKS
    rows = part // LANES * share
    owns, received = [], []
    low_up = None
    for c in range(CHUNKS):
        with_low = c == 0
        sent = shape((rows + (3 * rank if with_low else 0), LANES), bf16)
        outs = call(
            functools.partial(inputs_kernel, c * part, with_low, 512),
            (shape((share, part), f32), sent, sent, sent)
            + ((shape((rank, tokens), f32),) if with_low else ()),
            grads,
            mate_grads,
            in_vmem(gate_v),
            in_vmem(up_v),
            up_adapter_exit,
            up_adapter_entry,
            scratch=[
                pltpu.VMEM((tokens, hidden), bf16),
                pltpu.VMEM((tokens, hidden), bf16),
                pltpu.VMEM((tokens, part), f32),
            ],
        )
        if with_low:
            low_up = outs[4]
        owns.append(outs[0])
        received.append([swap(outs[k], "row", k, 4) for k in (1, 2, 3)])
    up_exit_gradient, down_entry_gradient, down_exit_gradient = call(
        small_kernel,
        (shape((rank, hidden), f32), shape((rank, hidden), f32), shape((rank, width), f32)),
        grads,
        mate_grads,
        low_full,
        hidden_state,
        up_adapter_activations,
        down_adapter_activations,
        own_gradient,
        *gathered,
        scratch=[pltpu.VMEM((tokens, width), bf16), pltpu.VMEM((tokens, hidden), bf16)],
    )
    up_entry_gradient = call(
        functools.partial(entry_kernel, rows),
        shape((rank, width), f32),
        inputs,
        *gathered_inputs,
        low_up,
        *received[0],
        scratch=[pltpu.VMEM((tokens, width), bf16), pltpu.VMEM((4, rank, tokens), f32)],
    )
    pieces = [
        call(finish_kernel, shape((share, part), bf16), owns[c], *received[c])
        for c in range(CHUNKS)
    ]
    return (
        jnp.concatenate(pieces, axis=1),
        up_entry_gradient,
        up_exit_gradient,
        down_entry_gradient,
        down_exit_gradient,
    )


def body(
    inputs,
    output_gradient,
    gate_preactivation,
    up_preactivation,
    gate_weight,
    up_weight,
    down_weight,
    up_adapter_entry,
    up_adapter_exit,
    down_adapter_entry,
    down_adapter_exit,
    up_adapter_activations,
    down_adapter_activations,
):
    highest_setting = HIGHEST
    complete_gradient = lax.all_gather(output_gradient, "row", axis=0, tiled=True)
    down_piece = contract_trailing(complete_gradient, down_adapter_exit)
    hidden_piece = contract_trailing(complete_gradient, down_weight)
    hidden_piece = hidden_piece + adapter_scale * jnp.dot(
        down_piece, down_adapter_entry.astype(f32), precision=highest_setting
    )
    hidden_gradient, down_full = lax.psum((hidden_piece, down_piece), "col")
    gate_f = gate_preactivation.astype(f32)
    up_f = up_preactivation.astype(f32)
    sigmoid_gate = jax.nn.sigmoid(gate_f)
    hidden_state = (gate_f * sigmoid_gate * up_f).astype(bf16)
    gate_grad = (
        hidden_gradient * up_f * sigmoid_gate * (1.0 + gate_f * (1.0 - sigmoid_gate))
    ).astype(bf16)
    up_gradient = (hidden_gradient * gate_f * sigmoid_gate).astype(bf16)
    down_rounded_value = down_full.astype(bf16)
    upper_piece = contract_trailing(up_gradient, up_adapter_exit)
    input_piece = contract_trailing(gate_grad, gate_weight) + contract_trailing(
        up_gradient, up_weight
    )
    input_piece = input_piece + adapter_scale * jnp.dot(
        upper_piece, up_adapter_entry.astype(f32), precision=highest_setting
    )
    input_grad, upper_full = (
        lax.psum_scatter(input_piece, "row", scatter_dimension=0, tiled=True),
        lax.psum_scatter(upper_piece, "row", scatter_dimension=0, tiled=True),
    )
    up_entry_term = adapter_scale * contract_leading(
        upper_full, inputs.astype(f32), matmul_accuracy=highest_setting
    )
    up_entry_gradient = lax.psum(up_entry_term, "row")
    up_exit_gradient = adapter_scale * jnp.dot(
        up_adapter_activations, up_gradient, preferred_element_type=f32
    )
    down_entry_gradient = adapter_scale * contract_leading(down_rounded_value, hidden_state)
    down_exit_gradient = adapter_scale * jnp.dot(
        down_adapter_activations, complete_gradient, preferred_element_type=f32
    )
    return (
        input_grad.astype(bf16),
        up_entry_gradient,
        up_exit_gradient,
        down_entry_gradient,
        down_exit_gradient,
    )


def solution(mesh):
    placed = (
        P(("grp", "row"), "col"),
        P(("grp", "row"), "col"),
        P("grp", "row"),
        P("grp", "row"),
        P("col", "row"),
        P("col", "row"),
        P("row", "col"),
        P(None, "col"),
        P(None, "row"),
        P(None, "row"),
        P(None, "col"),
        P(None, "grp"),
        P(None, "grp"),
    )
    exchange = mesh.shape["row"] == 4 and mesh.shape["col"] == 4
    return jax.shard_map(
        exchange_body if exchange else body,
        mesh=mesh,
        in_specs=placed,
        out_specs=(
            P(("grp", "row"), "col"),
            P("grp", "col"),
            P("grp", "row"),
            P("grp", "row"),
            P("grp", "col"),
        ),
        check_vma=False,
    )
```

time: 213 us -> 136 us (0.64)
  waiting for transfers between devices: 135 us -> 51.8 us
  matrix products: 50.8 us -> 0 us
  Pallas kernels: 0 us -> 26.8 us
  local copies, waits for them, and re-layouts: 3.27 us -> 28.9 us
  starting transfers between devices: 0.38 us -> 24.7 us
  between operations: 13.9 us -> 0.88 us
  blocking collectives: 6 us -> 0 us
  other arithmetic: 3.28 us -> 0.72 us
    psum x2 -> x0, waiting for transfers between devices: 71.5 us -> none  [the longest x1 35.8 us: body(): up_entry_gradient = lax.psum(up_entry_term, 'row')]
    ppermute x0 -> x16, waiting for transfers between devices: none -> 51.8 us  [swap(): return lax.ppermute(x, axis, [(i, i ^ distance) for i in range(n)])]
    dot_general x11 -> x0, matrix products: 50.8 us -> none  [the longest x5 39 us: contract_trailing(): lax.dot_general(left, right, (((1,), (1,)), ((), ())), preferred_element_...]
    all_gather x1 -> x0, waiting for transfers between devices: 32.3 us -> none  [body(): lax.all_gather(output_gradient, 'row', axis=0, tiled=True)]
    reduce_scatter x1 -> x0, waiting for transfers between devices: 30.6 us -> none  [body(): lax.psum_scatter(input_piece, 'row', scatter_dimension=0, tiled=True)]
    pallas_call x0 -> x14, Pallas kernels: none -> 26.8 us  [call(): pl.pallas_call(kernel, out_shape=tuple(outs), in_specs=specs if specs is...]
    unnamed x18 -> x30, local copies, waits for them, and re-layouts: 3.27 us -> 28.9 us
    ppermute x0 -> x16, starting transfers between devices: none -> 24.7 us  [swap(): return lax.ppermute(x, axis, [(i, i ^ distance) for i in range(n)])]
  transfers between devices with their start and end apart: 5 -> 16, of which waited for: 4 -> 6; matrix products, arithmetic and copies ran while one was open for 18% -> 1% of each run, Pallas kernels for 0% -> 12%
where the time goes in v1:
time: 136 us; the launch traced here: 134 us
  waiting for transfers between devices  51.8 us (38%)
  local copies, waits for them, and re-layouts  28.9 us (21%)
  Pallas kernels  26.8 us (20%)
  starting transfers between devices  24.7 us (18%)
    ppermute x16, waiting for transfers between devices, swap(): return lax.ppermute(x, axis, [(i, i ^ distance) for i in range(n)])  51.8 us
    unnamed x30, local copies, waits for them, and re-layouts  28.9 us
    pallas_call x14, Pallas kernels, call(): pl.pallas_call(kernel, out_shape=tuple(outs), in_specs=specs if specs is...  26.8 us
    ppermute x16, starting transfers between devices, swap(): return lax.ppermute(x, axis, [(i, i ^ distance) for i in range(n)])  24.7 us
  transfers between devices with their start and end apart: 16, of which 6 were waited for; matrix products, arithmetic and copies ran while one was open for 1% of the time, Pallas kernels for 12%

profile of v1, /device:TPU:0, one launch (start us, length us, event | category | flops | bytes accessed | tf_op | source)
XLA Modules:
  0.0 133.8 jit_solution(11653108268396549071)
XLA Ops:
  0.6 3.1 %collective-permute-start = (bf16[32,4096]{1,0:T(8,128)(2,1)}, bf16[32,4096]{1,0:T(8,128)(2,1)S(1)}, u32[]{:S(2)}, u32[]{:S(2)}) collective-permute-start(bf16[32,4096]{1,0:T(8,128)(2,1)} %o0.5), channel_id=1, source_target_pairs={{0,4},{4,0},{8,12},{12,8},{1,5},{5,1},{9,13},{13,9},{2,6},{6,2},{1... | collective-permute-start | bytes 786440 | tf_op jit(solution)/shard_map/ppermute | solution.py:237
  3.7 2.6 %collective-permute-start.1 = (bf16[32,4096]{1,0:T(8,128)(2,1)}, bf16[32,4096]{1,0:T(8,128)(2,1)S(1)}, u32[]{:S(2)}, u32[]{:S(2)}) collective-permute-start(bf16[32,4096]{1,0:T(8,128)(2,1)} %o0.5), channel_id=1, source_target_pairs={{0,8},{4,12},{8,0},{12,4},{1,9},{5,13},{9,1},{13,5},{2,10},{6,14},... | collective-permute-start | bytes 786440 | tf_op jit(solution)/shard_map/ppermute | solution.py:237
  6.3 5.8 %copy-done.2 = bf16[2048,4096]{1,0:T(8,128)(2,1)S(1)} copy-done((bf16[2048,4096]{1,0:T(8,128)(2,1)S(1)}, bf16[2048,4096]{1,0:T(8,128)(2,1)}, u32[]{:S(2)}) %copy-start.2) | copy-done | bytes 16777240
  12.1 1.2 shard_map.164.w
  13.3 1.8 %collective-permute-done.o1 = bf16[32,4096]{1,0:T(8,128)(2,1)S(1)} collective-permute-done((bf16[32,4096]{1,0:T(8,128)(2,1)}, bf16[32,4096]{1,0:T(8,128)(2,1)S(1)}, u32[]{:S(2)}, u32[]{:S(2)}) %collective-permute-start) | collective-permute-done | bytes 262176 | tf_op jit(solution)/shard_map/ppermute | solution.py:237
  15.1 10.2 %collective-permute-done.1.o2 = bf16[32,4096]{1,0:T(8,128)(2,1)S(1)} collective-permute-done((bf16[32,4096]{1,0:T(8,128)(2,1)}, bf16[32,4096]{1,0:T(8,128)(2,1)S(1)}, u32[]{:S(2)}, u32[]{:S(2)}) %collective-permute-start.1) | collective-permute-done | bytes 262176 | tf_op jit(solution)/shard_map/ppermute | solution.py:237
  25.3 4.0 %shard_map.166 = (f32[128,1024]{1,0:T(8,128)S(1)}, f32[16,128]{1,0:T(8,128)S(1)}) custom-call(bf16[32,4096]{1,0:T(8,128)(2,1)S(1)} %copy-done.5, bf16[32,4096]{1,0:T(8,128)(2,1)S(1)} %collective-permute-done.o1, bf16[32,4096]{1,0:T(8,128)(2,1)S(1)} %collective-permute-done.1.o2, bf16[32,4096]{1,0:T(8,128)(2,1)S(1)} %collective-permute-done.2.o3, ...), custom_call_target="tpu_custom_call" | custom-call | tf_op jit(solution)/shard_map/pallas_call | solution.py:42
  29.4 0.5 collective-permute-start.4
  29.9 4.0 %shard_map.165 = (f32[128,1024]{1,0:T(8,128)S(1)}, f32[16,128]{1,0:T(8,128)S(1)}) custom-call(bf16[32,4096]{1,0:T(8,128)(2,1)S(1)} %copy-done.5, bf16[32,4096]{1,0:T(8,128)(2,1)S(1)} %collective-permute-done.o1, bf16[32,4096]{1,0:T(8,128)(2,1)S(1)} %collective-permute-done.1.o2, bf16[32,4096]{1,0:T(8,128)(2,1)S(1)} %collective-permute-done.2.o3, ...), custom_call_target="tpu_custom_call" | custom-call | tf_op jit(solution)/shard_map/pallas_call | solution.py:42
  34.0 1.6 %collective-permute-start.5 = (bf16[1072,128]{1,0:T(8,128)(2,1)S(1)}, bf16[1072,128]{1,0:T(8,128)(2,1)S(1)}, u32[]{:S(2)}, u32[]{:S(2)}) collective-permute-start(bf16[1072,128]{1,0:T(8,128)(2,1)S(1)} %shard_map.167.mine), channel_id=1, source_target_pairs={{0,2},{1,3},{2,0},{3,1},{4,6},{5,7},{6,4},{7,5},{8,10},{9,11},{10,... | collective-permute-start | bytes 823304 | tf_op jit(solution)/shard_map/ppermute | solution.py:237
  35.6 0.6 shard_map.168
  36.2 6.4 %collective-permute-done.5.other = bf16[1072,128]{1,0:T(8,128)(2,1)S(1)} collective-permute-done((bf16[1072,128]{1,0:T(8,128)(2,1)S(1)}, bf16[1072,128]{1,0:T(8,128)(2,1)S(1)}, u32[]{:S(2)}, u32[]{:S(2)}) %collective-permute-start.5) | collective-permute-done | bytes 274464 | tf_op jit(solution)/shard_map/ppermute | solution.py:237
  42.9 5.8 %copy-done.3 = bf16[4096,2048]{1,0:T(8,128)(2,1)S(1)} copy-done((bf16[4096,2048]{1,0:T(8,128)(2,1)S(1)}, bf16[4096,2048]{1,0:T(8,128)(2,1)}, u32[]{:S(2)}) %copy-start.3) | copy-done | bytes 16777240
  48.7 1.2 shard_map.170.wg
  49.9 5.7 %copy-done = bf16[4096,2048]{1,0:T(8,128)(2,1)} copy-done((bf16[4096,2048]{1,0:T(8,128)(2,1)}, bf16[4096,2048]{1,0:T(8,128)(2,1)S(1)}, u32[]{:S(2)}) %copy-start) | copy-done | bytes 16777240
  55.6 5.8 %copy-done.4 = bf16[4096,2048]{1,0:T(8,128)(2,1)S(1)} copy-done((bf16[4096,2048]{1,0:T(8,128)(2,1)S(1)}, bf16[4096,2048]{1,0:T(8,128)(2,1)}, u32[]{:S(2)}) %copy-start.4) | copy-done | bytes 16777240
  61.4 1.4 %shard_map.171.wu = bf16[4096,2048]{1,0:T(8,128)(2,1)S(1)} custom-call(bf16[4096,2048]{1,0:T(8,128)(2,1)S(1)} %copy-done.4), custom_call_target="tpu_custom_call" | custom-call | bytes 33554432 | tf_op jit(solution)/shard_map/pallas_call | solution.py:42
  62.8 5.8 %copy-done.1 = bf16[4096,2048]{1,0:T(8,128)(2,1)S(1)} copy-done((bf16[4096,2048]{1,0:T(8,128)(2,1)S(1)}, bf16[4096,2048]{1,0:T(8,128)(2,1)}, u32[]{:S(2)}) %copy-start.1) | copy-done | bytes 16777240
  68.6 5.8 %shard_map.174 = (f32[32,2048]{1,0:T(8,128)S(1)}, bf16[512,128]{1,0:T(8,128)(2,1)S(1)}, bf16[512,128]{1,0:T(8,128)(2,1)S(1)}, bf16[512,128]{1,0:T(8,128)(2,1)S(1)}) custom-call(bf16[2,128,1024]{2,1,0:T(8,128)(2,1)S(1)} %get-tuple-element.32.own, bf16[2,128,1024]{2,1,0:T(8,128)(2,1)S(1)} %collective-permute-done.6.mate, bf16[4096,2048]{1,0:T(8,128)(2,1)S(1)} %copy-done.1, ...), custom_call_target="tpu_custom_call" | custom-call | tf_op jit(solution)/shard_map/pallas_call | solution.py:42
  74.4 4.8 %collective-permute-start.10 = (bf16[512,128]{1,0:T(8,128)(2,1)S(1)}, bf16[512,128]{1,0:T(8,128)(2,1)S(1)}, u32[]{:S(2)}, u32[]{:S(2)}) collective-permute-start(bf16[512,128]{1,0:T(8,128)(2,1)S(1)} %get-tuple-element.38), channel_id=1, source_target_pairs={{0,4},{4,0},{8,12},{12,8},{1,5},{5,1},{9,13},{13,9},{2,6},{6,2},{1... | collective-permute-start | bytes 393224 | tf_op jit(solution)/shard_map/ppermute | solution.py:237
  79.3 5.8 %shard_map.172 = (f32[32,2048]{1,0:T(8,128)S(1)}, bf16[560,128]{1,0:T(8,128)(2,1)S(1)}, bf16[560,128]{1,0:T(8,128)(2,1)S(1)}, bf16[560,128]{1,0:T(8,128)(2,1)S(1)}, f32[16,128]{1,0:T(8,128)S(1)}) custom-call(bf16[2,128,1024]{2,1,0:T(8,128)(2,1)S(1)} %get-tuple-element.32.own, bf16[2,128,1024]{2,1,0:T(8,128)(2,1)S(1)} %collective-permute-done.6.mate, ...), custom_call_target="tpu_custom_call" | custom-call | tf_op jit(solution)/shard_map/pallas_call | solution.py:42
  85.1 3.0 %collective-permute-start.8 = (bf16[560,128]{1,0:T(8,128)(2,1)S(1)}, bf16[560,128]{1,0:T(8,128)(2,1)S(1)}, u32[]{:S(2)}, u32[]{:S(2)}) collective-permute-start(bf16[560,128]{1,0:T(8,128)(2,1)S(1)} %get-tuple-element.35), channel_id=1, source_target_pairs={{0,8},{4,12},{8,0},{12,4},{1,9},{5,13},{9,1},{13,5},{2,10},{6,14},... | collective-permute-start | bytes 430088 | tf_op jit(solution)/shard_map/ppermute | solution.py:237
  88.1 1.4 %collective-permute-start.9 = (bf16[560,128]{1,0:T(8,128)(2,1)S(1)}, bf16[560,128]{1,0:T(8,128)(2,1)S(1)}, u32[]{:S(2)}, u32[]{:S(2)}) collective-permute-start(bf16[560,128]{1,0:T(8,128)(2,1)S(1)} %get-tuple-element.36), channel_id=1, source_target_pairs={{0,12},{4,8},{8,4},{12,0},{1,13},{5,9},{9,5},{13,1},{2,14},{6,10},... | collective-permute-start | bytes 430088 | tf_op jit(solution)/shard_map/ppermute | solution.py:237
  89.7 2.3 %collective-permute-start.12 = (bf16[512,128]{1,0:T(8,128)(2,1)S(1)}, bf16[512,128]{1,0:T(8,128)(2,1)S(1)}, u32[]{:S(2)}, u32[]{:S(2)}) collective-permute-start(bf16[512,128]{1,0:T(8,128)(2,1)S(1)} %get-tuple-element.40), channel_id=1, source_target_pairs={{0,12},{4,8},{8,4},{12,0},{1,13},{5,9},{9,5},{13,1},{2,14},{6,10},... | collective-permute-start | bytes 393224 | tf_op jit(solution)/shard_map/ppermute | solution.py:237
  92.0 1.2 shard_map.177
  93.2 17.2 %collective-permute-done.11.r2 = bf16[512,128]{1,0:T(8,128)(2,1)S(1)} collective-permute-done((bf16[512,128]{1,0:T(8,128)(2,1)S(1)}, bf16[512,128]{1,0:T(8,128)(2,1)S(1)}, u32[]{:S(2)}, u32[]{:S(2)}) %collective-permute-start.11) | collective-permute-done | bytes 131104 | tf_op jit(solution)/shard_map/ppermute | solution.py:237
  110.4 3.6 %collective-permute-start.14 = (bf16[32,4096]{1,0:T(8,128)(2,1)S(1)}, bf16[32,4096]{1,0:T(8,128)(2,1)S(1)}, u32[]{:S(2)}, u32[]{:S(2)}) collective-permute-start(bf16[32,4096]{1,0:T(8,128)(2,1)S(1)} %copy-done.12), channel_id=1, source_target_pairs={{0,8},{4,12},{8,0},{12,4},{1,9},{5,13},{9,1},{13,5},{2,10},{6,14},... | collective-permute-start | bytes 786440 | tf_op jit(solution)/shard_map/ppermute | solution.py:237
  114.1 1.5 %collective-permute-start.15 = (bf16[32,4096]{1,0:T(8,128)(2,1)S(1)}, bf16[32,4096]{1,0:T(8,128)(2,1)S(1)}, u32[]{:S(2)}, u32[]{:S(2)}) collective-permute-start(bf16[32,4096]{1,0:T(8,128)(2,1)S(1)} %copy-done.12), channel_id=1, source_target_pairs={{0,12},{4,8},{8,4},{12,0},{1,13},{5,9},{9,5},{13,1},{2,14},{6,10},... | collective-permute-start | bytes 786440 | tf_op jit(solution)/shard_map/ppermute | solution.py:237
  115.7 0.7 pad_maximum_fusion
  116.4 4.7 %collective-permute-done.13.i1 = bf16[32,4096]{1,0:T(8,128)(2,1)S(1)} collective-permute-done((bf16[32,4096]{1,0:T(8,128)(2,1)S(1)}, bf16[32,4096]{1,0:T(8,128)(2,1)S(1)}, u32[]{:S(2)}, u32[]{:S(2)}) %collective-permute-start.13) | collective-permute-done | bytes 262176 | tf_op jit(solution)/shard_map/ppermute | solution.py:237
  121.1 11.4 %collective-permute-done.14.i2 = bf16[32,4096]{1,0:T(8,128)(2,1)S(1)} collective-permute-done((bf16[32,4096]{1,0:T(8,128)(2,1)S(1)}, bf16[32,4096]{1,0:T(8,128)(2,1)S(1)}, u32[]{:S(2)}, u32[]{:S(2)}) %collective-permute-start.14) | collective-permute-done | bytes 262176 | tf_op jit(solution)/shard_map/ppermute | solution.py:237
  132.5 1.3 shard_map.176
  (45 shorter events, 0.9 us)
Async XLA Ops:
  0.6 14.5 %collective-permute-start = (bf16[32,4096]{1,0:T(8,128)(2,1)}, bf16[32,4096]{1,0:T(8,128)(2,1)S(1)}, u32[]{:S(2)}, u32[]{:S(2)}) collective-permute-start(bf16[32,4096]{1,0:T(8,128)(2,1)} %o0.5), channel_id=1, source_target_pairs={{0,4},{4,0},{8,12},{12,8},{1,5},{5,1},{9,13},{13,9},{2,6},{6,2},{1... | collective-permute-start | bytes 786440 | tf_op jit(solution)/shard_map/ppermute | solution.py:237
  3.7 21.6 %collective-permute-start.1 = (bf16[32,4096]{1,0:T(8,128)(2,1)}, bf16[32,4096]{1,0:T(8,128)(2,1)S(1)}, u32[]{:S(2)}, u32[]{:S(2)}) collective-permute-start(bf16[32,4096]{1,0:T(8,128)(2,1)} %o0.5), channel_id=1, source_target_pairs={{0,8},{4,12},{8,0},{12,4},{1,9},{5,13},{9,1},{13,5},{2,10},{6,14},... | collective-permute-start | bytes 786440 | tf_op jit(solution)/shard_map/ppermute | solution.py:237
  6.3 19.0 %collective-permute-start.2 = (bf16[32,4096]{1,0:T(8,128)(2,1)}, bf16[32,4096]{1,0:T(8,128)(2,1)S(1)}, u32[]{:S(2)}, u32[]{:S(2)}) collective-permute-start(bf16[32,4096]{1,0:T(8,128)(2,1)} %o0.5), channel_id=1, source_target_pairs={{0,12},{4,8},{8,4},{12,0},{1,13},{5,9},{9,5},{13,1},{2,14},{6,10},... | collective-permute-start | bytes 786440 | tf_op jit(solution)/shard_map/ppermute | solution.py:237
  6.3 5.8 %copy-start.2 = (bf16[2048,4096]{1,0:T(8,128)(2,1)S(1)}, bf16[2048,4096]{1,0:T(8,128)(2,1)}, u32[]{:S(2)}) copy-start(bf16[2048,4096]{1,0:T(8,128)(2,1)} %src.3) | copy-start | bytes 50331652
  12.1 13.2 %copy-start.5 = (bf16[32,4096]{1,0:T(8,128)(2,1)S(1)}, bf16[32,4096]{1,0:T(8,128)(2,1)}, u32[]{:S(2)}) copy-start(bf16[32,4096]{1,0:T(8,128)(2,1)} %o0.5) | copy-start | bytes 786436
  12.1 13.2 %copy-start.6 = (bf16[16,4096]{1,0:T(8,128)(2,1)S(1)}, bf16[16,4096]{1,0:T(8,128)(2,1)}, u32[]{:S(2)}) copy-start(bf16[16,4096]{1,0:T(8,128)(2,1)} %exit_ref.5) | copy-start | bytes 393220
  12.1 13.2 %copy-start.10 = (bf16[16,2048]{1,0:T(8,128)(2,1)S(1)}, bf16[16,2048]{1,0:T(8,128)(2,1)}, u32[]{:S(2)}) copy-start(bf16[16,2048]{1,0:T(8,128)(2,1)} %entry.5) | copy-start | bytes 196612
  13.3 22.3 %copy-start.8 = (bf16[128,2048]{1,0:T(8,128)(2,1)S(1)}, bf16[128,2048]{1,0:T(8,128)(2,1)}, u32[]{:S(2)}) copy-start(bf16[128,2048]{1,0:T(8,128)(2,1)} %g_ref.1) | copy-start | bytes 1572868
  13.3 22.3 %copy-start.9 = (bf16[128,2048]{1,0:T(8,128)(2,1)S(1)}, bf16[128,2048]{1,0:T(8,128)(2,1)}, u32[]{:S(2)}) copy-start(bf16[128,2048]{1,0:T(8,128)(2,1)} %u_ref.1) | copy-start | bytes 1572868
  29.3 4.6 %collective-permute-start.3 = (f32[128,1024]{1,0:T(8,128)S(1)}, f32[128,1024]{1,0:T(8,128)S(1)}, u32[]{:S(2)}, u32[]{:S(2)}) collective-permute-start(f32[128,1024]{1,0:T(8,128)S(1)} %get-tuple-element.27), channel_id=1, source_target_pairs={{0,1},{1,0},{2,3},{3,2},{4,5},{5,4},{6,7},{7,6},{8,9},{9,8},{10,11... | collective-permute-start | bytes 1572872 | tf_op jit(solution)/shard_map/ppermute | solution.py:237
  29.4 4.5 %collective-permute-start.4 = (f32[16,128]{1,0:T(8,128)S(1)}, f32[16,128]{1,0:T(8,128)S(1)}, u32[]{:S(2)}, u32[]{:S(2)}) collective-permute-start(f32[16,128]{1,0:T(8,128)S(1)} %get-tuple-element.29), channel_id=1, source_target_pairs={{0,1},{1,0},{2,3},{3,2},{4,5},{5,4},{6,7},{7,6},{8,9},{9,8},{10,11... | collective-permute-start | bytes 24584 | tf_op jit(solution)/shard_map/ppermute | solution.py:237
  34.0 8.6 %collective-permute-start.5 = (bf16[1072,128]{1,0:T(8,128)(2,1)S(1)}, bf16[1072,128]{1,0:T(8,128)(2,1)S(1)}, u32[]{:S(2)}, u32[]{:S(2)}) collective-permute-start(bf16[1072,128]{1,0:T(8,128)(2,1)S(1)} %shard_map.167.mine), channel_id=1, source_target_pairs={{0,2},{1,3},{2,0},{3,1},{4,6},{5,7},{6,4},{7,5},{8,10},{9,11},{10,... | collective-permute-start | bytes 823304 | tf_op jit(solution)/shard_map/ppermute | solution.py:237
  42.8 20.0 %collective-permute-start.6 = (bf16[2,128,1024]{2,1,0:T(8,128)(2,1)S(1)}, bf16[2,128,1024]{2,1,0:T(8,128)(2,1)S(1)}, u32[]{:S(2)}, u32[]{:S(2)}) collective-permute-start(bf16[2,128,1024]{2,1,0:T(8,128)(2,1)S(1)} %get-tuple-element.32.own), channel_id=1, source_target_pairs={{0,1},{1,0},{2,3},{3,2},{4,5},{5,4},{6,7},{7,6},{8,9},{9,8},{10,11... | collective-permute-start | bytes 1572872 | tf_op jit(solution)/shard_map/ppermute | solution.py:237
  42.9 5.8 %copy-start.3 = (bf16[4096,2048]{1,0:T(8,128)(2,1)S(1)}, bf16[4096,2048]{1,0:T(8,128)(2,1)}, u32[]{:S(2)}) copy-start(bf16[4096,2048]{1,0:T(8,128)(2,1)} %src.4) | copy-start | bytes 50331652
  49.9 5.8 %copy-start = (bf16[4096,2048]{1,0:T(8,128)(2,1)}, bf16[4096,2048]{1,0:T(8,128)(2,1)S(1)}, u32[]{:S(2)}) copy-start(bf16[4096,2048]{1,0:T(8,128)(2,1)S(1)} %shard_map.170.wg) | copy-start | bytes 50331652
  55.6 5.8 %copy-start.4 = (bf16[4096,2048]{1,0:T(8,128)(2,1)S(1)}, bf16[4096,2048]{1,0:T(8,128)(2,1)}, u32[]{:S(2)}) copy-start(bf16[4096,2048]{1,0:T(8,128)(2,1)} %src.5) | copy-start | bytes 50331652
  61.4 1.4 %copy-start.7 = (bf16[16,4096]{1,0:T(8,128)(2,1)S(1)}, bf16[16,4096]{1,0:T(8,128)(2,1)}, u32[]{:S(2)}) copy-start(bf16[16,4096]{1,0:T(8,128)(2,1)} %entry.7) | copy-start | bytes 393220
  61.4 1.4 %copy-start.11 = (bf16[16,2048]{1,0:T(8,128)(2,1)S(1)}, bf16[16,2048]{1,0:T(8,128)(2,1)}, u32[]{:S(2)}) copy-start(bf16[16,2048]{1,0:T(8,128)(2,1)} %exit_ref.7) | copy-start | bytes 196612
  62.8 5.8 %copy-start.1 = (bf16[4096,2048]{1,0:T(8,128)(2,1)S(1)}, bf16[4096,2048]{1,0:T(8,128)(2,1)}, u32[]{:S(2)}) copy-start(bf16[4096,2048]{1,0:T(8,128)(2,1)} %copy-done) | copy-start | bytes 50331652
  74.4 17.6 %copy-start.13 = (bf16[16,128]{1,0:T(8,128)(2,1)S(1)}, bf16[16,128]{1,0:T(8,128)(2,1)}, u32[]{:S(2)}) copy-start(bf16[16,128]{1,0:T(8,128)(2,1)} %up_act.1) | copy-start | bytes 12292
  74.4 17.6 %copy-start.14 = (bf16[16,128]{1,0:T(8,128)(2,1)S(1)}, bf16[16,128]{1,0:T(8,128)(2,1)}, u32[]{:S(2)}) copy-start(bf16[16,128]{1,0:T(8,128)(2,1)} %down_act.1) | copy-start | bytes 12292
  74.4 36.0 %copy-start.12 = (bf16[32,4096]{1,0:T(8,128)(2,1)S(1)}, bf16[32,4096]{1,0:T(8,128)(2,1)}, u32[]{:S(2)}) copy-start(bf16[32,4096]{1,0:T(8,128)(2,1)} %i0.1) | copy-start | bytes 786436
  74.4 15.3 %collective-permute-start.10 = (bf16[512,128]{1,0:T(8,128)(2,1)S(1)}, bf16[512,128]{1,0:T(8,128)(2,1)S(1)}, u32[]{:S(2)}, u32[]{:S(2)}) collective-permute-start(bf16[512,128]{1,0:T(8,128)(2,1)S(1)} %get-tuple-element.38), channel_id=1, source_target_pairs={{0,4},{4,0},{8,12},{12,8},{1,5},{5,1},{9,13},{13,9},{2,6},{6,2},{1... | collective-permute-start | bytes 393224 | tf_op jit(solution)/shard_map/ppermute | solution.py:237
  85.0 29.1 %collective-permute-start.7 = (bf16[560,128]{1,0:T(8,128)(2,1)S(1)}, bf16[560,128]{1,0:T(8,128)(2,1)S(1)}, u32[]{:S(2)}, u32[]{:S(2)}) collective-permute-start(bf16[560,128]{1,0:T(8,128)(2,1)S(1)} %get-tuple-element.34), channel_id=1, source_target_pairs={{0,4},{4,0},{8,12},{12,8},{1,5},{5,1},{9,13},{13,9},{2,6},{6,2},{1... | collective-permute-start | bytes 430088 | tf_op jit(solution)/shard_map/ppermute | solution.py:237
  85.1 30.5 %collective-permute-start.8 = (bf16[560,128]{1,0:T(8,128)(2,1)S(1)}, bf16[560,128]{1,0:T(8,128)(2,1)S(1)}, u32[]{:S(2)}, u32[]{:S(2)}) collective-permute-start(bf16[560,128]{1,0:T(8,128)(2,1)S(1)} %get-tuple-element.35), channel_id=1, source_target_pairs={{0,8},{4,12},{8,0},{12,4},{1,9},{5,13},{9,1},{13,5},{2,10},{6,14},... | collective-permute-start | bytes 430088 | tf_op jit(solution)/shard_map/ppermute | solution.py:237
  88.1 27.4 %collective-permute-start.9 = (bf16[560,128]{1,0:T(8,128)(2,1)S(1)}, bf16[560,128]{1,0:T(8,128)(2,1)S(1)}, u32[]{:S(2)}, u32[]{:S(2)}) collective-permute-start(bf16[560,128]{1,0:T(8,128)(2,1)S(1)} %get-tuple-element.36), channel_id=1, source_target_pairs={{0,12},{4,8},{8,4},{12,0},{1,13},{5,9},{9,5},{13,1},{2,14},{6,10},... | collective-permute-start | bytes 430088 | tf_op jit(solution)/shard_map/ppermute | solution.py:237
  89.5 20.9 %collective-permute-start.11 = (bf16[512,128]{1,0:T(8,128)(2,1)S(1)}, bf16[512,128]{1,0:T(8,128)(2,1)S(1)}, u32[]{:S(2)}, u32[]{:S(2)}) collective-permute-start(bf16[512,128]{1,0:T(8,128)(2,1)S(1)} %get-tuple-element.39), channel_id=1, source_target_pairs={{0,8},{4,12},{8,0},{12,4},{1,9},{5,13},{9,1},{13,5},{2,10},{6,14},... | collective-permute-start | bytes 393224 | tf_op jit(solution)/shard_map/ppermute | solution.py:237
  89.7 20.7 %collective-permute-start.12 = (bf16[512,128]{1,0:T(8,128)(2,1)S(1)}, bf16[512,128]{1,0:T(8,128)(2,1)S(1)}, u32[]{:S(2)}, u32[]{:S(2)}) collective-permute-start(bf16[512,128]{1,0:T(8,128)(2,1)S(1)} %get-tuple-element.40), channel_id=1, source_target_pairs={{0,12},{4,8},{8,4},{12,0},{1,13},{5,9},{9,5},{13,1},{2,14},{6,10},... | collective-permute-start | bytes 393224 | tf_op jit(solution)/shard_map/ppermute | solution.py:237
  110.4 10.7 %collective-permute-start.13 = (bf16[32,4096]{1,0:T(8,128)(2,1)S(1)}, bf16[32,4096]{1,0:T(8,128)(2,1)S(1)}, u32[]{:S(2)}, u32[]{:S(2)}) collective-permute-start(bf16[32,4096]{1,0:T(8,128)(2,1)S(1)} %copy-done.12), channel_id=1, source_target_pairs={{0,4},{4,0},{8,12},{12,8},{1,5},{5,1},{9,13},{13,9},{2,6},{6,2},{1... | collective-permute-start | bytes 786440 | tf_op jit(solution)/shard_map/ppermute | solution.py:237
  110.4 22.1 %collective-permute-start.14 = (bf16[32,4096]{1,0:T(8,128)(2,1)S(1)}, bf16[32,4096]{1,0:T(8,128)(2,1)S(1)}, u32[]{:S(2)}, u32[]{:S(2)}) collective-permute-start(bf16[32,4096]{1,0:T(8,128)(2,1)S(1)} %copy-done.12), channel_id=1, source_target_pairs={{0,8},{4,12},{8,0},{12,4},{1,9},{5,13},{9,1},{13,5},{2,10},{6,14},... | collective-permute-start | bytes 786440 | tf_op jit(solution)/shard_map/ppermute | solution.py:237
  114.1 18.3 %collective-permute-start.15 = (bf16[32,4096]{1,0:T(8,128)(2,1)S(1)}, bf16[32,4096]{1,0:T(8,128)(2,1)S(1)}, u32[]{:S(2)}, u32[]{:S(2)}) collective-permute-start(bf16[32,4096]{1,0:T(8,128)(2,1)S(1)} %copy-done.12), channel_id=1, source_target_pairs={{0,12},{4,8},{8,4},{12,0},{1,13},{5,9},{9,5},{13,1},{2,14},{6,10},... | collective-permute-start | bytes 786440 | tf_op jit(solution)/shard_map/ppermute | solution.py:237

commit v2 on v1

--- a/solution.py
+++ b/solution.py
@@ -11,7 +11,7 @@
 HIGHEST = lax.Precision.HIGHEST
 LANES = 128
 VMEM_SPEC = pl.BlockSpec(memory_space=pltpu.VMEM)
-ANY_SPEC = pl.BlockSpec(memory_space=pl.ANY)
+HBM_SPEC = pl.BlockSpec(memory_space=pltpu.HBM)
 f32 = jnp.float32
 bf16 = jnp.bfloat16
 
@@ -36,7 +36,11 @@
     return pltpu.with_memory_space_constraint(x, pltpu.VMEM)
 
 
-def call(kernel, out_shape, *args, scratch=(), specs=None, vmem=16 << 20, cost=None):
+def after(x, *others):
+    return lax.optimization_barrier((x, *others))[0]
+
+
+def call(kernel, out_shape, *args, scratch=(), specs=None, vmem=7 << 20):
     outs = out_shape if isinstance(out_shape, (tuple, list)) else (out_shape,)
     out_specs = tuple(VMEM_SPEC for _ in outs)
     result = pl.pallas_call(
@@ -46,7 +50,7 @@
         out_specs=out_specs,
         scratch_shapes=list(scratch),
         compiler_params=pltpu.CompilerParams(vmem_limit_bytes=vmem),
-        cost_estimate=cost,
+        cost_estimate=pl.CostEstimate(flops=0, transcendentals=0, bytes_accessed=0),
     )(*args)
     return result if isinstance(out_shape, (tuple, list)) else result[0]
 
@@ -55,11 +59,13 @@
     return jax.ShapeDtypeStruct(dims, dtype)
 
 
-def fetch_kernel(pieces, src, dst, sems):
-    rows = src.shape[0] // pieces
+def fetch_kernel(pieces, first, src, dst, sems):
+    rows = dst.shape[0] // pieces
     copies = [
         pltpu.make_async_copy(
-            src.at[pl.ds(i * rows, rows)], dst.at[pl.ds(i * rows, rows)], sems.at[i]
+            src.at[pl.ds(first + i * rows, rows)],
+            dst.at[pl.ds(i * rows, rows)],
+            sems.at[i],
         )
         for i in range(pieces)
     ]
@@ -69,15 +75,14 @@
         c.wait()
 
 
-def fetch(weight, pieces=8):
-    cost = pl.CostEstimate(flops=0, transcendentals=0, bytes_accessed=2 * weight.size * 2)
+def fetch(weight, first, rows, pieces=4):
     return call(
-        functools.partial(fetch_kernel, pieces),
-        pltpu.VMEM(weight.shape, weight.dtype),
-        weight,
+        functools.partial(fetch_kernel, pieces, first),
+        pltpu.VMEM((rows, weight.shape[1]), weight.dtype),
+        pltpu.with_memory_space_constraint(weight, pltpu.HBM),
         scratch=[pltpu.SemaphoreType.DMA((pieces,))],
-        specs=[ANY_SPEC],
-        cost=cost,
+        specs=[HBM_SPEC],
+        vmem=1 << 20,
     )
 
 
@@ -119,65 +124,83 @@
         full[pl.ds(pl.multiple_of((position ^ k) * n, n), n), :] = piece[...]
 
 
-def hidden_kernel(flip, block, o0, o1, o2, o3, w, exit_ref, entry, out, low_ref, full):
+def hidden_kernel(flip, half, block, o0, o1, o2, o3, w, exit_ref, entry, *rest):
+    outs, full = rest[:-1], rest[-1]
+    n = outs[0].shape[0]
     place_rows(full, (o0, o1, o2, o3), lax.axis_index("row"))
-    half = out.shape[1]
     which = lax.rem(lax.axis_index("col"), 2) ^ flip
     low = contract_trailing(exit_ref[...], full[...])
-    low_ref[...] = low
+    outs[0][: low.shape[0], half:] = low
     for i in range(half // block):
         rows = pl.ds(pl.multiple_of(which * half + i * block, block), block)
-        out[:, i * block : (i + 1) * block] = contract_trailing(
-            full[...], w[rows, :]
-        ) + adapter_scale * contract_leading(
+        piece = contract_trailing(full[...], w[rows, :]) + adapter_scale * contract_leading(
             low, entry[:, rows].astype(f32), HIGHEST
         )
-
-
-def payload_kernel(keep, got, low, low_got, out):
-    total = keep[...] + got[...]
-    rows, half = total.shape
-    for i in range(half // LANES):
-        out[i * rows : (i + 1) * rows, :] = total[:, i * LANES : (i + 1) * LANES].astype(bf16)
-    store_terms(out, half // LANES * rows, low[...] + low_got[...])
-
-
-def gradient_kernel(mine, other, a, b, out, low_ref):
+        for j, out in enumerate(outs):
+            out[:, i * block : (i + 1) * block] = piece[j * n : (j + 1) * n, :]
+
+
+def payload_kernel(rank, half, keep, *rest):
+    got, outs = rest[:-2], rest[-2:]
+    rows = keep.shape[0]
+    n = got[0].shape[0]
+    blocks = half // LANES // 2
+    for j, ref in enumerate(got):
+        total = keep[j * n : (j + 1) * n, :] + ref[...]
+        for i in range(2 * blocks):
+            first = i % blocks * rows + j * n
+            outs[i // blocks][first : first + n, :] = total[
+                :, i * LANES : (i + 1) * LANES
+            ].astype(bf16)
+        if j == 0:
+            store_terms(outs[0], blocks * rows, total[:rank, half:])
+
+
+def gradient_kernel(mine0, mine1, other0, other1, a, b, *outs):
+    gate_outs, up_outs, low_ref = outs[:2], outs[2:4], outs[4]
     rows = a.shape[0]
-    half = out.shape[2]
+    n, half = up_outs[0].shape
     rank = low_ref.shape[0]
-    blocks = half // LANES
+    blocks = half // LANES // 2
     start = pl.multiple_of(lax.rem(lax.axis_index("col"), 2) * half, half)
-    for i in range(blocks):
-        here = slice(i * rows, (i + 1) * rows)
+    for i in range(2 * blocks):
+        here = slice(i % blocks * rows, (i % blocks + 1) * rows)
+        mine, other = (mine0, other0) if i < blocks else (mine1, other1)
         grad = mine[here, :].astype(f32) + other[here, :].astype(f32)
         lanes = pl.ds(pl.multiple_of(start + i * LANES, LANES), LANES)
-        out[0, :, i * LANES : (i + 1) * LANES] = (grad * a[:, lanes]).astype(bf16)
-        out[1, :, i * LANES : (i + 1) * LANES] = (grad * b[:, lanes]).astype(bf16)
-    low_ref[...] = load_terms(mine, blocks * rows, rank) + load_terms(other, blocks * rows, rank)
-
-
-def inputs_kernel(first, with_low, block, own, mate, wg, wu, exit_ref, entry, *rest):
+        for refs, factor in ((gate_outs, a), (up_outs, b)):
+            value = (grad * factor[:, lanes]).astype(bf16)
+            for j, ref in enumerate(refs):
+                ref[:, i * LANES : (i + 1) * LANES] = value[j * n : (j + 1) * n, :]
+    low_ref[...] = load_terms(mine0, blocks * rows, rank) + load_terms(other0, blocks * rows, rank)
+
+
+def place_halves(full, own, mate):
+    n, half = own[0].shape
+    par = lax.rem(lax.axis_index("col"), 2)
+    for position, refs in ((par, own), (1 - par, mate)):
+        lanes = pl.ds(pl.multiple_of(position * half, half), half)
+        for j, ref in enumerate(refs):
+            full[j * n : (j + 1) * n, lanes] = ref[...]
+
+
+def inputs_kernel(first, with_low, block, *refs):
+    own, mate, (wg, wu, exit_ref, entry), rest = refs[:4], refs[4:8], refs[8:12], refs[12:]
     own_out, s1, s2, s3 = rest[:4]
     low_ref = rest[4] if with_low else None
     gg, ug, acc = rest[-3:]
-    half = own.shape[2]
     width = acc.shape[1]
     rank = exit_ref.shape[0]
-    par = lax.rem(lax.axis_index("col"), 2)
-    mine = pl.ds(pl.multiple_of(par * half, half), half)
-    theirs = pl.ds(pl.multiple_of((1 - par) * half, half), half)
-    gg[:, mine] = own[0]
-    ug[:, mine] = own[1]
-    gg[:, theirs] = mate[0]
-    ug[:, theirs] = mate[1]
+    place_halves(gg, own[:2], mate[:2])
+    place_halves(ug, own[2:], mate[2:])
     low = contract_trailing(exit_ref[...], ug[...])
     for i in range(width // block):
-        rows = slice(first + i * block, first + (i + 1) * block)
+        rows = slice(i * block, (i + 1) * block)
+        lanes = slice(first + i * block, first + (i + 1) * block)
         acc[:, i * block : (i + 1) * block] = (
             contract_trailing(gg[...], wg[rows, :])
             + contract_trailing(ug[...], wu[rows, :])
-            + adapter_scale * contract_leading(low, entry[:, rows].astype(f32), HIGHEST)
+            + adapter_scale * contract_leading(low, entry[:, lanes].astype(f32), HIGHEST)
         )
     row = lax.axis_index("row")
     n = own_out.shape[0]
@@ -192,12 +215,16 @@
         low_ref[...] = low
 
 
-def finish_kernel(own, r1, r2, r3, out):
+def finish_kernel(own, r1, r2, r3, *rest):
+    done, out = rest[:-1], rest[-1]
     n, width = own.shape
+    first = out.shape[1] - width
+    for ref in done:
+        out[:, :first] = ref[...]
     for i in range(width // LANES):
         here = slice(i * n, (i + 1) * n)
         lanes = slice(i * LANES, (i + 1) * LANES)
-        out[:, lanes] = (
+        out[:, first + i * LANES : first + (i + 1) * LANES] = (
             own[:, lanes]
             + r1[here, :].astype(f32)
             + r2[here, :].astype(f32)
@@ -205,26 +232,45 @@
         ).astype(bf16)
 
 
-def entry_kernel(offset, i0, i1, i2, i3, low, r1, r2, r3, out, full, lows):
+def stack_kernel(top, bottom, *outs):
+    n = top.shape[0]
+    first = 0
+    for out in outs:
+        lanes = slice(first, first + out.shape[1])
+        out[:n, :] = top[:, lanes]
+        out[n:, :] = bottom[:, lanes]
+        first = lanes.stop
+
+
+def entry_kernel(offset, pieces, low, r1, r2, r3, *rest):
+    near, far = rest[:pieces], rest[pieces : 2 * pieces]
+    out, full, lows = rest[2 * pieces :]
     row = lax.axis_index("row")
     rank = low.shape[0]
-    place_rows(full, (i0, i1, i2, i3), row)
+    n = near[0].shape[0] // 2
+    first = 0
+    for here, there in zip(near, far):
+        lanes = slice(first, first + here.shape[1])
+        for k in range(4):
+            ref = here if k < 2 else there
+            rows = pl.ds(pl.multiple_of((row ^ k) * n, n), n)
+            full[rows, lanes] = ref[(k % 2) * n : (k % 2 + 1) * n, :]
+        first = lanes.stop
     lows[row] = low[...]
     for k, ref in ((1, r1), (2, r2), (3, r3)):
         lows[row ^ k] = load_terms(ref, offset, rank)
     total = (lows[0] + lows[1]) + (lows[2] + lows[3])
-    parts = split_terms(total)
-    full_inputs = full[...]
+    whole = full[...]
     out[...] = adapter_scale * sum(
-        jnp.dot(part, full_inputs, preferred_element_type=f32) for part in parts
-    )
-
-
-def small_kernel(own, mate, low, hidden, up_act, down_act, o0, o1, o2, o3, up_exit, down_entry, down_exit, full, ug):
-    half = own.shape[2]
-    par = lax.rem(lax.axis_index("col"), 2)
-    ug[:, pl.ds(pl.multiple_of(par * half, half), half)] = own[1]
-    ug[:, pl.ds(pl.multiple_of((1 - par) * half, half), half)] = mate[1]
+        jnp.dot(term, whole, preferred_element_type=f32) for term in split_terms(total)
+    )
+
+
+def small_kernel(
+    own0, own1, mate0, mate1, low, hidden, up_act, down_act, o0, o1, o2, o3, *rest
+):
+    up_exit, down_entry, down_exit, full, ug = rest
+    place_halves(ug, (own0, own1), (mate0, mate1))
     place_rows(full, (o0, o1, o2, o3), lax.axis_index("row"))
     up_exit[...] = adapter_scale * jnp.dot(up_act[...], ug[...], preferred_element_type=f32)
     down_entry[...] = adapter_scale * jnp.dot(
@@ -237,7 +283,8 @@
     return lax.ppermute(x, axis, [(i, i ^ distance) for i in range(n)])
 
 
-CHUNKS = 2
+EIGHTHS = (4,4)
+CHUNKS = len(EIGHTHS)
 
 
 def exchange_body(
@@ -261,22 +308,25 @@
     half = hidden // 2
     own_gradient = output_gradient
     gathered = [swap(own_gradient, "row", k, 4) for k in (1, 2, 3)]
-    down_v = fetch(down_weight)
-    gate_v = fetch(gate_weight)
-    up_v = fetch(up_weight)
+    parts = [width // 8 * e for e in EIGHTHS]
+    firsts = [sum(parts[:c]) for c in range(CHUNKS)]
+    down_v = fetch(down_weight, 0, hidden)
+    gate_v = [fetch(gate_weight, firsts[c], parts[c]) for c in range(CHUNKS)]
+    up_v = [fetch(up_weight, firsts[c], parts[c]) for c in range(CHUNKS)]
     a, b, hidden_state = call(
         factors_kernel,
         (shape((tokens, hidden), f32), shape((tokens, hidden), f32), shape((tokens, hidden), bf16)),
         gate_preactivation,
         up_preactivation,
     )
-    gathered_inputs = [swap(inputs, "row", k, 4) for k in (1, 2, 3)]
-
-    def hidden_half(flip):
+    near = [call(stack_kernel, shape((2 * share, width), bf16), inputs, swap(inputs, "row", 1, 4))]
+    down_v = after(down_v, gate_v, up_v, a, b, near)
+
+    def hidden_half(flip, gradient, split):
         return call(
-            functools.partial(hidden_kernel, flip, 512),
-            (shape((tokens, half), f32), shape((rank, tokens), f32)),
-            own_gradient,
+            functools.partial(hidden_kernel, flip, half, 512),
+            (shape((tokens // split, half + LANES), f32),) * split,
+            gradient,
             *gathered,
             in_vmem(down_v),
             down_adapter_exit,
@@ -284,62 +334,76 @@
             scratch=[pltpu.VMEM((tokens, width), bf16)],
         )
 
-    send, low_piece = hidden_half(1)
-    got = swap(send, "col", 1, 4)
-    low_got = swap(low_piece, "col", 1, 4)
-    keep, low_piece2 = hidden_half(0)
+    send = hidden_half(1, own_gradient, 4)
+    got = [swap(x, "col", 1, 4) for x in send]
+    keep = hidden_half(0, after(own_gradient, send), 1)[0]
     blocks = half // LANES
+    far = [swap(near[0], "row", 2, 4)]
     payload = call(
-        payload_kernel,
-        shape((blocks * tokens + 3 * rank, LANES), bf16),
+        functools.partial(payload_kernel, rank, half),
+        (
+            shape((blocks // 2 * tokens + 3 * rank, LANES), bf16),
+            shape((blocks // 2 * tokens, LANES), bf16),
+        ),
         keep,
-        got,
-        low_piece2,
-        low_got,
-    )
-    other = swap(payload, "col", 2, 4)
-    grads, low_full = call(
+        *got,
+    )
+    other = [swap(x, "col", 2, 4) for x in payload]
+    *grads, low_full = call(
         gradient_kernel,
-        (shape((2, tokens, half), bf16), shape((rank, tokens), f32)),
-        payload,
-        other,
+        (shape((tokens // 2, half), bf16),) * 4 + (shape((rank, tokens), f32),),
+        *payload,
+        *other,
         a,
         b,
     )
-    mate_grads = swap(grads, "col", 1, 4)
-
-    part = width // CHUNKS
-    rows = part // LANES * share
+    mate_grads = [swap(x, "col", 1, 4) for x in grads]
+
     owns, received = [], []
-    low_up = None
+    outs = ()
     for c in range(CHUNKS):
         with_low = c == 0
+        rows = parts[c] // LANES * share
         sent = shape((rows + (3 * rank if with_low else 0), LANES), bf16)
         outs = call(
-            functools.partial(inputs_kernel, c * part, with_low, 512),
-            (shape((share, part), f32), sent, sent, sent)
+            functools.partial(inputs_kernel, firsts[c], with_low, 512),
+            (shape((share, parts[c]), f32), sent, sent, sent)
             + ((shape((rank, tokens), f32),) if with_low else ()),
-            grads,
-            mate_grads,
-            in_vmem(gate_v),
-            in_vmem(up_v),
+            *grads,
+            *mate_grads,
+            in_vmem(after(gate_v[c], outs, far) if c else gate_v[c]),
+            in_vmem(up_v[c]),
             up_adapter_exit,
             up_adapter_entry,
             scratch=[
                 pltpu.VMEM((tokens, hidden), bf16),
                 pltpu.VMEM((tokens, hidden), bf16),
-                pltpu.VMEM((tokens, part), f32),
+                pltpu.VMEM((tokens, parts[c]), f32),
             ],
         )
         if with_low:
             low_up = outs[4]
         owns.append(outs[0])
         received.append([swap(outs[k], "row", k, 4) for k in (1, 2, 3)])
+    input_grad = ()
+    for c in range(CHUNKS):
+        done = shape((share, firsts[c] + parts[c]), bf16)
+        own = after(owns[c], owns[c + 1]) if c + 1 < CHUNKS else owns[c]
+        input_grad = (call(finish_kernel, done, own, *received[c], *input_grad),)
+    entry_sum = call(
+        functools.partial(entry_kernel, parts[0] // LANES * share, 1),
+        shape((rank, width), f32),
+        after(low_up, owns),
+        *received[0],
+        *near,
+        *far,
+        scratch=[pltpu.VMEM((tokens, width), bf16), pltpu.VMEM((4, rank, tokens), f32)],
+    )
     up_exit_gradient, down_entry_gradient, down_exit_gradient = call(
         small_kernel,
         (shape((rank, hidden), f32), shape((rank, hidden), f32), shape((rank, width), f32)),
-        grads,
-        mate_grads,
+        *grads[2:],
+        *mate_grads[2:],
         low_full,
         hidden_state,
         up_adapter_activations,
@@ -348,22 +412,9 @@
         *gathered,
         scratch=[pltpu.VMEM((tokens, width), bf16), pltpu.VMEM((tokens, hidden), bf16)],
     )
-    up_entry_gradient = call(
-        functools.partial(entry_kernel, rows),
-        shape((rank, width), f32),
-        inputs,
-        *gathered_inputs,
-        low_up,
-        *received[0],
-        scratch=[pltpu.VMEM((tokens, width), bf16), pltpu.VMEM((4, rank, tokens), f32)],
-    )
-    pieces = [
-        call(finish_kernel, shape((share, part), bf16), owns[c], *received[c])
-        for c in range(CHUNKS)
-    ]
     return (
-        jnp.concatenate(pieces, axis=1),
-        up_entry_gradient,
+        input_grad[0],
+        entry_sum,
         up_exit_gradient,
         down_entry_gradient,
         down_exit_gradient,

time: 136 us -> 97.2 us (0.71); the launches traced: 134 us -> 97.1 us
  waiting for transfers between devices: 51.8 us -> 16.5 us
  Pallas kernels: 26.8 us -> 44 us
  local copies, waits for them, and re-layouts: 28.9 us -> 13.4 us
  starting transfers between devices: 24.7 us -> 22.3 us
    ppermute x16 -> x21, waiting for transfers between devices: 51.8 us -> 16.5 us  [swap(): return lax.ppermute(x, axis, [(i, i ^ distance) for i in range(n)])]
    pallas_call x14 -> x17, Pallas kernels: 26.8 us -> 44 us  [call(): pl.pallas_call(kernel, out_shape=tuple(outs), in_specs=specs if specs is...]
    unnamed x30 -> x28, local copies, waits for them, and re-layouts: 28.9 us -> 13.4 us
    ppermute x16 -> x21, starting transfers between devices: 24.7 us -> 22.3 us  [swap(): return lax.ppermute(x, axis, [(i, i ^ distance) for i in range(n)])]
  transfers between devices with their start and end apart: 16 -> 21, of which waited for: 6 -> 6; matrix products, arithmetic and copies ran while one was open for 1% -> 0% of each run, Pallas kernels for 12% -> 40%
where the time goes in v2:
time: 97.2 us; the launch traced here: 97.1 us
  Pallas kernels  44 us (45%)
  starting transfers between devices  22.3 us (23%)
  waiting for transfers between devices  16.5 us (17%)
  local copies, waits for them, and re-layouts  13.4 us (14%)
    pallas_call x17, Pallas kernels, call(): pl.pallas_call(kernel, out_shape=tuple(outs), in_specs=specs if specs is...  44 us
    ppermute x21, starting transfers between devices, swap(): return lax.ppermute(x, axis, [(i, i ^ distance) for i in range(n)])  22.3 us
    ppermute x21, waiting for transfers between devices, swap(): return lax.ppermute(x, axis, [(i, i ^ distance) for i in range(n)])  16.5 us
    unnamed x28, local copies, waits for them, and re-layouts  13.4 us
  transfers between devices with their start and end apart: 21, of which 6 were waited for; matrix products, arithmetic and copies ran while one was open for 0% of the time, Pallas kernels for 40%

profile of v2, /device:TPU:0, one launch (start us, length us, event | category | flops | bytes accessed | tf_op | source)
XLA Modules:
  0.0 97.1 jit_solution(10256251688012932853)
XLA Ops:
  0.6 3.1 %collective-permute-start.3 = (bf16[32,4096]{1,0:T(8,128)(2,1)}, bf16[32,4096]{1,0:T(8,128)(2,1)S(1)}, u32[]{:S(2)}, u32[]{:S(2)}) collective-permute-start(bf16[32,4096]{1,0:T(8,128)(2,1)} %top.1), channel_id=1, source_target_pairs={{0,4},{4,0},{8,12},{12,8},{1,5},{5,1},{9,13},{13,9},{2,6},{6,2},{1... | collective-permute-start | bytes 786440 | tf_op jit(solution)/shard_map/ppermute | solution.py:283
  3.8 3.0 %collective-permute-start.1 = (bf16[32,4096]{1,0:T(8,128)(2,1)}, bf16[32,4096]{1,0:T(8,128)(2,1)S(1)}, u32[]{:S(2)}, u32[]{:S(2)}) collective-permute-start(bf16[32,4096]{1,0:T(8,128)(2,1)} %o0.4), channel_id=1, source_target_pairs={{0,8},{4,12},{8,0},{12,4},{1,9},{5,13},{9,1},{13,5},{2,10},{6,14},... | collective-permute-start | bytes 786440 | tf_op jit(solution)/shard_map/ppermute | solution.py:283
  6.8 1.3 %collective-permute-start.2 = (bf16[32,4096]{1,0:T(8,128)(2,1)}, bf16[32,4096]{1,0:T(8,128)(2,1)S(1)}, u32[]{:S(2)}, u32[]{:S(2)}) collective-permute-start(bf16[32,4096]{1,0:T(8,128)(2,1)} %o0.4), channel_id=1, source_target_pairs={{0,12},{4,8},{8,4},{12,0},{1,13},{5,9},{9,5},{13,1},{2,14},{6,10},... | collective-permute-start | bytes 786440 | tf_op jit(solution)/shard_map/ppermute | solution.py:283
  8.1 3.5 %shard_map.165.refs_8_ = bf16[2048,2048]{1,0:T(8,128)(2,1)S(1)} custom-call(bf16[4096,2048]{1,0:T(8,128)(2,1)} %src.7), custom_call_target="tpu_custom_call" | custom-call | tf_op jit(solution)/shard_map/pallas_call | solution.py:46
  11.6 3.3 %copy-done = bf16[2048,2048]{1,0:T(8,128)(2,1)} copy-done((bf16[2048,2048]{1,0:T(8,128)(2,1)}, bf16[2048,2048]{1,0:T(8,128)(2,1)S(1)}, u32[]{:S(2)}) %copy-start) | copy-done | bytes 8388632
  14.9 3.5 %shard_map.166.refs_8_ = bf16[2048,2048]{1,0:T(8,128)(2,1)S(1)} custom-call(bf16[4096,2048]{1,0:T(8,128)(2,1)} %src.7), custom_call_target="tpu_custom_call" | custom-call | tf_op jit(solution)/shard_map/pallas_call | solution.py:46
  18.4 3.5 %shard_map.167.refs_9_ = bf16[2048,2048]{1,0:T(8,128)(2,1)S(1)} custom-call(bf16[4096,2048]{1,0:T(8,128)(2,1)} %src.9), custom_call_target="tpu_custom_call" | custom-call | tf_op jit(solution)/shard_map/pallas_call | solution.py:46
  21.9 3.2 %copy-done.2 = bf16[2048,2048]{1,0:T(8,128)(2,1)} copy-done((bf16[2048,2048]{1,0:T(8,128)(2,1)}, bf16[2048,2048]{1,0:T(8,128)(2,1)S(1)}, u32[]{:S(2)}) %copy-start.2) | copy-done | bytes 8388632
  25.2 3.5 %shard_map.168.refs_9_ = bf16[2048,2048]{1,0:T(8,128)(2,1)S(1)} custom-call(bf16[4096,2048]{1,0:T(8,128)(2,1)} %src.9), custom_call_target="tpu_custom_call" | custom-call | tf_op jit(solution)/shard_map/pallas_call | solution.py:46
  28.8 6.0 %shard_map.164.w = bf16[2048,4096]{1,0:T(8,128)(2,1)S(1)} custom-call(bf16[2048,4096]{1,0:T(8,128)(2,1)} %src.5), custom_call_target="tpu_custom_call" | custom-call | tf_op jit(solution)/shard_map/pallas_call | solution.py:46
  34.8 0.6 shard_map.169
  35.6 4.0 %shard_map.171 = (f32[32,1152]{1,0:T(8,128)S(1)}, f32[32,1152]{1,0:T(8,128)S(1)}, f32[32,1152]{1,0:T(8,128)S(1)}, f32[32,1152]{1,0:T(8,128)S(1)}) custom-call(bf16[32,4096]{1,0:T(8,128)(2,1)S(1)} %copy-done.4, bf16[32,4096]{1,0:T(8,128)(2,1)S(1)} %collective-permute-done.o1, bf16[32,4096]{1,0:T(8,128)(2,1)S(1)} %collective-permute-done.1.o2, ...), custom_call_target="tpu_custom_call" | custom-call | tf_op jit(solution)/shard_map/pallas_call | solution.py:46
  39.6 0.5 collective-permute-start.5
  40.6 1.7 %collective-permute-start.14 = (bf16[64,4096]{1,0:T(8,128)(2,1)S(1)}, bf16[64,4096]{1,0:T(8,128)(2,1)S(1)}, u32[]{:S(2)}, u32[]{:S(2)}) collective-permute-start(bf16[64,4096]{1,0:T(8,128)(2,1)S(1)} %shard_map.170.rest_0_), channel_id=1, source_target_pairs={{0,8},{4,12},{8,0},{12,4},{1,9},{5,13},{9,1},{13,5},{2,10},{6,14},... | collective-permute-start | bytes 1572872 | tf_op jit(solution)/shard_map/ppermute | solution.py:283
  42.3 4.0 %shard_map.172.keep = f32[128,1152]{1,0:T(8,128)S(1)} custom-call(bf16[32,4096]{1,0:T(8,128)(2,1)S(1)} %copy-done.4, bf16[32,4096]{1,0:T(8,128)(2,1)S(1)} %collective-permute-done.o1, bf16[32,4096]{1,0:T(8,128)(2,1)S(1)} %collective-permute-done.1.o2, bf16[32,4096]{1,0:T(8,128)(2,1)S(1)} %collective-permute-done.2.o3, bf16[2048,4096]{1,0:T(8,128)(2,1)S(1)} %shard_map.164.w, ...), custom_call_target="tpu_custom_call" | custom-call | tf_op jit(solution)/shard_map/pallas_call | solution.py:46
  46.4 1.6 %collective-permute-start.8 = (bf16[560,128]{1,0:T(8,128)(2,1)S(1)}, bf16[560,128]{1,0:T(8,128)(2,1)S(1)}, u32[]{:S(2)}, u32[]{:S(2)}) collective-permute-start(bf16[560,128]{1,0:T(8,128)(2,1)S(1)} %get-tuple-element.44.mine0), channel_id=1, source_target_pairs={{0,2},{1,3},{2,0},{3,1},{4,6},{5,7},{6,4},{7,5},{8,10},{9,11},{10,... | collective-permute-start | bytes 430088 | tf_op jit(solution)/shard_map/ppermute | solution.py:283
  48.0 0.5 collective-permute-start.9
  48.5 6.2 %collective-permute-done.9.other1 = bf16[512,128]{1,0:T(8,128)(2,1)S(1)} collective-permute-done((bf16[512,128]{1,0:T(8,128)(2,1)S(1)}, bf16[512,128]{1,0:T(8,128)(2,1)S(1)}, u32[]{:S(2)}, u32[]{:S(2)}) %collective-permute-start.9) | collective-permute-done | bytes 131104 | tf_op jit(solution)/shard_map/ppermute | solution.py:283
  55.0 0.5 collective-permute-start.13
  57.1 3.4 %copy-done.1 = bf16[2048,2048]{1,0:T(8,128)(2,1)S(1)} copy-done((bf16[2048,2048]{1,0:T(8,128)(2,1)S(1)}, bf16[2048,2048]{1,0:T(8,128)(2,1)}, u32[]{:S(2)}) %copy-start.1) | copy-done | bytes 8388632
  60.5 3.4 %copy-done.3 = bf16[2048,2048]{1,0:T(8,128)(2,1)S(1)} copy-done((bf16[2048,2048]{1,0:T(8,128)(2,1)S(1)}, bf16[2048,2048]{1,0:T(8,128)(2,1)}, u32[]{:S(2)}) %copy-start.3) | copy-done | bytes 8388632
  63.9 5.8 %shard_map.175 = (f32[32,2048]{1,0:T(8,128)S(1)}, bf16[560,128]{1,0:T(8,128)(2,1)S(1)}, bf16[560,128]{1,0:T(8,128)(2,1)S(1)}, bf16[560,128]{1,0:T(8,128)(2,1)S(1)}, f32[16,128]{1,0:T(8,128)S(1)}) custom-call(bf16[64,1024]{1,0:T(8,128)(2,1)S(1)} %get-tuple-element.46.refs_0_, bf16[64,1024]{1,0:T(8,128)(2,1)S(1)} %get-tuple-element.47.refs_1_, ...), custom_call_target="tpu_custom_call" | custom-call | tf_op jit(solution)/shard_map/pallas_call | solution.py:46
  69.6 1.4 %collective-permute-start.18 = (bf16[560,128]{1,0:T(8,128)(2,1)S(1)}, bf16[560,128]{1,0:T(8,128)(2,1)S(1)}, u32[]{:S(2)}, u32[]{:S(2)}) collective-permute-start(bf16[560,128]{1,0:T(8,128)(2,1)S(1)} %get-tuple-element.51), channel_id=1, source_target_pairs={{0,4},{4,0},{8,12},{12,8},{1,5},{5,1},{9,13},{13,9},{2,6},{6,2},{1... | collective-permute-start | bytes 430088 | tf_op jit(solution)/shard_map/ppermute | solution.py:283
  71.4 2.7 %collective-permute-start.20 = (bf16[560,128]{1,0:T(8,128)(2,1)S(1)}, bf16[560,128]{1,0:T(8,128)(2,1)S(1)}, u32[]{:S(2)}, u32[]{:S(2)}) collective-permute-start(bf16[560,128]{1,0:T(8,128)(2,1)S(1)} %get-tuple-element.53), channel_id=1, source_target_pairs={{0,12},{4,8},{8,4},{12,0},{1,13},{5,9},{9,5},{13,1},{2,14},{6,10},... | collective-permute-start | bytes 430088 | tf_op jit(solution)/shard_map/ppermute | solution.py:283
  74.1 6.0 %shard_map.176 = (f32[32,2048]{1,0:T(8,128)S(1)}, bf16[512,128]{1,0:T(8,128)(2,1)S(1)}, bf16[512,128]{1,0:T(8,128)(2,1)S(1)}, bf16[512,128]{1,0:T(8,128)(2,1)S(1)}) custom-call(bf16[64,1024]{1,0:T(8,128)(2,1)S(1)} %get-tuple-element.46.refs_0_, bf16[64,1024]{1,0:T(8,128)(2,1)S(1)} %get-tuple-element.47.refs_1_, ...), custom_call_target="tpu_custom_call" | custom-call | tf_op jit(solution)/shard_map/pallas_call | solution.py:46
  80.1 0.5 collective-permute-start.15
  80.6 1.2 %collective-permute-start.16 = (bf16[512,128]{1,0:T(8,128)(2,1)S(1)}, bf16[512,128]{1,0:T(8,128)(2,1)S(1)}, u32[]{:S(2)}, u32[]{:S(2)}) collective-permute-start(bf16[512,128]{1,0:T(8,128)(2,1)S(1)} %get-tuple-element.58), channel_id=1, source_target_pairs={{0,8},{4,12},{8,0},{12,4},{1,9},{5,13},{9,1},{13,5},{2,10},{6,14},... | collective-permute-start | bytes 393224 | tf_op jit(solution)/shard_map/ppermute | solution.py:283
  81.8 2.7 %collective-permute-start.17 = (bf16[512,128]{1,0:T(8,128)(2,1)S(1)}, bf16[512,128]{1,0:T(8,128)(2,1)S(1)}, u32[]{:S(2)}, u32[]{:S(2)}) collective-permute-start(bf16[512,128]{1,0:T(8,128)(2,1)S(1)} %get-tuple-element.59), channel_id=1, source_target_pairs={{0,12},{4,8},{8,4},{12,0},{1,13},{5,9},{9,5},{13,1},{2,14},{6,10},... | collective-permute-start | bytes 393224 | tf_op jit(solution)/shard_map/ppermute | solution.py:283
  84.5 1.2 %shard_map.180 = (f32[16,2048]{1,0:T(8,128)}, f32[16,2048]{1,0:T(8,128)}, f32[16,4096]{1,0:T(8,128)}) custom-call(bf16[64,1024]{1,0:T(8,128)(2,1)S(1)} %get-tuple-element.48.refs_2_.own0, bf16[64,1024]{1,0:T(8,128)(2,1)S(1)} %get-tuple-element.49.refs_3_.own1, bf16[64,1024]{1,0:T(8,128)(2,1)S(1)} %collective-permute-done.12.refs_6_.mate0, ...), custom_call_target="tpu_custom_call" | custom-call | tf_op jit(solution)/shard_map/pallas_call | solution.py:46
  85.7 1.3 %shard_map.179 = f32[16,4096]{1,0:T(8,128)} custom-call(f32[16,128]{1,0:T(8,128)S(1)} %get-tuple-element.61.low, bf16[560,128]{1,0:T(8,128)(2,1)S(1)} %collective-permute-done.18.r1, bf16[560,128]{1,0:T(8,128)(2,1)S(1)} %collective-permute-done.19.r2, bf16[560,128]{1,0:T(8,128)(2,1)S(1)} %collective-permute-done.20.r3, ...), custom_call_target="tpu_custom_call" | custom-call | tf_op jit(solution)/shard_map/pallas_call | solution.py:46
  87.1 9.1 %collective-permute-done.16.r2 = bf16[512,128]{1,0:T(8,128)(2,1)S(1)} collective-permute-done((bf16[512,128]{1,0:T(8,128)(2,1)S(1)}, bf16[512,128]{1,0:T(8,128)(2,1)S(1)}, u32[]{:S(2)}, u32[]{:S(2)}) %collective-permute-start.16) | collective-permute-done | bytes 131104 | tf_op jit(solution)/shard_map/ppermute | solution.py:283
  96.3 0.8 shard_map.178
  (55 shorter events, 3.0 us)
Async XLA Ops:
  0.6 34.8 %collective-permute-start.3 = (bf16[32,4096]{1,0:T(8,128)(2,1)}, bf16[32,4096]{1,0:T(8,128)(2,1)S(1)}, u32[]{:S(2)}, u32[]{:S(2)}) collective-permute-start(bf16[32,4096]{1,0:T(8,128)(2,1)} %top.1), channel_id=1, source_target_pairs={{0,4},{4,0},{8,12},{12,8},{1,5},{5,1},{9,13},{13,9},{2,6},{6,2},{1... | collective-permute-start | bytes 786440 | tf_op jit(solution)/shard_map/ppermute | solution.py:283
  3.7 31.8 %collective-permute-start = (bf16[32,4096]{1,0:T(8,128)(2,1)}, bf16[32,4096]{1,0:T(8,128)(2,1)S(1)}, u32[]{:S(2)}, u32[]{:S(2)}) collective-permute-start(bf16[32,4096]{1,0:T(8,128)(2,1)} %o0.4), channel_id=1, source_target_pairs={{0,4},{4,0},{8,12},{12,8},{1,5},{5,1},{9,13},{13,9},{2,6},{6,2},{1... | collective-permute-start | bytes 786440 | tf_op jit(solution)/shard_map/ppermute | solution.py:283
  3.8 31.7 %collective-permute-start.1 = (bf16[32,4096]{1,0:T(8,128)(2,1)}, bf16[32,4096]{1,0:T(8,128)(2,1)S(1)}, u32[]{:S(2)}, u32[]{:S(2)}) collective-permute-start(bf16[32,4096]{1,0:T(8,128)(2,1)} %o0.4), channel_id=1, source_target_pairs={{0,8},{4,12},{8,0},{12,4},{1,9},{5,13},{9,1},{13,5},{2,10},{6,14},... | collective-permute-start | bytes 786440 | tf_op jit(solution)/shard_map/ppermute | solution.py:283
  6.8 28.8 %collective-permute-start.2 = (bf16[32,4096]{1,0:T(8,128)(2,1)}, bf16[32,4096]{1,0:T(8,128)(2,1)S(1)}, u32[]{:S(2)}, u32[]{:S(2)}) collective-permute-start(bf16[32,4096]{1,0:T(8,128)(2,1)} %o0.4), channel_id=1, source_target_pairs={{0,12},{4,8},{8,4},{12,0},{1,13},{5,9},{9,5},{13,1},{2,14},{6,10},... | collective-permute-start | bytes 786440 | tf_op jit(solution)/shard_map/ppermute | solution.py:283
  28.7 6.1 %copy-start.7 = (bf16[128,2048]{1,0:T(8,128)(2,1)S(1)}, bf16[128,2048]{1,0:T(8,128)(2,1)}, u32[]{:S(2)}) copy-start(bf16[128,2048]{1,0:T(8,128)(2,1)} %g_ref.1) | copy-start | bytes 1572868
  28.7 6.1 %copy-start.8 = (bf16[128,2048]{1,0:T(8,128)(2,1)S(1)}, bf16[128,2048]{1,0:T(8,128)(2,1)}, u32[]{:S(2)}) copy-start(bf16[128,2048]{1,0:T(8,128)(2,1)} %u_ref.1) | copy-start | bytes 1572868
  28.7 6.7 %copy-start.11 = (bf16[32,4096]{1,0:T(8,128)(2,1)S(1)}, bf16[32,4096]{1,0:T(8,128)(2,1)}, u32[]{:S(2)}) copy-start(bf16[32,4096]{1,0:T(8,128)(2,1)} %top.1) | copy-start | bytes 786436
  28.7 6.8 %copy-start.4 = (bf16[32,4096]{1,0:T(8,128)(2,1)S(1)}, bf16[32,4096]{1,0:T(8,128)(2,1)}, u32[]{:S(2)}) copy-start(bf16[32,4096]{1,0:T(8,128)(2,1)} %o0.4) | copy-start | bytes 786436
  28.7 6.8 %copy-start.5 = (bf16[16,4096]{1,0:T(8,128)(2,1)S(1)}, bf16[16,4096]{1,0:T(8,128)(2,1)}, u32[]{:S(2)}) copy-start(bf16[16,4096]{1,0:T(8,128)(2,1)} %exit_ref.3) | copy-start | bytes 393220
  28.8 6.8 %copy-start.9 = (bf16[16,2048]{1,0:T(8,128)(2,1)S(1)}, bf16[16,2048]{1,0:T(8,128)(2,1)}, u32[]{:S(2)}) copy-start(bf16[16,2048]{1,0:T(8,128)(2,1)} %entry.3) | copy-start | bytes 196612
  35.5 21.6 %copy-start.6 = (bf16[16,4096]{1,0:T(8,128)(2,1)S(1)}, bf16[16,4096]{1,0:T(8,128)(2,1)}, u32[]{:S(2)}) copy-start(bf16[16,4096]{1,0:T(8,128)(2,1)} %refs_11_.3) | copy-start | bytes 393220
  35.5 21.6 %copy-start.10 = (bf16[16,2048]{1,0:T(8,128)(2,1)S(1)}, bf16[16,2048]{1,0:T(8,128)(2,1)}, u32[]{:S(2)}) copy-start(bf16[16,2048]{1,0:T(8,128)(2,1)} %refs_10_.3) | copy-start | bytes 196612
  39.6 6.8 %collective-permute-start.4 = (f32[32,1152]{1,0:T(8,128)S(1)}, f32[32,1152]{1,0:T(8,128)S(1)}, u32[]{:S(2)}, u32[]{:S(2)}) collective-permute-start(f32[32,1152]{1,0:T(8,128)S(1)} %get-tuple-element.39), channel_id=1, source_target_pairs={{0,1},{1,0},{2,3},{3,2},{4,5},{5,4},{6,7},{7,6},{8,9},{9,8},{10,11... | collective-permute-start | bytes 442376 | tf_op jit(solution)/shard_map/ppermute | solution.py:283
  39.6 6.7 %collective-permute-start.5 = (f32[32,1152]{1,0:T(8,128)S(1)}, f32[32,1152]{1,0:T(8,128)S(1)}, u32[]{:S(2)}, u32[]{:S(2)}) collective-permute-start(f32[32,1152]{1,0:T(8,128)S(1)} %get-tuple-element.40), channel_id=1, source_target_pairs={{0,1},{1,0},{2,3},{3,2},{4,5},{5,4},{6,7},{7,6},{8,9},{9,8},{10,11... | collective-permute-start | bytes 442376 | tf_op jit(solution)/shard_map/ppermute | solution.py:283
  40.1 6.2 %collective-permute-start.6 = (f32[32,1152]{1,0:T(8,128)S(1)}, f32[32,1152]{1,0:T(8,128)S(1)}, u32[]{:S(2)}, u32[]{:S(2)}) collective-permute-start(f32[32,1152]{1,0:T(8,128)S(1)} %get-tuple-element.41), channel_id=1, source_target_pairs={{0,1},{1,0},{2,3},{3,2},{4,5},{5,4},{6,7},{7,6},{8,9},{9,8},{10,11... | collective-permute-start | bytes 442376 | tf_op jit(solution)/shard_map/ppermute | solution.py:283
  40.2 6.2 %collective-permute-start.7 = (f32[32,1152]{1,0:T(8,128)S(1)}, f32[32,1152]{1,0:T(8,128)S(1)}, u32[]{:S(2)}, u32[]{:S(2)}) collective-permute-start(f32[32,1152]{1,0:T(8,128)S(1)} %get-tuple-element.42), channel_id=1, source_target_pairs={{0,1},{1,0},{2,3},{3,2},{4,5},{5,4},{6,7},{7,6},{8,9},{9,8},{10,11... | collective-permute-start | bytes 442376 | tf_op jit(solution)/shard_map/ppermute | solution.py:283
  40.6 33.5 %collective-permute-start.14 = (bf16[64,4096]{1,0:T(8,128)(2,1)S(1)}, bf16[64,4096]{1,0:T(8,128)(2,1)S(1)}, u32[]{:S(2)}, u32[]{:S(2)}) collective-permute-start(bf16[64,4096]{1,0:T(8,128)(2,1)S(1)} %shard_map.170.rest_0_), channel_id=1, source_target_pairs={{0,8},{4,12},{8,0},{12,4},{1,9},{5,13},{9,1},{13,5},{2,10},{6,14},... | collective-permute-start | bytes 1572872 | tf_op jit(solution)/shard_map/ppermute | solution.py:283
  46.4 8.3 %collective-permute-start.8 = (bf16[560,128]{1,0:T(8,128)(2,1)S(1)}, bf16[560,128]{1,0:T(8,128)(2,1)S(1)}, u32[]{:S(2)}, u32[]{:S(2)}) collective-permute-start(bf16[560,128]{1,0:T(8,128)(2,1)S(1)} %get-tuple-element.44.mine0), channel_id=1, source_target_pairs={{0,2},{1,3},{2,0},{3,1},{4,6},{5,7},{6,4},{7,5},{8,10},{9,11},{10,... | collective-permute-start | bytes 430088 | tf_op jit(solution)/shard_map/ppermute | solution.py:283
  48.0 6.8 %collective-permute-start.9 = (bf16[512,128]{1,0:T(8,128)(2,1)S(1)}, bf16[512,128]{1,0:T(8,128)(2,1)S(1)}, u32[]{:S(2)}, u32[]{:S(2)}) collective-permute-start(bf16[512,128]{1,0:T(8,128)(2,1)S(1)} %get-tuple-element.45.mine1), channel_id=1, source_target_pairs={{0,2},{1,3},{2,0},{3,1},{4,6},{5,7},{6,4},{7,5},{8,10},{9,11},{10,... | collective-permute-start | bytes 393224 | tf_op jit(solution)/shard_map/ppermute | solution.py:283
  55.0 1.4 %collective-permute-start.12 = (bf16[64,1024]{1,0:T(8,128)(2,1)S(1)}, bf16[64,1024]{1,0:T(8,128)(2,1)S(1)}, u32[]{:S(2)}, u32[]{:S(2)}) collective-permute-start(bf16[64,1024]{1,0:T(8,128)(2,1)S(1)} %get-tuple-element.48.refs_2_.own0), channel_id=1, source_target_pairs={{0,1},{1,0},{2,3},{3,2},{4,5},{5,4},{6,7},{7,6},{8,9},{9,8},{10,11... | collective-permute-start | bytes 393224 | tf_op jit(solution)/shard_map/ppermute | solution.py:283
  55.0 1.5 %collective-permute-start.13 = (bf16[64,1024]{1,0:T(8,128)(2,1)S(1)}, bf16[64,1024]{1,0:T(8,128)(2,1)S(1)}, u32[]{:S(2)}, u32[]{:S(2)}) collective-permute-start(bf16[64,1024]{1,0:T(8,128)(2,1)S(1)} %get-tuple-element.49.refs_3_.own1), channel_id=1, source_target_pairs={{0,1},{1,0},{2,3},{3,2},{4,5},{5,4},{6,7},{7,6},{8,9},{9,8},{10,11... | collective-permute-start | bytes 393224 | tf_op jit(solution)/shard_map/ppermute | solution.py:283
  55.5 1.3 %collective-permute-start.10 = (bf16[64,1024]{1,0:T(8,128)(2,1)S(1)}, bf16[64,1024]{1,0:T(8,128)(2,1)S(1)}, u32[]{:S(2)}, u32[]{:S(2)}) collective-permute-start(bf16[64,1024]{1,0:T(8,128)(2,1)S(1)} %get-tuple-element.46.refs_0_), channel_id=1, source_target_pairs={{0,1},{1,0},{2,3},{3,2},{4,5},{5,4},{6,7},{7,6},{8,9},{9,8},{10,11... | collective-permute-start | bytes 393224 | tf_op jit(solution)/shard_map/ppermute | solution.py:283
  55.6 1.5 %collective-permute-start.11 = (bf16[64,1024]{1,0:T(8,128)(2,1)S(1)}, bf16[64,1024]{1,0:T(8,128)(2,1)S(1)}, u32[]{:S(2)}, u32[]{:S(2)}) collective-permute-start(bf16[64,1024]{1,0:T(8,128)(2,1)S(1)} %get-tuple-element.47.refs_1_), channel_id=1, source_target_pairs={{0,1},{1,0},{2,3},{3,2},{4,5},{5,4},{6,7},{7,6},{8,9},{9,8},{10,11... | collective-permute-start | bytes 393224 | tf_op jit(solution)/shard_map/ppermute | solution.py:283
  57.1 3.4 %copy-start.1 = (bf16[2048,2048]{1,0:T(8,128)(2,1)S(1)}, bf16[2048,2048]{1,0:T(8,128)(2,1)}, u32[]{:S(2)}) copy-start(bf16[2048,2048]{1,0:T(8,128)(2,1)} %copy-done) | copy-start | bytes 25165828
  63.8 20.7 %copy-start.12 = (bf16[16,128]{1,0:T(8,128)(2,1)S(1)}, bf16[16,128]{1,0:T(8,128)(2,1)}, u32[]{:S(2)}) copy-start(bf16[16,128]{1,0:T(8,128)(2,1)} %up_act.1) | copy-start | bytes 12292
  63.8 20.7 %copy-start.13 = (bf16[16,128]{1,0:T(8,128)(2,1)S(1)}, bf16[16,128]{1,0:T(8,128)(2,1)}, u32[]{:S(2)}) copy-start(bf16[16,128]{1,0:T(8,128)(2,1)} %down_act.1) | copy-start | bytes 12292
  69.6 12.2 %collective-permute-start.18 = (bf16[560,128]{1,0:T(8,128)(2,1)S(1)}, bf16[560,128]{1,0:T(8,128)(2,1)S(1)}, u32[]{:S(2)}, u32[]{:S(2)}) collective-permute-start(bf16[560,128]{1,0:T(8,128)(2,1)S(1)} %get-tuple-element.51), channel_id=1, source_target_pairs={{0,4},{4,0},{8,12},{12,8},{1,5},{5,1},{9,13},{13,9},{2,6},{6,2},{1... | collective-permute-start | bytes 430088 | tf_op jit(solution)/shard_map/ppermute | solution.py:283
  71.1 14.7 %collective-permute-start.19 = (bf16[560,128]{1,0:T(8,128)(2,1)S(1)}, bf16[560,128]{1,0:T(8,128)(2,1)S(1)}, u32[]{:S(2)}, u32[]{:S(2)}) collective-permute-start(bf16[560,128]{1,0:T(8,128)(2,1)S(1)} %get-tuple-element.52), channel_id=1, source_target_pairs={{0,8},{4,12},{8,0},{12,4},{1,9},{5,13},{9,1},{13,5},{2,10},{6,14},... | collective-permute-start | bytes 430088 | tf_op jit(solution)/shard_map/ppermute | solution.py:283
  71.4 14.4 %collective-permute-start.20 = (bf16[560,128]{1,0:T(8,128)(2,1)S(1)}, bf16[560,128]{1,0:T(8,128)(2,1)S(1)}, u32[]{:S(2)}, u32[]{:S(2)}) collective-permute-start(bf16[560,128]{1,0:T(8,128)(2,1)S(1)} %get-tuple-element.53), channel_id=1, source_target_pairs={{0,12},{4,8},{8,4},{12,0},{1,13},{5,9},{9,5},{13,1},{2,14},{6,10},... | collective-permute-start | bytes 430088 | tf_op jit(solution)/shard_map/ppermute | solution.py:283
  80.1 7.0 %collective-permute-start.15 = (bf16[512,128]{1,0:T(8,128)(2,1)S(1)}, bf16[512,128]{1,0:T(8,128)(2,1)S(1)}, u32[]{:S(2)}, u32[]{:S(2)}) collective-permute-start(bf16[512,128]{1,0:T(8,128)(2,1)S(1)} %get-tuple-element.57), channel_id=1, source_target_pairs={{0,4},{4,0},{8,12},{12,8},{1,5},{5,1},{9,13},{13,9},{2,6},{6,2},{1... | collective-permute-start | bytes 393224 | tf_op jit(solution)/shard_map/ppermute | solution.py:283
  80.6 15.7 %collective-permute-start.16 = (bf16[512,128]{1,0:T(8,128)(2,1)S(1)}, bf16[512,128]{1,0:T(8,128)(2,1)S(1)}, u32[]{:S(2)}, u32[]{:S(2)}) collective-permute-start(bf16[512,128]{1,0:T(8,128)(2,1)S(1)} %get-tuple-element.58), channel_id=1, source_target_pairs={{0,8},{4,12},{8,0},{12,4},{1,9},{5,13},{9,1},{13,5},{2,10},{6,14},... | collective-permute-start | bytes 393224 | tf_op jit(solution)/shard_map/ppermute | solution.py:283
  81.8 14.5 %collective-permute-start.17 = (bf16[512,128]{1,0:T(8,128)(2,1)S(1)}, bf16[512,128]{1,0:T(8,128)(2,1)S(1)}, u32[]{:S(2)}, u32[]{:S(2)}) collective-permute-start(bf16[512,128]{1,0:T(8,128)(2,1)S(1)} %get-tuple-element.59), channel_id=1, source_target_pairs={{0,12},{4,8},{8,4},{12,0},{1,13},{5,9},{9,5},{13,1},{2,14},{6,10},... | collective-permute-start | bytes 393224 | tf_op jit(solution)/shard_map/ppermute | solution.py:283
  (3 other events, 9.9 us)

commit v3 on v2

--- a/solution.py
+++ b/solution.py
@@ -40,7 +40,7 @@
     return lax.optimization_barrier((x, *others))[0]
 
 
-def call(kernel, out_shape, *args, scratch=(), specs=None, vmem=7 << 20):
+def call(kernel, out_shape, *args, scratch=(), specs=None, vmem=6 << 20):
     outs = out_shape if isinstance(out_shape, (tuple, list)) else (out_shape,)
     out_specs = tuple(VMEM_SPEC for _ in outs)
     result = pl.pallas_call(
@@ -324,7 +324,7 @@
 
     def hidden_half(flip, gradient, split):
         return call(
-            functools.partial(hidden_kernel, flip, half, 512),
+            functools.partial(hidden_kernel, flip, half, 256),
             (shape((tokens // split, half + LANES), f32),) * split,
             gradient,
             *gathered,

time: 97.2 us -> 84.7 us (0.87)
  local copies, waits for them, and re-layouts: 13.4 us -> 0.06 us
  starting transfers between devices: 22.3 us -> 23.6 us
  waiting for transfers between devices: 16.5 us -> 15.5 us
    unnamed x28 -> x20, local copies, waits for them, and re-layouts: 13.4 us -> 0.06 us
    ppermute x21, starting transfers between devices: 22.3 us -> 23.6 us  [swap(): return lax.ppermute(x, axis, [(i, i ^ distance) for i in range(n)])]
  transfers between devices with their start and end apart: 21 -> 21, of which waited for: 6 -> 7; matrix products, arithmetic and copies ran while one was open for 0% -> 0% of each run, Pallas kernels for 40% -> 47%
where the time goes in v3:
time: 84.7 us; the launch traced here: 84.6 us
  Pallas kernels  44.4 us (52%)
  starting transfers between devices  23.6 us (28%)
  waiting for transfers between devices  15.5 us (18%)
  between operations  0.93 us (1%)
    pallas_call x17, Pallas kernels, call(): pl.pallas_call(kernel, out_shape=tuple(outs), in_specs=specs if specs is...  44.4 us
    ppermute x21, starting transfers between devices, swap(): return lax.ppermute(x, axis, [(i, i ^ distance) for i in range(n)])  23.6 us
    ppermute x21, waiting for transfers between devices, swap(): return lax.ppermute(x, axis, [(i, i ^ distance) for i in range(n)])  15.5 us
  transfers between devices with their start and end apart: 21, of which 7 were waited for; matrix products, arithmetic and copies ran while one was open for 0% of the time, Pallas kernels for 47%

profile of v3, /device:TPU:0, one launch (start us, length us, event | category | flops | bytes accessed | tf_op | source)
XLA Modules:
  0.0 84.6 jit_solution(9717968495051160087)
XLA Ops:
  0.6 3.1 %collective-permute-start.3 = (bf16[32,4096]{1,0:T(8,128)(2,1)}, bf16[32,4096]{1,0:T(8,128)(2,1)S(1)}, u32[]{:S(2)}, u32[]{:S(2)}) collective-permute-start(bf16[32,4096]{1,0:T(8,128)(2,1)} %top.1), channel_id=1, source_target_pairs={{0,4},{4,0},{8,12},{12,8},{1,5},{5,1},{9,13},{13,9},{2,6},{6,2},{1... | collective-permute-start | bytes 786440 | tf_op jit(solution)/shard_map/ppermute | solution.py:283
  3.8 3.0 %collective-permute-start.1 = (bf16[32,4096]{1,0:T(8,128)(2,1)}, bf16[32,4096]{1,0:T(8,128)(2,1)S(1)}, u32[]{:S(2)}, u32[]{:S(2)}) collective-permute-start(bf16[32,4096]{1,0:T(8,128)(2,1)} %o0.4), channel_id=1, source_target_pairs={{0,8},{4,12},{8,0},{12,4},{1,9},{5,13},{9,1},{13,5},{2,10},{6,14},... | collective-permute-start | bytes 786440 | tf_op jit(solution)/shard_map/ppermute | solution.py:283
  6.8 1.3 %collective-permute-start.2 = (bf16[32,4096]{1,0:T(8,128)(2,1)}, bf16[32,4096]{1,0:T(8,128)(2,1)S(1)}, u32[]{:S(2)}, u32[]{:S(2)}) collective-permute-start(bf16[32,4096]{1,0:T(8,128)(2,1)} %o0.4), channel_id=1, source_target_pairs={{0,12},{4,8},{8,4},{12,0},{1,13},{5,9},{9,5},{13,1},{2,14},{6,10},... | collective-permute-start | bytes 786440 | tf_op jit(solution)/shard_map/ppermute | solution.py:283
  8.1 3.5 %shard_map.165.refs_8_ = bf16[2048,2048]{1,0:T(8,128)(2,1)S(1)} custom-call(bf16[4096,2048]{1,0:T(8,128)(2,1)} %src.7), custom_call_target="tpu_custom_call" | custom-call | tf_op jit(solution)/shard_map/pallas_call | solution.py:46
  11.6 3.5 %shard_map.166.refs_8_ = bf16[2048,2048]{1,0:T(8,128)(2,1)S(1)} custom-call(bf16[4096,2048]{1,0:T(8,128)(2,1)} %src.7), custom_call_target="tpu_custom_call" | custom-call | tf_op jit(solution)/shard_map/pallas_call | solution.py:46
  15.1 3.5 %shard_map.167.refs_9_ = bf16[2048,2048]{1,0:T(8,128)(2,1)S(1)} custom-call(bf16[4096,2048]{1,0:T(8,128)(2,1)} %src.9), custom_call_target="tpu_custom_call" | custom-call | tf_op jit(solution)/shard_map/pallas_call | solution.py:46
  18.6 3.5 %shard_map.168.refs_9_ = bf16[2048,2048]{1,0:T(8,128)(2,1)S(1)} custom-call(bf16[4096,2048]{1,0:T(8,128)(2,1)} %src.9), custom_call_target="tpu_custom_call" | custom-call | tf_op jit(solution)/shard_map/pallas_call | solution.py:46
  22.2 6.0 %shard_map.164.w = bf16[2048,4096]{1,0:T(8,128)(2,1)S(1)} custom-call(bf16[2048,4096]{1,0:T(8,128)(2,1)} %src.5), custom_call_target="tpu_custom_call" | custom-call | tf_op jit(solution)/shard_map/pallas_call | solution.py:46
  28.2 0.6 shard_map.169
  29.0 0.4 collective-permute-done.2.o3
  29.4 4.2 %shard_map.171 = (f32[32,1152]{1,0:T(8,128)S(1)}, f32[32,1152]{1,0:T(8,128)S(1)}, f32[32,1152]{1,0:T(8,128)S(1)}, f32[32,1152]{1,0:T(8,128)S(1)}) custom-call(bf16[32,4096]{1,0:T(8,128)(2,1)S(1)} %copy-done, bf16[32,4096]{1,0:T(8,128)(2,1)S(1)} %collective-permute-done.o1, bf16[32,4096]{1,0:T(8,128)(2,1)S(1)} %collective-permute-done.1.o2, ...), custom_call_target="tpu_custom_call" | custom-call | tf_op jit(solution)/shard_map/pallas_call | solution.py:46
  33.7 0.5 collective-permute-start.5
  34.3 0.4 collective-permute-start.7
  34.7 3.0 %collective-permute-start.14 = (bf16[64,4096]{1,0:T(8,128)(2,1)S(1)}, bf16[64,4096]{1,0:T(8,128)(2,1)S(1)}, u32[]{:S(2)}, u32[]{:S(2)}) collective-permute-start(bf16[64,4096]{1,0:T(8,128)(2,1)S(1)} %shard_map.170.rest_0_), channel_id=1, source_target_pairs={{0,8},{4,12},{8,0},{12,4},{1,9},{5,13},{9,1},{13,5},{2,10},{6,14},... | collective-permute-start | bytes 1572872 | tf_op jit(solution)/shard_map/ppermute | solution.py:283
  37.7 4.2 %shard_map.172.keep = f32[128,1152]{1,0:T(8,128)S(1)} custom-call(bf16[32,4096]{1,0:T(8,128)(2,1)S(1)} %copy-done, bf16[32,4096]{1,0:T(8,128)(2,1)S(1)} %collective-permute-done.o1, bf16[32,4096]{1,0:T(8,128)(2,1)S(1)} %collective-permute-done.1.o2, bf16[32,4096]{1,0:T(8,128)(2,1)S(1)} %collective-permute-done.2.o3, bf16[2048,4096]{1,0:T(8,128)(2,1)S(1)} %shard_map.164.w, ...), custom_call_target="tpu_custom_call" | custom-call | tf_op jit(solution)/shard_map/pallas_call | solution.py:46
  42.0 1.5 %collective-permute-start.8 = (bf16[560,128]{1,0:T(8,128)(2,1)S(1)}, bf16[560,128]{1,0:T(8,128)(2,1)S(1)}, u32[]{:S(2)}, u32[]{:S(2)}) collective-permute-start(bf16[560,128]{1,0:T(8,128)(2,1)S(1)} %get-tuple-element.44.mine0), channel_id=1, source_target_pairs={{0,2},{1,3},{2,0},{3,1},{4,6},{5,7},{6,4},{7,5},{8,10},{9,11},{10,... | collective-permute-start | bytes 430088 | tf_op jit(solution)/shard_map/ppermute | solution.py:283
  43.6 0.5 collective-permute-start.9
  44.1 6.2 %collective-permute-done.9.other1 = bf16[512,128]{1,0:T(8,128)(2,1)S(1)} collective-permute-done((bf16[512,128]{1,0:T(8,128)(2,1)S(1)}, bf16[512,128]{1,0:T(8,128)(2,1)S(1)}, u32[]{:S(2)}, u32[]{:S(2)}) %collective-permute-start.9) | collective-permute-done | bytes 131104 | tf_op jit(solution)/shard_map/ppermute | solution.py:283
  50.6 0.5 collective-permute-start.13
  51.2 0.4 collective-permute-start.11
  51.6 0.3 collective-permute-done.12.refs_6_.mate0
  52.1 0.3 collective-permute-done.10.refs_4_
  52.6 5.8 %shard_map.175 = (f32[32,2048]{1,0:T(8,128)S(1)}, bf16[560,128]{1,0:T(8,128)(2,1)S(1)}, bf16[560,128]{1,0:T(8,128)(2,1)S(1)}, bf16[560,128]{1,0:T(8,128)(2,1)S(1)}, f32[16,128]{1,0:T(8,128)S(1)}) custom-call(bf16[64,1024]{1,0:T(8,128)(2,1)S(1)} %get-tuple-element.46.refs_0_, bf16[64,1024]{1,0:T(8,128)(2,1)S(1)} %get-tuple-element.47.refs_1_, ...), custom_call_target="tpu_custom_call" | custom-call | tf_op jit(solution)/shard_map/pallas_call | solution.py:46
  58.5 1.1 %collective-permute-start.19 = (bf16[560,128]{1,0:T(8,128)(2,1)S(1)}, bf16[560,128]{1,0:T(8,128)(2,1)S(1)}, u32[]{:S(2)}, u32[]{:S(2)}) collective-permute-start(bf16[560,128]{1,0:T(8,128)(2,1)S(1)} %get-tuple-element.52), channel_id=1, source_target_pairs={{0,8},{4,12},{8,0},{12,4},{1,9},{5,13},{9,1},{13,5},{2,10},{6,14},... | collective-permute-start | bytes 430088 | tf_op jit(solution)/shard_map/ppermute | solution.py:283
  59.6 3.3 %collective-permute-start.20 = (bf16[560,128]{1,0:T(8,128)(2,1)S(1)}, bf16[560,128]{1,0:T(8,128)(2,1)S(1)}, u32[]{:S(2)}, u32[]{:S(2)}) collective-permute-start(bf16[560,128]{1,0:T(8,128)(2,1)S(1)} %get-tuple-element.53), channel_id=1, source_target_pairs={{0,12},{4,8},{8,4},{12,0},{1,13},{5,9},{9,5},{13,1},{2,14},{6,10},... | collective-permute-start | bytes 430088 | tf_op jit(solution)/shard_map/ppermute | solution.py:283
  62.9 6.0 %shard_map.176 = (f32[32,2048]{1,0:T(8,128)S(1)}, bf16[512,128]{1,0:T(8,128)(2,1)S(1)}, bf16[512,128]{1,0:T(8,128)(2,1)S(1)}, bf16[512,128]{1,0:T(8,128)(2,1)S(1)}) custom-call(bf16[64,1024]{1,0:T(8,128)(2,1)S(1)} %get-tuple-element.46.refs_0_, bf16[64,1024]{1,0:T(8,128)(2,1)S(1)} %get-tuple-element.47.refs_1_, ...), custom_call_target="tpu_custom_call" | custom-call | tf_op jit(solution)/shard_map/pallas_call | solution.py:46
  69.0 1.1 %collective-permute-start.16 = (bf16[512,128]{1,0:T(8,128)(2,1)S(1)}, bf16[512,128]{1,0:T(8,128)(2,1)S(1)}, u32[]{:S(2)}, u32[]{:S(2)}) collective-permute-start(bf16[512,128]{1,0:T(8,128)(2,1)S(1)} %get-tuple-element.58), channel_id=1, source_target_pairs={{0,8},{4,12},{8,0},{12,4},{1,9},{5,13},{9,1},{13,5},{2,10},{6,14},... | collective-permute-start | bytes 393224 | tf_op jit(solution)/shard_map/ppermute | solution.py:283
  70.1 3.2 %collective-permute-start.17 = (bf16[512,128]{1,0:T(8,128)(2,1)S(1)}, bf16[512,128]{1,0:T(8,128)(2,1)S(1)}, u32[]{:S(2)}, u32[]{:S(2)}) collective-permute-start(bf16[512,128]{1,0:T(8,128)(2,1)S(1)} %get-tuple-element.59), channel_id=1, source_target_pairs={{0,12},{4,8},{8,4},{12,0},{1,13},{5,9},{9,5},{13,1},{2,14},{6,10},... | collective-permute-start | bytes 393224 | tf_op jit(solution)/shard_map/ppermute | solution.py:283
  73.3 1.2 %shard_map.180 = (f32[16,2048]{1,0:T(8,128)}, f32[16,2048]{1,0:T(8,128)}, f32[16,4096]{1,0:T(8,128)}) custom-call(bf16[64,1024]{1,0:T(8,128)(2,1)S(1)} %get-tuple-element.48.refs_2_.own0, bf16[64,1024]{1,0:T(8,128)(2,1)S(1)} %get-tuple-element.49.refs_3_.own1, bf16[64,1024]{1,0:T(8,128)(2,1)S(1)} %collective-permute-done.12.refs_6_.mate0, ...), custom_call_target="tpu_custom_call" | custom-call | tf_op jit(solution)/shard_map/pallas_call | solution.py:46
  74.5 1.3 %shard_map.179 = f32[16,4096]{1,0:T(8,128)} custom-call(f32[16,128]{1,0:T(8,128)S(1)} %get-tuple-element.61.low, bf16[560,128]{1,0:T(8,128)(2,1)S(1)} %collective-permute-done.18.r1, bf16[560,128]{1,0:T(8,128)(2,1)S(1)} %collective-permute-done.19.r2, bf16[560,128]{1,0:T(8,128)(2,1)S(1)} %collective-permute-done.20.r3, ...), custom_call_target="tpu_custom_call" | custom-call | tf_op jit(solution)/shard_map/pallas_call | solution.py:46
  75.9 7.8 %collective-permute-done.16.r2 = bf16[512,128]{1,0:T(8,128)(2,1)S(1)} collective-permute-done((bf16[512,128]{1,0:T(8,128)(2,1)S(1)}, bf16[512,128]{1,0:T(8,128)(2,1)S(1)}, u32[]{:S(2)}, u32[]{:S(2)}) %collective-permute-start.16) | collective-permute-done | bytes 131104 | tf_op jit(solution)/shard_map/ppermute | solution.py:283
  83.8 0.8 shard_map.178
  (47 shorter events, 1.3 us)
Async XLA Ops:
  0.6 28.2 %collective-permute-start.3 = (bf16[32,4096]{1,0:T(8,128)(2,1)}, bf16[32,4096]{1,0:T(8,128)(2,1)S(1)}, u32[]{:S(2)}, u32[]{:S(2)}) collective-permute-start(bf16[32,4096]{1,0:T(8,128)(2,1)} %top.1), channel_id=1, source_target_pairs={{0,4},{4,0},{8,12},{12,8},{1,5},{5,1},{9,13},{13,9},{2,6},{6,2},{1... | collective-permute-start | bytes 786440 | tf_op jit(solution)/shard_map/ppermute | solution.py:283
  3.7 25.2 %collective-permute-start = (bf16[32,4096]{1,0:T(8,128)(2,1)}, bf16[32,4096]{1,0:T(8,128)(2,1)S(1)}, u32[]{:S(2)}, u32[]{:S(2)}) collective-permute-start(bf16[32,4096]{1,0:T(8,128)(2,1)} %o0.4), channel_id=1, source_target_pairs={{0,4},{4,0},{8,12},{12,8},{1,5},{5,1},{9,13},{13,9},{2,6},{6,2},{1... | collective-permute-start | bytes 786440 | tf_op jit(solution)/shard_map/ppermute | solution.py:283
  3.8 25.2 %collective-permute-start.1 = (bf16[32,4096]{1,0:T(8,128)(2,1)}, bf16[32,4096]{1,0:T(8,128)(2,1)S(1)}, u32[]{:S(2)}, u32[]{:S(2)}) collective-permute-start(bf16[32,4096]{1,0:T(8,128)(2,1)} %o0.4), channel_id=1, source_target_pairs={{0,8},{4,12},{8,0},{12,4},{1,9},{5,13},{9,1},{13,5},{2,10},{6,14},... | collective-permute-start | bytes 786440 | tf_op jit(solution)/shard_map/ppermute | solution.py:283
  6.8 22.6 %collective-permute-start.2 = (bf16[32,4096]{1,0:T(8,128)(2,1)}, bf16[32,4096]{1,0:T(8,128)(2,1)S(1)}, u32[]{:S(2)}, u32[]{:S(2)}) collective-permute-start(bf16[32,4096]{1,0:T(8,128)(2,1)} %o0.4), channel_id=1, source_target_pairs={{0,12},{4,8},{8,4},{12,0},{1,13},{5,9},{9,5},{13,1},{2,14},{6,10},... | collective-permute-start | bytes 786440 | tf_op jit(solution)/shard_map/ppermute | solution.py:283
  22.2 6.1 %copy-start.3 = (bf16[128,2048]{1,0:T(8,128)(2,1)S(1)}, bf16[128,2048]{1,0:T(8,128)(2,1)}, u32[]{:S(2)}) copy-start(bf16[128,2048]{1,0:T(8,128)(2,1)} %g_ref.1) | copy-start | bytes 1572868
  22.2 6.1 %copy-start.4 = (bf16[128,2048]{1,0:T(8,128)(2,1)S(1)}, bf16[128,2048]{1,0:T(8,128)(2,1)}, u32[]{:S(2)}) copy-start(bf16[128,2048]{1,0:T(8,128)(2,1)} %u_ref.1) | copy-start | bytes 1572868
  22.2 6.7 %copy-start.7 = (bf16[32,4096]{1,0:T(8,128)(2,1)S(1)}, bf16[32,4096]{1,0:T(8,128)(2,1)}, u32[]{:S(2)}) copy-start(bf16[32,4096]{1,0:T(8,128)(2,1)} %top.1) | copy-start | bytes 786436
  22.2 7.2 %copy-start = (bf16[32,4096]{1,0:T(8,128)(2,1)S(1)}, bf16[32,4096]{1,0:T(8,128)(2,1)}, u32[]{:S(2)}) copy-start(bf16[32,4096]{1,0:T(8,128)(2,1)} %o0.4) | copy-start | bytes 786436
  22.2 7.2 %copy-start.1 = (bf16[16,4096]{1,0:T(8,128)(2,1)S(1)}, bf16[16,4096]{1,0:T(8,128)(2,1)}, u32[]{:S(2)}) copy-start(bf16[16,4096]{1,0:T(8,128)(2,1)} %exit_ref.3) | copy-start | bytes 393220
  22.2 7.2 %copy-start.5 = (bf16[16,2048]{1,0:T(8,128)(2,1)S(1)}, bf16[16,2048]{1,0:T(8,128)(2,1)}, u32[]{:S(2)}) copy-start(bf16[16,2048]{1,0:T(8,128)(2,1)} %entry.3) | copy-start | bytes 196612
  28.9 23.7 %copy-start.2 = (bf16[16,4096]{1,0:T(8,128)(2,1)S(1)}, bf16[16,4096]{1,0:T(8,128)(2,1)}, u32[]{:S(2)}) copy-start(bf16[16,4096]{1,0:T(8,128)(2,1)} %refs_11_.3) | copy-start | bytes 393220
  28.9 23.7 %copy-start.6 = (bf16[16,2048]{1,0:T(8,128)(2,1)S(1)}, bf16[16,2048]{1,0:T(8,128)(2,1)}, u32[]{:S(2)}) copy-start(bf16[16,2048]{1,0:T(8,128)(2,1)} %refs_10_.3) | copy-start | bytes 196612
  33.6 8.3 %collective-permute-start.4 = (f32[32,1152]{1,0:T(8,128)S(1)}, f32[32,1152]{1,0:T(8,128)S(1)}, u32[]{:S(2)}, u32[]{:S(2)}) collective-permute-start(f32[32,1152]{1,0:T(8,128)S(1)} %get-tuple-element.39), channel_id=1, source_target_pairs={{0,1},{1,0},{2,3},{3,2},{4,5},{5,4},{6,7},{7,6},{8,9},{9,8},{10,11... | collective-permute-start | bytes 442376 | tf_op jit(solution)/shard_map/ppermute | solution.py:283
  33.7 8.2 %collective-permute-start.5 = (f32[32,1152]{1,0:T(8,128)S(1)}, f32[32,1152]{1,0:T(8,128)S(1)}, u32[]{:S(2)}, u32[]{:S(2)}) collective-permute-start(f32[32,1152]{1,0:T(8,128)S(1)} %get-tuple-element.40), channel_id=1, source_target_pairs={{0,1},{1,0},{2,3},{3,2},{4,5},{5,4},{6,7},{7,6},{8,9},{9,8},{10,11... | collective-permute-start | bytes 442376 | tf_op jit(solution)/shard_map/ppermute | solution.py:283
  34.2 7.8 %collective-permute-start.6 = (f32[32,1152]{1,0:T(8,128)S(1)}, f32[32,1152]{1,0:T(8,128)S(1)}, u32[]{:S(2)}, u32[]{:S(2)}) collective-permute-start(f32[32,1152]{1,0:T(8,128)S(1)} %get-tuple-element.41), channel_id=1, source_target_pairs={{0,1},{1,0},{2,3},{3,2},{4,5},{5,4},{6,7},{7,6},{8,9},{9,8},{10,11... | collective-permute-start | bytes 442376 | tf_op jit(solution)/shard_map/ppermute | solution.py:283
  34.3 7.7 %collective-permute-start.7 = (f32[32,1152]{1,0:T(8,128)S(1)}, f32[32,1152]{1,0:T(8,128)S(1)}, u32[]{:S(2)}, u32[]{:S(2)}) collective-permute-start(f32[32,1152]{1,0:T(8,128)S(1)} %get-tuple-element.42), channel_id=1, source_target_pairs={{0,1},{1,0},{2,3},{3,2},{4,5},{5,4},{6,7},{7,6},{8,9},{9,8},{10,11... | collective-permute-start | bytes 442376 | tf_op jit(solution)/shard_map/ppermute | solution.py:283
  34.7 28.2 %collective-permute-start.14 = (bf16[64,4096]{1,0:T(8,128)(2,1)S(1)}, bf16[64,4096]{1,0:T(8,128)(2,1)S(1)}, u32[]{:S(2)}, u32[]{:S(2)}) collective-permute-start(bf16[64,4096]{1,0:T(8,128)(2,1)S(1)} %shard_map.170.rest_0_), channel_id=1, source_target_pairs={{0,8},{4,12},{8,0},{12,4},{1,9},{5,13},{9,1},{13,5},{2,10},{6,14},... | collective-permute-start | bytes 1572872 | tf_op jit(solution)/shard_map/ppermute | solution.py:283
  42.0 8.3 %collective-permute-start.8 = (bf16[560,128]{1,0:T(8,128)(2,1)S(1)}, bf16[560,128]{1,0:T(8,128)(2,1)S(1)}, u32[]{:S(2)}, u32[]{:S(2)}) collective-permute-start(bf16[560,128]{1,0:T(8,128)(2,1)S(1)} %get-tuple-element.44.mine0), channel_id=1, source_target_pairs={{0,2},{1,3},{2,0},{3,1},{4,6},{5,7},{6,4},{7,5},{8,10},{9,11},{10,... | collective-permute-start | bytes 430088 | tf_op jit(solution)/shard_map/ppermute | solution.py:283
  43.6 6.8 %collective-permute-start.9 = (bf16[512,128]{1,0:T(8,128)(2,1)S(1)}, bf16[512,128]{1,0:T(8,128)(2,1)S(1)}, u32[]{:S(2)}, u32[]{:S(2)}) collective-permute-start(bf16[512,128]{1,0:T(8,128)(2,1)S(1)} %get-tuple-element.45.mine1), channel_id=1, source_target_pairs={{0,2},{1,3},{2,0},{3,1},{4,6},{5,7},{6,4},{7,5},{8,10},{9,11},{10,... | collective-permute-start | bytes 393224 | tf_op jit(solution)/shard_map/ppermute | solution.py:283
  50.5 1.4 %collective-permute-start.12 = (bf16[64,1024]{1,0:T(8,128)(2,1)S(1)}, bf16[64,1024]{1,0:T(8,128)(2,1)S(1)}, u32[]{:S(2)}, u32[]{:S(2)}) collective-permute-start(bf16[64,1024]{1,0:T(8,128)(2,1)S(1)} %get-tuple-element.48.refs_2_.own0), channel_id=1, source_target_pairs={{0,1},{1,0},{2,3},{3,2},{4,5},{5,4},{6,7},{7,6},{8,9},{9,8},{10,11... | collective-permute-start | bytes 393224 | tf_op jit(solution)/shard_map/ppermute | solution.py:283
  50.6 1.5 %collective-permute-start.13 = (bf16[64,1024]{1,0:T(8,128)(2,1)S(1)}, bf16[64,1024]{1,0:T(8,128)(2,1)S(1)}, u32[]{:S(2)}, u32[]{:S(2)}) collective-permute-start(bf16[64,1024]{1,0:T(8,128)(2,1)S(1)} %get-tuple-element.49.refs_3_.own1), channel_id=1, source_target_pairs={{0,1},{1,0},{2,3},{3,2},{4,5},{5,4},{6,7},{7,6},{8,9},{9,8},{10,11... | collective-permute-start | bytes 393224 | tf_op jit(solution)/shard_map/ppermute | solution.py:283
  51.1 1.3 %collective-permute-start.10 = (bf16[64,1024]{1,0:T(8,128)(2,1)S(1)}, bf16[64,1024]{1,0:T(8,128)(2,1)S(1)}, u32[]{:S(2)}, u32[]{:S(2)}) collective-permute-start(bf16[64,1024]{1,0:T(8,128)(2,1)S(1)} %get-tuple-element.46.refs_0_), channel_id=1, source_target_pairs={{0,1},{1,0},{2,3},{3,2},{4,5},{5,4},{6,7},{7,6},{8,9},{9,8},{10,11... | collective-permute-start | bytes 393224 | tf_op jit(solution)/shard_map/ppermute | solution.py:283
  51.2 22.2 %copy-start.8 = (bf16[16,128]{1,0:T(8,128)(2,1)S(1)}, bf16[16,128]{1,0:T(8,128)(2,1)}, u32[]{:S(2)}) copy-start(bf16[16,128]{1,0:T(8,128)(2,1)} %up_act.1) | copy-start | bytes 12292
  51.2 22.2 %copy-start.9 = (bf16[16,128]{1,0:T(8,128)(2,1)S(1)}, bf16[16,128]{1,0:T(8,128)(2,1)}, u32[]{:S(2)}) copy-start(bf16[16,128]{1,0:T(8,128)(2,1)} %down_act.1) | copy-start | bytes 12292
  51.2 1.5 %collective-permute-start.11 = (bf16[64,1024]{1,0:T(8,128)(2,1)S(1)}, bf16[64,1024]{1,0:T(8,128)(2,1)S(1)}, u32[]{:S(2)}, u32[]{:S(2)}) collective-permute-start(bf16[64,1024]{1,0:T(8,128)(2,1)S(1)} %get-tuple-element.47.refs_1_), channel_id=1, source_target_pairs={{0,1},{1,0},{2,3},{3,2},{4,5},{5,4},{6,7},{7,6},{8,9},{9,8},{10,11... | collective-permute-start | bytes 393224 | tf_op jit(solution)/shard_map/ppermute | solution.py:283
  58.4 11.6 %collective-permute-start.18 = (bf16[560,128]{1,0:T(8,128)(2,1)S(1)}, bf16[560,128]{1,0:T(8,128)(2,1)S(1)}, u32[]{:S(2)}, u32[]{:S(2)}) collective-permute-start(bf16[560,128]{1,0:T(8,128)(2,1)S(1)} %get-tuple-element.51), channel_id=1, source_target_pairs={{0,4},{4,0},{8,12},{12,8},{1,5},{5,1},{9,13},{13,9},{2,6},{6,2},{1... | collective-permute-start | bytes 430088 | tf_op jit(solution)/shard_map/ppermute | solution.py:283
  58.5 16.0 %collective-permute-start.19 = (bf16[560,128]{1,0:T(8,128)(2,1)S(1)}, bf16[560,128]{1,0:T(8,128)(2,1)S(1)}, u32[]{:S(2)}, u32[]{:S(2)}) collective-permute-start(bf16[560,128]{1,0:T(8,128)(2,1)S(1)} %get-tuple-element.52), channel_id=1, source_target_pairs={{0,8},{4,12},{8,0},{12,4},{1,9},{5,13},{9,1},{13,5},{2,10},{6,14},... | collective-permute-start | bytes 430088 | tf_op jit(solution)/shard_map/ppermute | solution.py:283
  59.6 14.9 %collective-permute-start.20 = (bf16[560,128]{1,0:T(8,128)(2,1)S(1)}, bf16[560,128]{1,0:T(8,128)(2,1)S(1)}, u32[]{:S(2)}, u32[]{:S(2)}) collective-permute-start(bf16[560,128]{1,0:T(8,128)(2,1)S(1)} %get-tuple-element.53), channel_id=1, source_target_pairs={{0,12},{4,8},{8,4},{12,0},{1,13},{5,9},{9,5},{13,1},{2,14},{6,10},... | collective-permute-start | bytes 430088 | tf_op jit(solution)/shard_map/ppermute | solution.py:283
  68.9 7.0 %collective-permute-start.15 = (bf16[512,128]{1,0:T(8,128)(2,1)S(1)}, bf16[512,128]{1,0:T(8,128)(2,1)S(1)}, u32[]{:S(2)}, u32[]{:S(2)}) collective-permute-start(bf16[512,128]{1,0:T(8,128)(2,1)S(1)} %get-tuple-element.57), channel_id=1, source_target_pairs={{0,4},{4,0},{8,12},{12,8},{1,5},{5,1},{9,13},{13,9},{2,6},{6,2},{1... | collective-permute-start | bytes 393224 | tf_op jit(solution)/shard_map/ppermute | solution.py:283
  69.0 14.8 %collective-permute-start.16 = (bf16[512,128]{1,0:T(8,128)(2,1)S(1)}, bf16[512,128]{1,0:T(8,128)(2,1)S(1)}, u32[]{:S(2)}, u32[]{:S(2)}) collective-permute-start(bf16[512,128]{1,0:T(8,128)(2,1)S(1)} %get-tuple-element.58), channel_id=1, source_target_pairs={{0,8},{4,12},{8,0},{12,4},{1,9},{5,13},{9,1},{13,5},{2,10},{6,14},... | collective-permute-start | bytes 393224 | tf_op jit(solution)/shard_map/ppermute | solution.py:283
  70.1 13.7 %collective-permute-start.17 = (bf16[512,128]{1,0:T(8,128)(2,1)S(1)}, bf16[512,128]{1,0:T(8,128)(2,1)S(1)}, u32[]{:S(2)}, u32[]{:S(2)}) collective-permute-start(bf16[512,128]{1,0:T(8,128)(2,1)S(1)} %get-tuple-element.59), channel_id=1, source_target_pairs={{0,12},{4,8},{8,4},{12,0},{1,13},{5,9},{9,5},{13,1},{2,14},{6,10},... | collective-permute-start | bytes 393224 | tf_op jit(solution)/shard_map/ppermute | solution.py:283

commit v4 on v3

--- a/solution.py
+++ b/solution.py
@@ -40,7 +40,7 @@
     return lax.optimization_barrier((x, *others))[0]
 
 
-def call(kernel, out_shape, *args, scratch=(), specs=None, vmem=6 << 20):
+def call(kernel, out_shape, *args, scratch=(), specs=None, vmem=5 << 20):
     outs = out_shape if isinstance(out_shape, (tuple, list)) else (out_shape,)
     out_specs = tuple(VMEM_SPEC for _ in outs)
     result = pl.pallas_call(
@@ -124,36 +124,54 @@
         full[pl.ds(pl.multiple_of((position ^ k) * n, n), n), :] = piece[...]
 
 
-def hidden_kernel(flip, half, block, o0, o1, o2, o3, w, exit_ref, entry, *rest):
-    outs, full = rest[:-1], rest[-1]
+def hidden_block(full, low, w, entry, first, size):
+    rows = pl.ds(pl.multiple_of(first, LANES), size)
+    return contract_trailing(full[...], w[rows, :]) + adapter_scale * contract_leading(
+        low, entry[:, rows].astype(f32), HIGHEST
+    )
+
+
+def send_kernel(half, block, o0, o1, o2, o3, w, exit_ref, entry, *outs):
+    outs, low_ref, full = outs[:-2], outs[-2], outs[-1]
     n = outs[0].shape[0]
     place_rows(full, (o0, o1, o2, o3), lax.axis_index("row"))
-    which = lax.rem(lax.axis_index("col"), 2) ^ flip
+    start = (1 - lax.rem(lax.axis_index("col"), 2)) * half
     low = contract_trailing(exit_ref[...], full[...])
+    low_ref[...] = low
     outs[0][: low.shape[0], half:] = low
     for i in range(half // block):
-        rows = pl.ds(pl.multiple_of(which * half + i * block, block), block)
-        piece = contract_trailing(full[...], w[rows, :]) + adapter_scale * contract_leading(
-            low, entry[:, rows].astype(f32), HIGHEST
-        )
+        piece = hidden_block(full, low, w, entry, start + i * block, block)
         for j, out in enumerate(outs):
             out[:, i * block : (i + 1) * block] = piece[j * n : (j + 1) * n, :]
 
 
-def payload_kernel(rank, half, keep, *rest):
-    got, outs = rest[:-2], rest[-2:]
-    rows = keep.shape[0]
-    n = got[0].shape[0]
-    blocks = half // LANES // 2
-    for j, ref in enumerate(got):
-        total = keep[j * n : (j + 1) * n, :] + ref[...]
-        for i in range(2 * blocks):
-            first = i % blocks * rows + j * n
-            outs[i // blocks][first : first + n, :] = total[
-                :, i * LANES : (i + 1) * LANES
-            ].astype(bf16)
-        if j == 0:
-            store_terms(outs[0], blocks * rows, total[:rank, half:])
+def keep_kernel(half, block, full, low, w, entry, out):
+    start = lax.rem(lax.axis_index("col"), 2) * half
+    for i in range(0, out.shape[1], block):
+        size = min(block, out.shape[1] - i)
+        out[:, i : i + size] = hidden_block(full, low[...], w, entry, start + i, size)
+
+
+def store_blocks(out, piece, got, first):
+    rows = piece.shape[0]
+    for i in range(0, piece.shape[1], LANES):
+        here = i // LANES * rows
+        other = jnp.concatenate([ref[:, first + i : first + i + LANES] for ref in got], axis=0)
+        out[here : here + rows, :] = (piece[:, i : i + LANES] + other).astype(bf16)
+
+
+def payload_kernel(half, keep, low, *rest):
+    got, out = rest[:-1], rest[-1]
+    rank = low.shape[0]
+    store_blocks(out, keep[...], got, 0)
+    store_terms(out, out.shape[0] - 3 * rank, low[...] + got[0][:rank, half:])
+
+
+def rest_kernel(half, first, full, low, w, entry, *rest):
+    got, out = rest[:-1], rest[-1]
+    start = lax.rem(lax.axis_index("col"), 2) * half + first
+    piece = hidden_block(full, low[...], w, entry, start, half - first)
+    store_blocks(out, piece, got, first)
 
 
 def gradient_kernel(mine0, mine1, other0, other1, a, b, *outs):
@@ -161,18 +179,22 @@
     rows = a.shape[0]
     n, half = up_outs[0].shape
     rank = low_ref.shape[0]
-    blocks = half // LANES // 2
+    blocks = half // LANES
+    later = mine1.shape[0] // rows
     start = pl.multiple_of(lax.rem(lax.axis_index("col"), 2) * half, half)
-    for i in range(2 * blocks):
-        here = slice(i % blocks * rows, (i % blocks + 1) * rows)
-        mine, other = (mine0, other0) if i < blocks else (mine1, other1)
+    for i in range(blocks):
+        early = i < blocks - later
+        k = i if early else i - (blocks - later)
+        here = slice(k * rows, (k + 1) * rows)
+        mine, other = (mine0, other0) if early else (mine1, other1)
         grad = mine[here, :].astype(f32) + other[here, :].astype(f32)
         lanes = pl.ds(pl.multiple_of(start + i * LANES, LANES), LANES)
         for refs, factor in ((gate_outs, a), (up_outs, b)):
             value = (grad * factor[:, lanes]).astype(bf16)
             for j, ref in enumerate(refs):
                 ref[:, i * LANES : (i + 1) * LANES] = value[j * n : (j + 1) * n, :]
-    low_ref[...] = load_terms(mine0, blocks * rows, rank) + load_terms(other0, blocks * rows, rank)
+    terms = (blocks - later) * rows
+    low_ref[...] = load_terms(mine0, terms, rank) + load_terms(other0, terms, rank)
 
 
 def place_halves(full, own, mate):
@@ -266,12 +288,9 @@
     )
 
 
-def small_kernel(
-    own0, own1, mate0, mate1, low, hidden, up_act, down_act, o0, o1, o2, o3, *rest
-):
-    up_exit, down_entry, down_exit, full, ug = rest
+def small_kernel(own0, own1, mate0, mate1, low, hidden, up_act, down_act, full, *rest):
+    up_exit, down_entry, down_exit, ug = rest
     place_halves(ug, (own0, own1), (mate0, mate1))
-    place_rows(full, (o0, o1, o2, o3), lax.axis_index("row"))
     up_exit[...] = adapter_scale * jnp.dot(up_act[...], ug[...], preferred_element_type=f32)
     down_entry[...] = adapter_scale * jnp.dot(
         low[...].astype(bf16), hidden[...], preferred_element_type=f32
@@ -285,6 +304,7 @@
 
 EIGHTHS = (4,4)
 CHUNKS = len(EIGHTHS)
+KEEP_EIGHTHS = 5
 
 
 def exchange_body(
@@ -322,32 +342,44 @@
     near = [call(stack_kernel, shape((2 * share, width), bf16), inputs, swap(inputs, "row", 1, 4))]
     down_v = after(down_v, gate_v, up_v, a, b, near)
 
-    def hidden_half(flip, gradient, split):
-        return call(
-            functools.partial(hidden_kernel, flip, half, 256),
-            (shape((tokens // split, half + LANES), f32),) * split,
-            gradient,
-            *gathered,
-            in_vmem(down_v),
-            down_adapter_exit,
-            down_adapter_entry,
-            scratch=[pltpu.VMEM((tokens, width), bf16)],
-        )
-
-    send = hidden_half(1, own_gradient, 4)
+    quarter = shape((tokens // 4, half + LANES), f32)
+    *send, low_piece, full_gradient = call(
+        functools.partial(send_kernel, half, 256),
+        (quarter,) * 4 + (shape((rank, tokens), f32), shape((tokens, width), bf16)),
+        own_gradient,
+        *gathered,
+        in_vmem(down_v),
+        down_adapter_exit,
+        down_adapter_entry,
+    )
     got = [swap(x, "col", 1, 4) for x in send]
-    keep = hidden_half(0, after(own_gradient, send), 1)[0]
-    blocks = half // LANES
     far = [swap(near[0], "row", 2, 4)]
-    payload = call(
-        functools.partial(payload_kernel, rank, half),
-        (
-            shape((blocks // 2 * tokens + 3 * rank, LANES), bf16),
-            shape((blocks // 2 * tokens, LANES), bf16),
-        ),
+    first = half // 8 * KEEP_EIGHTHS
+    keep = call(
+        functools.partial(keep_kernel, half, 256),
+        shape((tokens, first), f32),
+        full_gradient,
+        low_piece,
+        in_vmem(down_v),
+        down_adapter_entry,
+    )
+    early = call(
+        functools.partial(payload_kernel, half),
+        shape((first // LANES * tokens + 3 * rank, LANES), bf16),
         keep,
+        low_piece,
         *got,
     )
+    late = call(
+        functools.partial(rest_kernel, half, first),
+        shape(((half - first) // LANES * tokens, LANES), bf16),
+        after(full_gradient, early),
+        low_piece,
+        in_vmem(down_v),
+        down_adapter_entry,
+        *got,
+    )
+    payload = (early, late)
     other = [swap(x, "col", 2, 4) for x in payload]
     *grads, low_full = call(
         gradient_kernel,
@@ -408,9 +440,8 @@
         hidden_state,
         up_adapter_activations,
         down_adapter_activations,
-        own_gradient,
-        *gathered,
-        scratch=[pltpu.VMEM((tokens, width), bf16), pltpu.VMEM((tokens, hidden), bf16)],
+        full_gradient,
+        scratch=[pltpu.VMEM((tokens, hidden), bf16)],
     )
     return (
         input_grad[0],

time: 84.7 us -> 83.1 us (0.981)
  Pallas kernels: 44.4 us -> 43.4 us
    pallas_call x17 -> x18, Pallas kernels: 44.4 us -> 43.4 us  [call(): pl.pallas_call(kernel, out_shape=tuple(outs), in_specs=specs if specs is...]
  transfers between devices with their start and end apart: 21 -> 21, of which waited for: 7 -> 8; matrix products, arithmetic and copies ran while one was open for 0% -> 0% of each run, Pallas kernels for 47% -> 46%
where the time goes in v4:
time: 83.1 us; the launch traced here: 82.9 us
  Pallas kernels  43.4 us (52%)
  starting transfers between devices  23.7 us (29%)
  waiting for transfers between devices  14.9 us (18%)
  between operations  0.92 us (1%)
    pallas_call x18, Pallas kernels, call(): pl.pallas_call(kernel, out_shape=tuple(outs), in_specs=specs if specs is...  43.4 us
    ppermute x21, starting transfers between devices, swap(): return lax.ppermute(x, axis, [(i, i ^ distance) for i in range(n)])  23.7 us
    ppermute x21, waiting for transfers between devices, swap(): return lax.ppermute(x, axis, [(i, i ^ distance) for i in range(n)])  14.9 us
  transfers between devices with their start and end apart: 21, of which 8 were waited for; matrix products, arithmetic and copies ran while one was open for 0% of the time, Pallas kernels for 46%

profile of v4, /device:TPU:0, one launch (start us, length us, event | category | flops | bytes accessed | tf_op | source)
XLA Modules:
  0.0 82.9 jit_solution(9083064746616639990)
XLA Ops:
  0.6 3.1 %collective-permute-start.3 = (bf16[32,4096]{1,0:T(8,128)(2,1)}, bf16[32,4096]{1,0:T(8,128)(2,1)S(1)}, u32[]{:S(2)}, u32[]{:S(2)}) collective-permute-start(bf16[32,4096]{1,0:T(8,128)(2,1)} %top.1), channel_id=1, source_target_pairs={{0,4},{4,0},{8,12},{12,8},{1,5},{5,1},{9,13},{13,9},{2,6},{6,2},{1... | collective-permute-start | bytes 786440 | tf_op jit(solution)/shard_map/ppermute | solution.py:302
  3.8 3.0 %collective-permute-start.1 = (bf16[32,4096]{1,0:T(8,128)(2,1)}, bf16[32,4096]{1,0:T(8,128)(2,1)S(1)}, u32[]{:S(2)}, u32[]{:S(2)}) collective-permute-start(bf16[32,4096]{1,0:T(8,128)(2,1)} %o0.1), channel_id=1, source_target_pairs={{0,8},{4,12},{8,0},{12,4},{1,9},{5,13},{9,1},{13,5},{2,10},{6,14},... | collective-permute-start | bytes 786440 | tf_op jit(solution)/shard_map/ppermute | solution.py:302
  6.8 1.3 %collective-permute-start.2 = (bf16[32,4096]{1,0:T(8,128)(2,1)}, bf16[32,4096]{1,0:T(8,128)(2,1)S(1)}, u32[]{:S(2)}, u32[]{:S(2)}) collective-permute-start(bf16[32,4096]{1,0:T(8,128)(2,1)} %o0.1), channel_id=1, source_target_pairs={{0,12},{4,8},{8,4},{12,0},{1,13},{5,9},{9,5},{13,1},{2,14},{6,10},... | collective-permute-start | bytes 786440 | tf_op jit(solution)/shard_map/ppermute | solution.py:302
  8.1 3.5 %shard_map.165.refs_8_ = bf16[2048,2048]{1,0:T(8,128)(2,1)S(1)} custom-call(bf16[4096,2048]{1,0:T(8,128)(2,1)} %src.7), custom_call_target="tpu_custom_call" | custom-call | tf_op jit(solution)/shard_map/pallas_call | solution.py:46
  11.6 3.5 %shard_map.166.refs_8_ = bf16[2048,2048]{1,0:T(8,128)(2,1)S(1)} custom-call(bf16[4096,2048]{1,0:T(8,128)(2,1)} %src.7), custom_call_target="tpu_custom_call" | custom-call | tf_op jit(solution)/shard_map/pallas_call | solution.py:46
  15.1 3.5 %shard_map.167.refs_9_ = bf16[2048,2048]{1,0:T(8,128)(2,1)S(1)} custom-call(bf16[4096,2048]{1,0:T(8,128)(2,1)} %src.9), custom_call_target="tpu_custom_call" | custom-call | tf_op jit(solution)/shard_map/pallas_call | solution.py:46
  18.6 3.5 %shard_map.168.refs_9_ = bf16[2048,2048]{1,0:T(8,128)(2,1)S(1)} custom-call(bf16[4096,2048]{1,0:T(8,128)(2,1)} %src.9), custom_call_target="tpu_custom_call" | custom-call | tf_op jit(solution)/shard_map/pallas_call | solution.py:46
  22.2 6.0 %shard_map.164.w = bf16[2048,4096]{1,0:T(8,128)(2,1)S(1)} custom-call(bf16[2048,4096]{1,0:T(8,128)(2,1)} %src.5), custom_call_target="tpu_custom_call" | custom-call | tf_op jit(solution)/shard_map/pallas_call | solution.py:46
  28.2 0.6 shard_map.169
  29.0 0.4 collective-permute-done.2.o3
  29.4 4.2 %shard_map.171 = (f32[32,1152]{1,0:T(8,128)S(1)}, f32[32,1152]{1,0:T(8,128)S(1)}, f32[32,1152]{1,0:T(8,128)S(1)}, f32[32,1152]{1,0:T(8,128)S(1)}, f32[16,128]{1,0:T(8,128)S(1)}, /*index=5*/bf16[128,4096]{1,0:T(8,128)(2,1)S(1)}) custom-call(bf16[32,4096]{1,0:T(8,128)(2,1)S(1)} %copy-done.4, bf16[32,4096]{1,0:T(8,128)(2,1)S(1)} %collective-permute-done.o1, ...), custom_call_target="tpu_custom_call" | custom-call | tf_op jit(solution)/shard_map/pallas_call | solution.py:46
  33.7 0.5 collective-permute-start.5
  34.3 0.4 collective-permute-start.7
  34.7 3.0 %collective-permute-start.14 = (bf16[64,4096]{1,0:T(8,128)(2,1)S(1)}, bf16[64,4096]{1,0:T(8,128)(2,1)S(1)}, u32[]{:S(2)}, u32[]{:S(2)}) collective-permute-start(bf16[64,4096]{1,0:T(8,128)(2,1)S(1)} %shard_map.170.rest_0_), channel_id=1, source_target_pairs={{0,8},{4,12},{8,0},{12,4},{1,9},{5,13},{9,1},{13,5},{2,10},{6,14},... | collective-permute-start | bytes 1572872 | tf_op jit(solution)/shard_map/ppermute | solution.py:302
  37.7 1.9 %shard_map.172.keep = f32[128,640]{1,0:T(8,128)S(1)} custom-call(bf16[128,4096]{1,0:T(8,128)(2,1)S(1)} %get-tuple-element.45.full, f32[16,128]{1,0:T(8,128)S(1)} %get-tuple-element.40.low, bf16[2048,4096]{1,0:T(8,128)(2,1)S(1)} %shard_map.164.w, bf16[16,2048]{1,0:T(8,128)(2,1)S(1)} %copy-done), custom_call_target="tpu_custom_call" | custom-call | tf_op jit(solution)/shard_map/pallas_call | solution.py:46
  39.7 1.6 %collective-permute-start.8 = (bf16[688,128]{1,0:T(8,128)(2,1)S(1)}, bf16[688,128]{1,0:T(8,128)(2,1)S(1)}, u32[]{:S(2)}, u32[]{:S(2)}) collective-permute-start(bf16[688,128]{1,0:T(8,128)(2,1)S(1)} %shard_map.173.mine0), channel_id=1, source_target_pairs={{0,2},{1,3},{2,0},{3,1},{4,6},{5,7},{6,4},{7,5},{8,10},{9,11},{10,... | collective-permute-start | bytes 528392 | tf_op jit(solution)/shard_map/ppermute | solution.py:302
  41.2 1.3 %shard_map.174.mine1 = bf16[384,128]{1,0:T(8,128)(2,1)S(1)} custom-call(bf16[128,4096]{1,0:T(8,128)(2,1)S(1)} %get-tuple-element.45.full, f32[16,128]{1,0:T(8,128)S(1)} %get-tuple-element.40.low, bf16[2048,4096]{1,0:T(8,128)(2,1)S(1)} %shard_map.164.w, bf16[16,2048]{1,0:T(8,128)(2,1)S(1)} %copy-done, f32[32,1152]{1,0:T(8,128)S(1)} %collective-permute-done.4.rest_0_, ...), custom_call_target="tpu_custom_call" | custom-call | tf_op jit(solution)/shard_map/pallas_call | solution.py:46
  42.5 0.6 collective-permute-start.9
  43.1 4.9 %collective-permute-done.9.other1 = bf16[384,128]{1,0:T(8,128)(2,1)S(1)} collective-permute-done((bf16[384,128]{1,0:T(8,128)(2,1)S(1)}, bf16[384,128]{1,0:T(8,128)(2,1)S(1)}, u32[]{:S(2)}, u32[]{:S(2)}) %collective-permute-start.9) | collective-permute-done | bytes 98336 | tf_op jit(solution)/shard_map/ppermute | solution.py:302
  48.3 0.5 collective-permute-start.13
  48.9 0.4 collective-permute-start.11
  50.3 5.8 %shard_map.176 = (f32[32,2048]{1,0:T(8,128)S(1)}, bf16[560,128]{1,0:T(8,128)(2,1)S(1)}, bf16[560,128]{1,0:T(8,128)(2,1)S(1)}, bf16[560,128]{1,0:T(8,128)(2,1)S(1)}, f32[16,128]{1,0:T(8,128)S(1)}) custom-call(bf16[64,1024]{1,0:T(8,128)(2,1)S(1)} %get-tuple-element.46.refs_0_, bf16[64,1024]{1,0:T(8,128)(2,1)S(1)} %get-tuple-element.47.refs_1_, ...), custom_call_target="tpu_custom_call" | custom-call | tf_op jit(solution)/shard_map/pallas_call | solution.py:46
  56.2 1.1 %collective-permute-start.19 = (bf16[560,128]{1,0:T(8,128)(2,1)S(1)}, bf16[560,128]{1,0:T(8,128)(2,1)S(1)}, u32[]{:S(2)}, u32[]{:S(2)}) collective-permute-start(bf16[560,128]{1,0:T(8,128)(2,1)S(1)} %get-tuple-element.52), channel_id=1, source_target_pairs={{0,8},{4,12},{8,0},{12,4},{1,9},{5,13},{9,1},{13,5},{2,10},{6,14},... | collective-permute-start | bytes 430088 | tf_op jit(solution)/shard_map/ppermute | solution.py:302
  57.3 3.2 %collective-permute-start.20 = (bf16[560,128]{1,0:T(8,128)(2,1)S(1)}, bf16[560,128]{1,0:T(8,128)(2,1)S(1)}, u32[]{:S(2)}, u32[]{:S(2)}) collective-permute-start(bf16[560,128]{1,0:T(8,128)(2,1)S(1)} %get-tuple-element.53), channel_id=1, source_target_pairs={{0,12},{4,8},{8,4},{12,0},{1,13},{5,9},{9,5},{13,1},{2,14},{6,10},... | collective-permute-start | bytes 430088 | tf_op jit(solution)/shard_map/ppermute | solution.py:302
  60.6 1.0 %collective-permute-done.14.rest_1_ = bf16[64,4096]{1,0:T(8,128)(2,1)S(1)} collective-permute-done((bf16[64,4096]{1,0:T(8,128)(2,1)S(1)}, bf16[64,4096]{1,0:T(8,128)(2,1)S(1)}, u32[]{:S(2)}, u32[]{:S(2)}) %collective-permute-start.14) | collective-permute-done | bytes 524320 | tf_op jit(solution)/shard_map/ppermute | solution.py:302
  61.5 6.0 %shard_map.177 = (f32[32,2048]{1,0:T(8,128)S(1)}, bf16[512,128]{1,0:T(8,128)(2,1)S(1)}, bf16[512,128]{1,0:T(8,128)(2,1)S(1)}, bf16[512,128]{1,0:T(8,128)(2,1)S(1)}) custom-call(bf16[64,1024]{1,0:T(8,128)(2,1)S(1)} %get-tuple-element.46.refs_0_, bf16[64,1024]{1,0:T(8,128)(2,1)S(1)} %get-tuple-element.47.refs_1_, ...), custom_call_target="tpu_custom_call" | custom-call | tf_op jit(solution)/shard_map/pallas_call | solution.py:46
  67.6 2.8 %collective-permute-start.16 = (bf16[512,128]{1,0:T(8,128)(2,1)S(1)}, bf16[512,128]{1,0:T(8,128)(2,1)S(1)}, u32[]{:S(2)}, u32[]{:S(2)}) collective-permute-start(bf16[512,128]{1,0:T(8,128)(2,1)S(1)} %get-tuple-element.58), channel_id=1, source_target_pairs={{0,8},{4,12},{8,0},{12,4},{1,9},{5,13},{9,1},{13,5},{2,10},{6,14},... | collective-permute-start | bytes 393224 | tf_op jit(solution)/shard_map/ppermute | solution.py:302
  70.5 1.5 %collective-permute-start.17 = (bf16[512,128]{1,0:T(8,128)(2,1)S(1)}, bf16[512,128]{1,0:T(8,128)(2,1)S(1)}, u32[]{:S(2)}, u32[]{:S(2)}) collective-permute-start(bf16[512,128]{1,0:T(8,128)(2,1)S(1)} %get-tuple-element.59), channel_id=1, source_target_pairs={{0,12},{4,8},{8,4},{12,0},{1,13},{5,9},{9,5},{13,1},{2,14},{6,10},... | collective-permute-start | bytes 393224 | tf_op jit(solution)/shard_map/ppermute | solution.py:302
  72.0 1.2 %shard_map.181 = (f32[16,2048]{1,0:T(8,128)}, f32[16,2048]{1,0:T(8,128)}, f32[16,4096]{1,0:T(8,128)}) custom-call(bf16[64,1024]{1,0:T(8,128)(2,1)S(1)} %get-tuple-element.48.refs_2_.own0, bf16[64,1024]{1,0:T(8,128)(2,1)S(1)} %get-tuple-element.49.refs_3_.own1, bf16[64,1024]{1,0:T(8,128)(2,1)S(1)} %collective-permute-done.12.refs_6_.mate0, ...), custom_call_target="tpu_custom_call" | custom-call | tf_op jit(solution)/shard_map/pallas_call | solution.py:46
  73.2 1.3 %shard_map.180 = f32[16,4096]{1,0:T(8,128)} custom-call(f32[16,128]{1,0:T(8,128)S(1)} %get-tuple-element.61.low, bf16[560,128]{1,0:T(8,128)(2,1)S(1)} %collective-permute-done.18.r1, bf16[560,128]{1,0:T(8,128)(2,1)S(1)} %collective-permute-done.19.r2, bf16[560,128]{1,0:T(8,128)(2,1)S(1)} %collective-permute-done.20.r3, ...), custom_call_target="tpu_custom_call" | custom-call | tf_op jit(solution)/shard_map/pallas_call | solution.py:46
  74.6 7.6 %collective-permute-done.16.r2 = bf16[512,128]{1,0:T(8,128)(2,1)S(1)} collective-permute-done((bf16[512,128]{1,0:T(8,128)(2,1)S(1)}, bf16[512,128]{1,0:T(8,128)(2,1)S(1)}, u32[]{:S(2)}, u32[]{:S(2)}) %collective-permute-start.16) | collective-permute-done | bytes 131104 | tf_op jit(solution)/shard_map/ppermute | solution.py:302
  82.2 0.8 shard_map.179
  (48 shorter events, 2.0 us)
Async XLA Ops:
  0.6 28.2 %collective-permute-start.3 = (bf16[32,4096]{1,0:T(8,128)(2,1)}, bf16[32,4096]{1,0:T(8,128)(2,1)S(1)}, u32[]{:S(2)}, u32[]{:S(2)}) collective-permute-start(bf16[32,4096]{1,0:T(8,128)(2,1)} %top.1), channel_id=1, source_target_pairs={{0,4},{4,0},{8,12},{12,8},{1,5},{5,1},{9,13},{13,9},{2,6},{6,2},{1... | collective-permute-start | bytes 786440 | tf_op jit(solution)/shard_map/ppermute | solution.py:302
  3.7 25.2 %collective-permute-start = (bf16[32,4096]{1,0:T(8,128)(2,1)}, bf16[32,4096]{1,0:T(8,128)(2,1)S(1)}, u32[]{:S(2)}, u32[]{:S(2)}) collective-permute-start(bf16[32,4096]{1,0:T(8,128)(2,1)} %o0.1), channel_id=1, source_target_pairs={{0,4},{4,0},{8,12},{12,8},{1,5},{5,1},{9,13},{13,9},{2,6},{6,2},{1... | collective-permute-start | bytes 786440 | tf_op jit(solution)/shard_map/ppermute | solution.py:302
  3.8 25.1 %collective-permute-start.1 = (bf16[32,4096]{1,0:T(8,128)(2,1)}, bf16[32,4096]{1,0:T(8,128)(2,1)S(1)}, u32[]{:S(2)}, u32[]{:S(2)}) collective-permute-start(bf16[32,4096]{1,0:T(8,128)(2,1)} %o0.1), channel_id=1, source_target_pairs={{0,8},{4,12},{8,0},{12,4},{1,9},{5,13},{9,1},{13,5},{2,10},{6,14},... | collective-permute-start | bytes 786440 | tf_op jit(solution)/shard_map/ppermute | solution.py:302
  6.8 22.6 %collective-permute-start.2 = (bf16[32,4096]{1,0:T(8,128)(2,1)}, bf16[32,4096]{1,0:T(8,128)(2,1)S(1)}, u32[]{:S(2)}, u32[]{:S(2)}) collective-permute-start(bf16[32,4096]{1,0:T(8,128)(2,1)} %o0.1), channel_id=1, source_target_pairs={{0,12},{4,8},{8,4},{12,0},{1,13},{5,9},{9,5},{13,1},{2,14},{6,10},... | collective-permute-start | bytes 786440 | tf_op jit(solution)/shard_map/ppermute | solution.py:302
  22.2 6.1 %copy-start.2 = (bf16[128,2048]{1,0:T(8,128)(2,1)S(1)}, bf16[128,2048]{1,0:T(8,128)(2,1)}, u32[]{:S(2)}) copy-start(bf16[128,2048]{1,0:T(8,128)(2,1)} %g_ref.1) | copy-start | bytes 1572868
  22.2 6.1 %copy-start.3 = (bf16[128,2048]{1,0:T(8,128)(2,1)S(1)}, bf16[128,2048]{1,0:T(8,128)(2,1)}, u32[]{:S(2)}) copy-start(bf16[128,2048]{1,0:T(8,128)(2,1)} %u_ref.1) | copy-start | bytes 1572868
  22.2 6.7 %copy-start.6 = (bf16[32,4096]{1,0:T(8,128)(2,1)S(1)}, bf16[32,4096]{1,0:T(8,128)(2,1)}, u32[]{:S(2)}) copy-start(bf16[32,4096]{1,0:T(8,128)(2,1)} %top.1) | copy-start | bytes 786436
  22.2 7.2 %copy-start = (bf16[16,2048]{1,0:T(8,128)(2,1)S(1)}, bf16[16,2048]{1,0:T(8,128)(2,1)}, u32[]{:S(2)}) copy-start(bf16[16,2048]{1,0:T(8,128)(2,1)} %entry.5) | copy-start | bytes 196612
  22.2 7.2 %copy-start.4 = (bf16[32,4096]{1,0:T(8,128)(2,1)S(1)}, bf16[32,4096]{1,0:T(8,128)(2,1)}, u32[]{:S(2)}) copy-start(bf16[32,4096]{1,0:T(8,128)(2,1)} %o0.1) | copy-start | bytes 786436
  22.2 7.2 %copy-start.7 = (bf16[16,4096]{1,0:T(8,128)(2,1)S(1)}, bf16[16,4096]{1,0:T(8,128)(2,1)}, u32[]{:S(2)}) copy-start(bf16[16,4096]{1,0:T(8,128)(2,1)} %exit_ref.1) | copy-start | bytes 393220
  33.6 6.0 %collective-permute-start.4 = (f32[32,1152]{1,0:T(8,128)S(1)}, f32[32,1152]{1,0:T(8,128)S(1)}, u32[]{:S(2)}, u32[]{:S(2)}) collective-permute-start(f32[32,1152]{1,0:T(8,128)S(1)} %get-tuple-element.41), channel_id=1, source_target_pairs={{0,1},{1,0},{2,3},{3,2},{4,5},{5,4},{6,7},{7,6},{8,9},{9,8},{10,11... | collective-permute-start | bytes 442376 | tf_op jit(solution)/shard_map/ppermute | solution.py:302
  33.7 5.9 %collective-permute-start.5 = (f32[32,1152]{1,0:T(8,128)S(1)}, f32[32,1152]{1,0:T(8,128)S(1)}, u32[]{:S(2)}, u32[]{:S(2)}) collective-permute-start(f32[32,1152]{1,0:T(8,128)S(1)} %get-tuple-element.42), channel_id=1, source_target_pairs={{0,1},{1,0},{2,3},{3,2},{4,5},{5,4},{6,7},{7,6},{8,9},{9,8},{10,11... | collective-permute-start | bytes 442376 | tf_op jit(solution)/shard_map/ppermute | solution.py:302
  34.2 5.4 %collective-permute-start.6 = (f32[32,1152]{1,0:T(8,128)S(1)}, f32[32,1152]{1,0:T(8,128)S(1)}, u32[]{:S(2)}, u32[]{:S(2)}) collective-permute-start(f32[32,1152]{1,0:T(8,128)S(1)} %get-tuple-element.43), channel_id=1, source_target_pairs={{0,1},{1,0},{2,3},{3,2},{4,5},{5,4},{6,7},{7,6},{8,9},{9,8},{10,11... | collective-permute-start | bytes 442376 | tf_op jit(solution)/shard_map/ppermute | solution.py:302
  34.3 5.3 %collective-permute-start.7 = (f32[32,1152]{1,0:T(8,128)S(1)}, f32[32,1152]{1,0:T(8,128)S(1)}, u32[]{:S(2)}, u32[]{:S(2)}) collective-permute-start(f32[32,1152]{1,0:T(8,128)S(1)} %get-tuple-element.44), channel_id=1, source_target_pairs={{0,1},{1,0},{2,3},{3,2},{4,5},{5,4},{6,7},{7,6},{8,9},{9,8},{10,11... | collective-permute-start | bytes 442376 | tf_op jit(solution)/shard_map/ppermute | solution.py:302
  34.7 26.8 %collective-permute-start.14 = (bf16[64,4096]{1,0:T(8,128)(2,1)S(1)}, bf16[64,4096]{1,0:T(8,128)(2,1)S(1)}, u32[]{:S(2)}, u32[]{:S(2)}) collective-permute-start(bf16[64,4096]{1,0:T(8,128)(2,1)S(1)} %shard_map.170.rest_0_), channel_id=1, source_target_pairs={{0,8},{4,12},{8,0},{12,4},{1,9},{5,13},{9,1},{13,5},{2,10},{6,14},... | collective-permute-start | bytes 1572872 | tf_op jit(solution)/shard_map/ppermute | solution.py:302
  37.7 12.6 %copy-start.1 = (bf16[16,4096]{1,0:T(8,128)(2,1)S(1)}, bf16[16,4096]{1,0:T(8,128)(2,1)}, u32[]{:S(2)}) copy-start(bf16[16,4096]{1,0:T(8,128)(2,1)} %refs_11_.3) | copy-start | bytes 393220
  37.7 12.6 %copy-start.5 = (bf16[16,2048]{1,0:T(8,128)(2,1)S(1)}, bf16[16,2048]{1,0:T(8,128)(2,1)}, u32[]{:S(2)}) copy-start(bf16[16,2048]{1,0:T(8,128)(2,1)} %refs_10_.3) | copy-start | bytes 196612
  39.7 8.3 %collective-permute-start.8 = (bf16[688,128]{1,0:T(8,128)(2,1)S(1)}, bf16[688,128]{1,0:T(8,128)(2,1)S(1)}, u32[]{:S(2)}, u32[]{:S(2)}) collective-permute-start(bf16[688,128]{1,0:T(8,128)(2,1)S(1)} %shard_map.173.mine0), channel_id=1, source_target_pairs={{0,2},{1,3},{2,0},{3,1},{4,6},{5,7},{6,4},{7,5},{8,10},{9,11},{10,... | collective-permute-start | bytes 528392 | tf_op jit(solution)/shard_map/ppermute | solution.py:302
  42.5 5.5 %collective-permute-start.9 = (bf16[384,128]{1,0:T(8,128)(2,1)S(1)}, bf16[384,128]{1,0:T(8,128)(2,1)S(1)}, u32[]{:S(2)}, u32[]{:S(2)}) collective-permute-start(bf16[384,128]{1,0:T(8,128)(2,1)S(1)} %shard_map.174.mine1), channel_id=1, source_target_pairs={{0,2},{1,3},{2,0},{3,1},{4,6},{5,7},{6,4},{7,5},{8,10},{9,11},{10,... | collective-permute-start | bytes 294920 | tf_op jit(solution)/shard_map/ppermute | solution.py:302
  48.2 1.4 %collective-permute-start.12 = (bf16[64,1024]{1,0:T(8,128)(2,1)S(1)}, bf16[64,1024]{1,0:T(8,128)(2,1)S(1)}, u32[]{:S(2)}, u32[]{:S(2)}) collective-permute-start(bf16[64,1024]{1,0:T(8,128)(2,1)S(1)} %get-tuple-element.48.refs_2_.own0), channel_id=1, source_target_pairs={{0,1},{1,0},{2,3},{3,2},{4,5},{5,4},{6,7},{7,6},{8,9},{9,8},{10,11... | collective-permute-start | bytes 393224 | tf_op jit(solution)/shard_map/ppermute | solution.py:302
  48.3 1.5 %collective-permute-start.13 = (bf16[64,1024]{1,0:T(8,128)(2,1)S(1)}, bf16[64,1024]{1,0:T(8,128)(2,1)S(1)}, u32[]{:S(2)}, u32[]{:S(2)}) collective-permute-start(bf16[64,1024]{1,0:T(8,128)(2,1)S(1)} %get-tuple-element.49.refs_3_.own1), channel_id=1, source_target_pairs={{0,1},{1,0},{2,3},{3,2},{4,5},{5,4},{6,7},{7,6},{8,9},{9,8},{10,11... | collective-permute-start | bytes 393224 | tf_op jit(solution)/shard_map/ppermute | solution.py:302
  48.8 1.3 %collective-permute-start.10 = (bf16[64,1024]{1,0:T(8,128)(2,1)S(1)}, bf16[64,1024]{1,0:T(8,128)(2,1)S(1)}, u32[]{:S(2)}, u32[]{:S(2)}) collective-permute-start(bf16[64,1024]{1,0:T(8,128)(2,1)S(1)} %get-tuple-element.46.refs_0_), channel_id=1, source_target_pairs={{0,1},{1,0},{2,3},{3,2},{4,5},{5,4},{6,7},{7,6},{8,9},{9,8},{10,11... | collective-permute-start | bytes 393224 | tf_op jit(solution)/shard_map/ppermute | solution.py:302
  48.9 23.1 %copy-start.8 = (bf16[16,128]{1,0:T(8,128)(2,1)S(1)}, bf16[16,128]{1,0:T(8,128)(2,1)}, u32[]{:S(2)}) copy-start(bf16[16,128]{1,0:T(8,128)(2,1)} %up_act.1) | copy-start | bytes 12292
  48.9 23.1 %copy-start.9 = (bf16[16,128]{1,0:T(8,128)(2,1)S(1)}, bf16[16,128]{1,0:T(8,128)(2,1)}, u32[]{:S(2)}) copy-start(bf16[16,128]{1,0:T(8,128)(2,1)} %down_act.1) | copy-start | bytes 12292
  48.9 1.5 %collective-permute-start.11 = (bf16[64,1024]{1,0:T(8,128)(2,1)S(1)}, bf16[64,1024]{1,0:T(8,128)(2,1)S(1)}, u32[]{:S(2)}, u32[]{:S(2)}) collective-permute-start(bf16[64,1024]{1,0:T(8,128)(2,1)S(1)} %get-tuple-element.47.refs_1_), channel_id=1, source_target_pairs={{0,1},{1,0},{2,3},{3,2},{4,5},{5,4},{6,7},{7,6},{8,9},{9,8},{10,11... | collective-permute-start | bytes 393224 | tf_op jit(solution)/shard_map/ppermute | solution.py:302
  56.1 14.3 %collective-permute-start.18 = (bf16[560,128]{1,0:T(8,128)(2,1)S(1)}, bf16[560,128]{1,0:T(8,128)(2,1)S(1)}, u32[]{:S(2)}, u32[]{:S(2)}) collective-permute-start(bf16[560,128]{1,0:T(8,128)(2,1)S(1)} %get-tuple-element.51), channel_id=1, source_target_pairs={{0,4},{4,0},{8,12},{12,8},{1,5},{5,1},{9,13},{13,9},{2,6},{6,2},{1... | collective-permute-start | bytes 430088 | tf_op jit(solution)/shard_map/ppermute | solution.py:302
  56.2 17.0 %collective-permute-start.19 = (bf16[560,128]{1,0:T(8,128)(2,1)S(1)}, bf16[560,128]{1,0:T(8,128)(2,1)S(1)}, u32[]{:S(2)}, u32[]{:S(2)}) collective-permute-start(bf16[560,128]{1,0:T(8,128)(2,1)S(1)} %get-tuple-element.52), channel_id=1, source_target_pairs={{0,8},{4,12},{8,0},{12,4},{1,9},{5,13},{9,1},{13,5},{2,10},{6,14},... | collective-permute-start | bytes 430088 | tf_op jit(solution)/shard_map/ppermute | solution.py:302
  57.3 15.8 %collective-permute-start.20 = (bf16[560,128]{1,0:T(8,128)(2,1)S(1)}, bf16[560,128]{1,0:T(8,128)(2,1)S(1)}, u32[]{:S(2)}, u32[]{:S(2)}) collective-permute-start(bf16[560,128]{1,0:T(8,128)(2,1)S(1)} %get-tuple-element.53), channel_id=1, source_target_pairs={{0,12},{4,8},{8,4},{12,0},{1,13},{5,9},{9,5},{13,1},{2,14},{6,10},... | collective-permute-start | bytes 430088 | tf_op jit(solution)/shard_map/ppermute | solution.py:302
  67.5 7.0 %collective-permute-start.15 = (bf16[512,128]{1,0:T(8,128)(2,1)S(1)}, bf16[512,128]{1,0:T(8,128)(2,1)S(1)}, u32[]{:S(2)}, u32[]{:S(2)}) collective-permute-start(bf16[512,128]{1,0:T(8,128)(2,1)S(1)} %get-tuple-element.57), channel_id=1, source_target_pairs={{0,4},{4,0},{8,12},{12,8},{1,5},{5,1},{9,13},{13,9},{2,6},{6,2},{1... | collective-permute-start | bytes 393224 | tf_op jit(solution)/shard_map/ppermute | solution.py:302
  67.6 14.5 %collective-permute-start.16 = (bf16[512,128]{1,0:T(8,128)(2,1)S(1)}, bf16[512,128]{1,0:T(8,128)(2,1)S(1)}, u32[]{:S(2)}, u32[]{:S(2)}) collective-permute-start(bf16[512,128]{1,0:T(8,128)(2,1)S(1)} %get-tuple-element.58), channel_id=1, source_target_pairs={{0,8},{4,12},{8,0},{12,4},{1,9},{5,13},{9,1},{13,5},{2,10},{6,14},... | collective-permute-start | bytes 393224 | tf_op jit(solution)/shard_map/ppermute | solution.py:302
  70.5 11.7 %collective-permute-start.17 = (bf16[512,128]{1,0:T(8,128)(2,1)S(1)}, bf16[512,128]{1,0:T(8,128)(2,1)S(1)}, u32[]{:S(2)}, u32[]{:S(2)}) collective-permute-start(bf16[512,128]{1,0:T(8,128)(2,1)S(1)} %get-tuple-element.59), channel_id=1, source_target_pairs={{0,12},{4,8},{8,4},{12,0},{1,13},{5,9},{9,5},{13,1},{2,14},{6,10},... | collective-permute-start | bytes 393224 | tf_op jit(solution)/shard_map/ppermute | solution.py:302

commit v5 on v4

--- a/solution.py
+++ b/solution.py
@@ -254,30 +254,10 @@
         ).astype(bf16)
 
 
-def stack_kernel(top, bottom, *outs):
-    n = top.shape[0]
-    first = 0
-    for out in outs:
-        lanes = slice(first, first + out.shape[1])
-        out[:n, :] = top[:, lanes]
-        out[n:, :] = bottom[:, lanes]
-        first = lanes.stop
-
-
-def entry_kernel(offset, pieces, low, r1, r2, r3, *rest):
-    near, far = rest[:pieces], rest[pieces : 2 * pieces]
-    out, full, lows = rest[2 * pieces :]
+def entry_kernel(offset, low, r1, r2, r3, i0, i1, i2, i3, out, full, lows):
     row = lax.axis_index("row")
     rank = low.shape[0]
-    n = near[0].shape[0] // 2
-    first = 0
-    for here, there in zip(near, far):
-        lanes = slice(first, first + here.shape[1])
-        for k in range(4):
-            ref = here if k < 2 else there
-            rows = pl.ds(pl.multiple_of((row ^ k) * n, n), n)
-            full[rows, lanes] = ref[(k % 2) * n : (k % 2 + 1) * n, :]
-        first = lanes.stop
+    place_rows(full, (i0, i1, i2, i3), row)
     lows[row] = low[...]
     for k, ref in ((1, r1), (2, r2), (3, r3)):
         lows[row ^ k] = load_terms(ref, offset, rank)
@@ -327,20 +307,15 @@
     rank = up_adapter_exit.shape[0]
     half = hidden // 2
     own_gradient = output_gradient
-    gathered = [swap(own_gradient, "row", k, 4) for k in (1, 2, 3)]
+    gathered = [swap(own_gradient, "row", k, 4) for k in (1, 2)]
     parts = [width // 8 * e for e in EIGHTHS]
     firsts = [sum(parts[:c]) for c in range(CHUNKS)]
     down_v = fetch(down_weight, 0, hidden)
     gate_v = [fetch(gate_weight, firsts[c], parts[c]) for c in range(CHUNKS)]
-    up_v = [fetch(up_weight, firsts[c], parts[c]) for c in range(CHUNKS)]
-    a, b, hidden_state = call(
-        factors_kernel,
-        (shape((tokens, hidden), f32), shape((tokens, hidden), f32), shape((tokens, hidden), bf16)),
-        gate_preactivation,
-        up_preactivation,
-    )
-    near = [call(stack_kernel, shape((2 * share, width), bf16), inputs, swap(inputs, "row", 1, 4))]
-    down_v = after(down_v, gate_v, up_v, a, b, near)
+    up_v = [fetch(up_weight, firsts[c], parts[c]) for c in range(CHUNKS - 1)]
+    near = swap(inputs, "row", 1, 4)
+    gathered.append(swap(after(gathered[1], gate_v, up_v, near), "row", 1, 4))
+    down_v = after(down_v, gate_v, up_v, near)
 
     quarter = shape((tokens // 4, half + LANES), f32)
     *send, low_piece, full_gradient = call(
@@ -353,7 +328,8 @@
         down_adapter_entry,
     )
     got = [swap(x, "col", 1, 4) for x in send]
-    far = [swap(near[0], "row", 2, 4)]
+    far = swap(after(inputs, gathered, near), "row", 2, 4)
+    last = swap(far, "row", 1, 4)
     first = half // 8 * KEEP_EIGHTHS
     keep = call(
         functools.partial(keep_kernel, half, 256),
@@ -381,12 +357,19 @@
     )
     payload = (early, late)
     other = [swap(x, "col", 2, 4) for x in payload]
+    up_v.append(fetch(after(up_weight, payload), firsts[-1], parts[-1]))
+    a, b, hidden_state = call(
+        factors_kernel,
+        (shape((tokens, hidden), f32), shape((tokens, hidden), f32), shape((tokens, hidden), bf16)),
+        after(gate_preactivation, payload),
+        up_preactivation,
+    )
     *grads, low_full = call(
         gradient_kernel,
         (shape((tokens // 2, half), bf16),) * 4 + (shape((rank, tokens), f32),),
         *payload,
         *other,
-        a,
+        after(a, up_v),
         b,
     )
     mate_grads = [swap(x, "col", 1, 4) for x in grads]
@@ -403,7 +386,7 @@
             + ((shape((rank, tokens), f32),) if with_low else ()),
             *grads,
             *mate_grads,
-            in_vmem(after(gate_v[c], outs, far) if c else gate_v[c]),
+            in_vmem(after(gate_v[c], outs, last) if c else gate_v[c]),
             in_vmem(up_v[c]),
             up_adapter_exit,
             up_adapter_entry,
@@ -423,12 +406,14 @@
         own = after(owns[c], owns[c + 1]) if c + 1 < CHUNKS else owns[c]
         input_grad = (call(finish_kernel, done, own, *received[c], *input_grad),)
     entry_sum = call(
-        functools.partial(entry_kernel, parts[0] // LANES * share, 1),
+        functools.partial(entry_kernel, parts[0] // LANES * share),
         shape((rank, width), f32),
         after(low_up, owns),
         *received[0],
-        *near,
-        *far,
+        inputs,
+        near,
+        far,
+        last,
         scratch=[pltpu.VMEM((tokens, width), bf16), pltpu.VMEM((4, rank, tokens), f32)],
     )
     up_exit_gradient, down_entry_gradient, down_exit_gradient = call(

time: 83.1 us -> 81.4 us (0.980)
  waiting for transfers between devices: 14.9 us -> 11.3 us
  starting transfers between devices: 23.7 us -> 25.8 us
    ppermute x21 -> x22, waiting for transfers between devices: 14.9 us -> 11.3 us  [swap(): return lax.ppermute(x, axis, [(i, i ^ distance) for i in range(n)])]
    ppermute x21 -> x22, starting transfers between devices: 23.7 us -> 25.8 us  [swap(): return lax.ppermute(x, axis, [(i, i ^ distance) for i in range(n)])]
    pallas_call x18 -> x17, Pallas kernels: 43.4 us -> 43.3 us  [call(): pl.pallas_call(kernel, out_shape=tuple(outs), in_specs=specs if specs is...]
  transfers between devices with their start and end apart: 21 -> 22, of which waited for: 8 -> 4; matrix products, arithmetic and copies ran while one was open for 0% -> 0% of each run, Pallas kernels for 46% -> 47%
where the time goes in v5:
time: 81.4 us; the launch traced here: 81.3 us
  Pallas kernels  43.3 us (53%)
  starting transfers between devices  25.8 us (32%)
  waiting for transfers between devices  11.3 us (14%)
  between operations  0.94 us (1%)
    pallas_call x17, Pallas kernels, call(): pl.pallas_call(kernel, out_shape=tuple(outs), in_specs=specs if specs is...  43.3 us
    ppermute x22, starting transfers between devices, swap(): return lax.ppermute(x, axis, [(i, i ^ distance) for i in range(n)])  25.8 us
    ppermute x22, waiting for transfers between devices, swap(): return lax.ppermute(x, axis, [(i, i ^ distance) for i in range(n)])  11.3 us
  transfers between devices with their start and end apart: 22, of which 4 were waited for; matrix products, arithmetic and copies ran while one was open for 0% of the time, Pallas kernels for 47%

profile of v5, /device:TPU:0, one launch (start us, length us, event | category | flops | bytes accessed | tf_op | source)
XLA Modules:
  0.0 81.3 jit_solution(3332716421551582347)
XLA Ops:
  0.6 3.1 %collective-permute-start.2 = (bf16[32,4096]{1,0:T(8,128)(2,1)}, bf16[32,4096]{1,0:T(8,128)(2,1)S(1)}, u32[]{:S(2)}, u32[]{:S(2)}) collective-permute-start(bf16[32,4096]{1,0:T(8,128)(2,1)} %i0.1), channel_id=1, source_target_pairs={{0,4},{4,0},{8,12},{12,8},{1,5},{5,1},{9,13},{13,9},{2,6},{6,2},{1... | collective-permute-start | bytes 786440 | tf_op jit(solution)/shard_map/ppermute | solution.py:282
  3.7 2.6 %collective-permute-start.1 = (bf16[32,4096]{1,0:T(8,128)(2,1)}, bf16[32,4096]{1,0:T(8,128)(2,1)S(1)}, u32[]{:S(2)}, u32[]{:S(2)}) collective-permute-start(bf16[32,4096]{1,0:T(8,128)(2,1)} %o0.1), channel_id=1, source_target_pairs={{0,8},{4,12},{8,0},{12,4},{1,9},{5,13},{9,1},{13,5},{2,10},{6,14},... | collective-permute-start | bytes 786440 | tf_op jit(solution)/shard_map/ppermute | solution.py:282
  6.8 3.5 %shard_map.164.refs_8_ = bf16[2048,2048]{1,0:T(8,128)(2,1)S(1)} custom-call(bf16[4096,2048]{1,0:T(8,128)(2,1)} %src.5), custom_call_target="tpu_custom_call" | custom-call | tf_op jit(solution)/shard_map/pallas_call | solution.py:46
  10.3 3.5 %shard_map.165.refs_8_ = bf16[2048,2048]{1,0:T(8,128)(2,1)S(1)} custom-call(bf16[4096,2048]{1,0:T(8,128)(2,1)} %src.5), custom_call_target="tpu_custom_call" | custom-call | tf_op jit(solution)/shard_map/pallas_call | solution.py:46
  13.8 3.5 %shard_map.166.refs_9_ = bf16[2048,2048]{1,0:T(8,128)(2,1)S(1)} custom-call(bf16[4096,2048]{1,0:T(8,128)(2,1)} %src.8), custom_call_target="tpu_custom_call" | custom-call | tf_op jit(solution)/shard_map/pallas_call | solution.py:46
  17.3 2.4 %collective-permute-start.3 = (bf16[32,4096]{1,0:T(8,128)(2,1)S(1)}, bf16[32,4096]{1,0:T(8,128)(2,1)S(1)}, u32[]{:S(2)}, u32[]{:S(2)}) collective-permute-start(bf16[32,4096]{1,0:T(8,128)(2,1)S(1)} %collective-permute-done.1.o2), channel_id=1, source_target_pairs={{0,4},{4,0},{8,12},{12,8},{1,5},{5,1},{9,13},{13,9},{2,6},{6,2},{1... | collective-permute-start | bytes 786440 | tf_op jit(solution)/shard_map/ppermute | solution.py:282
  19.8 5.9 %shard_map.167.w = bf16[2048,4096]{1,0:T(8,128)(2,1)S(1)} custom-call(bf16[2048,4096]{1,0:T(8,128)(2,1)} %src.7), custom_call_target="tpu_custom_call" | custom-call | tf_op jit(solution)/shard_map/pallas_call | solution.py:46
  25.7 1.4 %collective-permute-done.3.o3 = bf16[32,4096]{1,0:T(8,128)(2,1)S(1)} collective-permute-done((bf16[32,4096]{1,0:T(8,128)(2,1)S(1)}, bf16[32,4096]{1,0:T(8,128)(2,1)S(1)}, u32[]{:S(2)}, u32[]{:S(2)}) %collective-permute-start.3) | collective-permute-done | bytes 262176 | tf_op jit(solution)/shard_map/ppermute | solution.py:282
  27.1 4.2 %shard_map.168 = (f32[32,1152]{1,0:T(8,128)S(1)}, f32[32,1152]{1,0:T(8,128)S(1)}, f32[32,1152]{1,0:T(8,128)S(1)}, f32[32,1152]{1,0:T(8,128)S(1)}, f32[16,128]{1,0:T(8,128)S(1)}, /*index=5*/bf16[128,4096]{1,0:T(8,128)(2,1)S(1)}) custom-call(bf16[32,4096]{1,0:T(8,128)(2,1)S(1)} %copy-done.4, bf16[32,4096]{1,0:T(8,128)(2,1)S(1)} %collective-permute-done.o1, ...), custom_call_target="tpu_custom_call" | custom-call | tf_op jit(solution)/shard_map/pallas_call | solution.py:46
  31.4 0.5 collective-permute-start.5
  32.4 2.8 %collective-permute-start.14 = (bf16[32,4096]{1,0:T(8,128)(2,1)S(1)}, bf16[32,4096]{1,0:T(8,128)(2,1)S(1)}, u32[]{:S(2)}, u32[]{:S(2)}) collective-permute-start(bf16[32,4096]{1,0:T(8,128)(2,1)S(1)} %copy-done.6), channel_id=1, source_target_pairs={{0,8},{4,12},{8,0},{12,4},{1,9},{5,13},{9,1},{13,5},{2,10},{6,14},... | collective-permute-start | bytes 786440 | tf_op jit(solution)/shard_map/ppermute | solution.py:282
  35.2 1.9 %shard_map.169.keep = f32[128,640]{1,0:T(8,128)S(1)} custom-call(bf16[128,4096]{1,0:T(8,128)(2,1)S(1)} %get-tuple-element.49.full, f32[16,128]{1,0:T(8,128)S(1)} %get-tuple-element.44.low, bf16[2048,4096]{1,0:T(8,128)(2,1)S(1)} %shard_map.167.w, bf16[16,2048]{1,0:T(8,128)(2,1)S(1)} %copy-done), custom_call_target="tpu_custom_call" | custom-call | tf_op jit(solution)/shard_map/pallas_call | solution.py:46
  37.2 1.6 %collective-permute-start.8 = (bf16[688,128]{1,0:T(8,128)(2,1)S(1)}, bf16[688,128]{1,0:T(8,128)(2,1)S(1)}, u32[]{:S(2)}, u32[]{:S(2)}) collective-permute-start(bf16[688,128]{1,0:T(8,128)(2,1)S(1)} %shard_map.170.mine0), channel_id=1, source_target_pairs={{0,2},{1,3},{2,0},{3,1},{4,6},{5,7},{6,4},{7,5},{8,10},{9,11},{10,... | collective-permute-start | bytes 528392 | tf_op jit(solution)/shard_map/ppermute | solution.py:282
  38.8 1.3 %shard_map.171.mine1 = bf16[384,128]{1,0:T(8,128)(2,1)S(1)} custom-call(bf16[128,4096]{1,0:T(8,128)(2,1)S(1)} %get-tuple-element.49.full, f32[16,128]{1,0:T(8,128)S(1)} %get-tuple-element.44.low, bf16[2048,4096]{1,0:T(8,128)(2,1)S(1)} %shard_map.167.w, bf16[16,2048]{1,0:T(8,128)(2,1)S(1)} %copy-done, f32[32,1152]{1,0:T(8,128)S(1)} %collective-permute-done.4.rest_0_, ...), custom_call_target="tpu_custom_call" | custom-call | tf_op jit(solution)/shard_map/pallas_call | solution.py:46
  40.1 0.6 collective-permute-start.9
  40.7 3.5 %shard_map.173.refs_9_ = bf16[2048,2048]{1,0:T(8,128)(2,1)S(1)} custom-call(bf16[4096,2048]{1,0:T(8,128)(2,1)} %src.8), custom_call_target="tpu_custom_call" | custom-call | tf_op jit(solution)/shard_map/pallas_call | solution.py:46
  44.2 0.6 shard_map.172
  44.8 0.7 collective-permute-done.9.other1
  46.8 0.6 collective-permute-done.14.i2
  47.4 1.0 %collective-permute-start.15 = (bf16[32,4096]{1,0:T(8,128)(2,1)S(1)}, bf16[32,4096]{1,0:T(8,128)(2,1)S(1)}, u32[]{:S(2)}, u32[]{:S(2)}) collective-permute-start(bf16[32,4096]{1,0:T(8,128)(2,1)S(1)} %collective-permute-done.14.i2), channel_id=1, source_target_pairs={{0,4},{4,0},{8,12},{12,8},{1,5},{5,1},{9,13},{13,9},{2,6},{6,2},{1... | collective-permute-start | bytes 786440 | tf_op jit(solution)/shard_map/ppermute | solution.py:282
  48.4 5.8 %shard_map.175 = (f32[32,2048]{1,0:T(8,128)S(1)}, bf16[560,128]{1,0:T(8,128)(2,1)S(1)}, bf16[560,128]{1,0:T(8,128)(2,1)S(1)}, bf16[560,128]{1,0:T(8,128)(2,1)S(1)}, f32[16,128]{1,0:T(8,128)S(1)}) custom-call(bf16[64,1024]{1,0:T(8,128)(2,1)S(1)} %get-tuple-element.55.refs_0_, bf16[64,1024]{1,0:T(8,128)(2,1)S(1)} %get-tuple-element.56.refs_1_, ...), custom_call_target="tpu_custom_call" | custom-call | tf_op jit(solution)/shard_map/pallas_call | solution.py:46
  54.2 1.1 %collective-permute-start.19 = (bf16[560,128]{1,0:T(8,128)(2,1)S(1)}, bf16[560,128]{1,0:T(8,128)(2,1)S(1)}, u32[]{:S(2)}, u32[]{:S(2)}) collective-permute-start(bf16[560,128]{1,0:T(8,128)(2,1)S(1)} %get-tuple-element.60), channel_id=1, source_target_pairs={{0,4},{4,0},{8,12},{12,8},{1,5},{5,1},{9,13},{13,9},{2,6},{6,2},{1... | collective-permute-start | bytes 430088 | tf_op jit(solution)/shard_map/ppermute | solution.py:282
  55.3 2.2 %collective-permute-start.20 = (bf16[560,128]{1,0:T(8,128)(2,1)S(1)}, bf16[560,128]{1,0:T(8,128)(2,1)S(1)}, u32[]{:S(2)}, u32[]{:S(2)}) collective-permute-start(bf16[560,128]{1,0:T(8,128)(2,1)S(1)} %get-tuple-element.61), channel_id=1, source_target_pairs={{0,8},{4,12},{8,0},{12,4},{1,9},{5,13},{9,1},{13,5},{2,10},{6,14},... | collective-permute-start | bytes 430088 | tf_op jit(solution)/shard_map/ppermute | solution.py:282
  57.5 1.4 %collective-permute-start.21 = (bf16[560,128]{1,0:T(8,128)(2,1)S(1)}, bf16[560,128]{1,0:T(8,128)(2,1)S(1)}, u32[]{:S(2)}, u32[]{:S(2)}) collective-permute-start(bf16[560,128]{1,0:T(8,128)(2,1)S(1)} %get-tuple-element.62), channel_id=1, source_target_pairs={{0,12},{4,8},{8,4},{12,0},{1,13},{5,9},{9,5},{13,1},{2,14},{6,10},... | collective-permute-start | bytes 430088 | tf_op jit(solution)/shard_map/ppermute | solution.py:282
  58.9 6.0 %shard_map.176 = (f32[32,2048]{1,0:T(8,128)S(1)}, bf16[512,128]{1,0:T(8,128)(2,1)S(1)}, bf16[512,128]{1,0:T(8,128)(2,1)S(1)}, bf16[512,128]{1,0:T(8,128)(2,1)S(1)}) custom-call(bf16[64,1024]{1,0:T(8,128)(2,1)S(1)} %get-tuple-element.55.refs_0_, bf16[64,1024]{1,0:T(8,128)(2,1)S(1)} %get-tuple-element.56.refs_1_, ...), custom_call_target="tpu_custom_call" | custom-call | tf_op jit(solution)/shard_map/pallas_call | solution.py:46
  64.9 0.6 collective-permute-start.16
  65.5 2.5 %collective-permute-start.17 = (bf16[512,128]{1,0:T(8,128)(2,1)S(1)}, bf16[512,128]{1,0:T(8,128)(2,1)S(1)}, u32[]{:S(2)}, u32[]{:S(2)}) collective-permute-start(bf16[512,128]{1,0:T(8,128)(2,1)S(1)} %get-tuple-element.68), channel_id=1, source_target_pairs={{0,8},{4,12},{8,0},{12,4},{1,9},{5,13},{9,1},{13,5},{2,10},{6,14},... | collective-permute-start | bytes 393224 | tf_op jit(solution)/shard_map/ppermute | solution.py:282
  68.0 1.4 %collective-permute-start.18 = (bf16[512,128]{1,0:T(8,128)(2,1)S(1)}, bf16[512,128]{1,0:T(8,128)(2,1)S(1)}, u32[]{:S(2)}, u32[]{:S(2)}) collective-permute-start(bf16[512,128]{1,0:T(8,128)(2,1)S(1)} %get-tuple-element.69), channel_id=1, source_target_pairs={{0,12},{4,8},{8,4},{12,0},{1,13},{5,9},{9,5},{13,1},{2,14},{6,10},... | collective-permute-start | bytes 393224 | tf_op jit(solution)/shard_map/ppermute | solution.py:282
  69.3 1.2 %shard_map.180 = (f32[16,2048]{1,0:T(8,128)}, f32[16,2048]{1,0:T(8,128)}, f32[16,4096]{1,0:T(8,128)}) custom-call(bf16[64,1024]{1,0:T(8,128)(2,1)S(1)} %get-tuple-element.57.refs_2_.own0, bf16[64,1024]{1,0:T(8,128)(2,1)S(1)} %get-tuple-element.58.refs_3_.own1, bf16[64,1024]{1,0:T(8,128)(2,1)S(1)} %collective-permute-done.12.refs_6_.mate0, ...), custom_call_target="tpu_custom_call" | custom-call | tf_op jit(solution)/shard_map/pallas_call | solution.py:46
  70.5 1.3 %shard_map.179 = f32[16,4096]{1,0:T(8,128)} custom-call(f32[16,128]{1,0:T(8,128)S(1)} %get-tuple-element.71.low, bf16[560,128]{1,0:T(8,128)(2,1)S(1)} %collective-permute-done.19.r1, bf16[560,128]{1,0:T(8,128)(2,1)S(1)} %collective-permute-done.20.r2, bf16[560,128]{1,0:T(8,128)(2,1)S(1)} %collective-permute-done.21.r3, bf16[32,4096]{1,0:T(8,128)(2,1)S(1)} %copy-done.6, ...), custom_call_target="tpu_custom_call" | custom-call | tf_op jit(solution)/shard_map/pallas_call | solution.py:46
  71.9 8.6 %collective-permute-done.17.r2 = bf16[512,128]{1,0:T(8,128)(2,1)S(1)} collective-permute-done((bf16[512,128]{1,0:T(8,128)(2,1)S(1)}, bf16[512,128]{1,0:T(8,128)(2,1)S(1)}, u32[]{:S(2)}, u32[]{:S(2)}) %collective-permute-start.17) | collective-permute-done | bytes 131104 | tf_op jit(solution)/shard_map/ppermute | solution.py:282
  80.5 0.8 shard_map.178
  (49 shorter events, 2.5 us)
Async XLA Ops:
  0.6 16.7 %collective-permute-start.2 = (bf16[32,4096]{1,0:T(8,128)(2,1)}, bf16[32,4096]{1,0:T(8,128)(2,1)S(1)}, u32[]{:S(2)}, u32[]{:S(2)}) collective-permute-start(bf16[32,4096]{1,0:T(8,128)(2,1)} %i0.1), channel_id=1, source_target_pairs={{0,4},{4,0},{8,12},{12,8},{1,5},{5,1},{9,13},{13,9},{2,6},{6,2},{1... | collective-permute-start | bytes 786440 | tf_op jit(solution)/shard_map/ppermute | solution.py:282
  3.7 13.6 %collective-permute-start.1 = (bf16[32,4096]{1,0:T(8,128)(2,1)}, bf16[32,4096]{1,0:T(8,128)(2,1)S(1)}, u32[]{:S(2)}, u32[]{:S(2)}) collective-permute-start(bf16[32,4096]{1,0:T(8,128)(2,1)} %o0.1), channel_id=1, source_target_pairs={{0,8},{4,12},{8,0},{12,4},{1,9},{5,13},{9,1},{13,5},{2,10},{6,14},... | collective-permute-start | bytes 786440 | tf_op jit(solution)/shard_map/ppermute | solution.py:282
  6.3 19.4 %collective-permute-start = (bf16[32,4096]{1,0:T(8,128)(2,1)}, bf16[32,4096]{1,0:T(8,128)(2,1)S(1)}, u32[]{:S(2)}, u32[]{:S(2)}) collective-permute-start(bf16[32,4096]{1,0:T(8,128)(2,1)} %o0.1), channel_id=1, source_target_pairs={{0,4},{4,0},{8,12},{12,8},{1,5},{5,1},{9,13},{13,9},{2,6},{6,2},{1... | collective-permute-start | bytes 786440 | tf_op jit(solution)/shard_map/ppermute | solution.py:282
  17.3 9.8 %copy-start = (bf16[16,2048]{1,0:T(8,128)(2,1)S(1)}, bf16[16,2048]{1,0:T(8,128)(2,1)}, u32[]{:S(2)}) copy-start(bf16[16,2048]{1,0:T(8,128)(2,1)} %entry.5) | copy-start | bytes 196612
  17.3 9.8 %copy-start.4 = (bf16[32,4096]{1,0:T(8,128)(2,1)S(1)}, bf16[32,4096]{1,0:T(8,128)(2,1)}, u32[]{:S(2)}) copy-start(bf16[32,4096]{1,0:T(8,128)(2,1)} %o0.1) | copy-start | bytes 786436
  17.3 9.8 %copy-start.7 = (bf16[16,4096]{1,0:T(8,128)(2,1)S(1)}, bf16[16,4096]{1,0:T(8,128)(2,1)}, u32[]{:S(2)}) copy-start(bf16[16,4096]{1,0:T(8,128)(2,1)} %exit_ref.1) | copy-start | bytes 393220
  17.3 9.7 %collective-permute-start.3 = (bf16[32,4096]{1,0:T(8,128)(2,1)S(1)}, bf16[32,4096]{1,0:T(8,128)(2,1)S(1)}, u32[]{:S(2)}, u32[]{:S(2)}) collective-permute-start(bf16[32,4096]{1,0:T(8,128)(2,1)S(1)} %collective-permute-done.1.o2), channel_id=1, source_target_pairs={{0,4},{4,0},{8,12},{12,8},{1,5},{5,1},{9,13},{13,9},{2,6},{6,2},{1... | collective-permute-start | bytes 786440 | tf_op jit(solution)/shard_map/ppermute | solution.py:282
  25.7 6.7 %copy-start.6 = (bf16[32,4096]{1,0:T(8,128)(2,1)S(1)}, bf16[32,4096]{1,0:T(8,128)(2,1)}, u32[]{:S(2)}) copy-start(bf16[32,4096]{1,0:T(8,128)(2,1)} %i0.1) | copy-start | bytes 786436
  31.3 5.8 %collective-permute-start.4 = (f32[32,1152]{1,0:T(8,128)S(1)}, f32[32,1152]{1,0:T(8,128)S(1)}, u32[]{:S(2)}, u32[]{:S(2)}) collective-permute-start(f32[32,1152]{1,0:T(8,128)S(1)} %get-tuple-element.45), channel_id=1, source_target_pairs={{0,1},{1,0},{2,3},{3,2},{4,5},{5,4},{6,7},{7,6},{8,9},{9,8},{10,11... | collective-permute-start | bytes 442376 | tf_op jit(solution)/shard_map/ppermute | solution.py:282
  31.4 5.7 %collective-permute-start.5 = (f32[32,1152]{1,0:T(8,128)S(1)}, f32[32,1152]{1,0:T(8,128)S(1)}, u32[]{:S(2)}, u32[]{:S(2)}) collective-permute-start(f32[32,1152]{1,0:T(8,128)S(1)} %get-tuple-element.46), channel_id=1, source_target_pairs={{0,1},{1,0},{2,3},{3,2},{4,5},{5,4},{6,7},{7,6},{8,9},{9,8},{10,11... | collective-permute-start | bytes 442376 | tf_op jit(solution)/shard_map/ppermute | solution.py:282
  31.9 5.2 %collective-permute-start.6 = (f32[32,1152]{1,0:T(8,128)S(1)}, f32[32,1152]{1,0:T(8,128)S(1)}, u32[]{:S(2)}, u32[]{:S(2)}) collective-permute-start(f32[32,1152]{1,0:T(8,128)S(1)} %get-tuple-element.47), channel_id=1, source_target_pairs={{0,1},{1,0},{2,3},{3,2},{4,5},{5,4},{6,7},{7,6},{8,9},{9,8},{10,11... | collective-permute-start | bytes 442376 | tf_op jit(solution)/shard_map/ppermute | solution.py:282
  32.0 5.2 %collective-permute-start.7 = (f32[32,1152]{1,0:T(8,128)S(1)}, f32[32,1152]{1,0:T(8,128)S(1)}, u32[]{:S(2)}, u32[]{:S(2)}) collective-permute-start(f32[32,1152]{1,0:T(8,128)S(1)} %get-tuple-element.48), channel_id=1, source_target_pairs={{0,1},{1,0},{2,3},{3,2},{4,5},{5,4},{6,7},{7,6},{8,9},{9,8},{10,11... | collective-permute-start | bytes 442376 | tf_op jit(solution)/shard_map/ppermute | solution.py:282
  32.4 15.0 %collective-permute-start.14 = (bf16[32,4096]{1,0:T(8,128)(2,1)S(1)}, bf16[32,4096]{1,0:T(8,128)(2,1)S(1)}, u32[]{:S(2)}, u32[]{:S(2)}) collective-permute-start(bf16[32,4096]{1,0:T(8,128)(2,1)S(1)} %copy-done.6), channel_id=1, source_target_pairs={{0,8},{4,12},{8,0},{12,4},{1,9},{5,13},{9,1},{13,5},{2,10},{6,14},... | collective-permute-start | bytes 786440 | tf_op jit(solution)/shard_map/ppermute | solution.py:282
  37.2 8.3 %collective-permute-start.8 = (bf16[688,128]{1,0:T(8,128)(2,1)S(1)}, bf16[688,128]{1,0:T(8,128)(2,1)S(1)}, u32[]{:S(2)}, u32[]{:S(2)}) collective-permute-start(bf16[688,128]{1,0:T(8,128)(2,1)S(1)} %shard_map.170.mine0), channel_id=1, source_target_pairs={{0,2},{1,3},{2,0},{3,1},{4,6},{5,7},{6,4},{7,5},{8,10},{9,11},{10,... | collective-permute-start | bytes 528392 | tf_op jit(solution)/shard_map/ppermute | solution.py:282
  40.0 4.1 %copy-start.2 = (bf16[128,2048]{1,0:T(8,128)(2,1)S(1)}, bf16[128,2048]{1,0:T(8,128)(2,1)}, u32[]{:S(2)}) copy-start(bf16[128,2048]{1,0:T(8,128)(2,1)} %g_ref) | copy-start | bytes 1572868
  40.0 4.1 %copy-start.3 = (bf16[128,2048]{1,0:T(8,128)(2,1)S(1)}, bf16[128,2048]{1,0:T(8,128)(2,1)}, u32[]{:S(2)}) copy-start(bf16[128,2048]{1,0:T(8,128)(2,1)} %u_ref.1) | copy-start | bytes 1572868
  40.1 8.3 %copy-start.1 = (bf16[16,4096]{1,0:T(8,128)(2,1)S(1)}, bf16[16,4096]{1,0:T(8,128)(2,1)}, u32[]{:S(2)}) copy-start(bf16[16,4096]{1,0:T(8,128)(2,1)} %refs_11_.3) | copy-start | bytes 393220
  40.1 8.3 %copy-start.5 = (bf16[16,2048]{1,0:T(8,128)(2,1)S(1)}, bf16[16,2048]{1,0:T(8,128)(2,1)}, u32[]{:S(2)}) copy-start(bf16[16,2048]{1,0:T(8,128)(2,1)} %refs_10_.3) | copy-start | bytes 196612
  40.1 5.4 %collective-permute-start.9 = (bf16[384,128]{1,0:T(8,128)(2,1)S(1)}, bf16[384,128]{1,0:T(8,128)(2,1)S(1)}, u32[]{:S(2)}, u32[]{:S(2)}) collective-permute-start(bf16[384,128]{1,0:T(8,128)(2,1)S(1)} %shard_map.171.mine1), channel_id=1, source_target_pairs={{0,2},{1,3},{2,0},{3,1},{4,6},{5,7},{6,4},{7,5},{8,10},{9,11},{10,... | collective-permute-start | bytes 294920 | tf_op jit(solution)/shard_map/ppermute | solution.py:282
  45.7 2.6 %collective-permute-start.12 = (bf16[64,1024]{1,0:T(8,128)(2,1)S(1)}, bf16[64,1024]{1,0:T(8,128)(2,1)S(1)}, u32[]{:S(2)}, u32[]{:S(2)}) collective-permute-start(bf16[64,1024]{1,0:T(8,128)(2,1)S(1)} %get-tuple-element.57.refs_2_.own0), channel_id=1, source_target_pairs={{0,1},{1,0},{2,3},{3,2},{4,5},{5,4},{6,7},{7,6},{8,9},{9,8},{10,11... | collective-permute-start | bytes 393224 | tf_op jit(solution)/shard_map/ppermute | solution.py:282
  45.8 2.6 %collective-permute-start.13 = (bf16[64,1024]{1,0:T(8,128)(2,1)S(1)}, bf16[64,1024]{1,0:T(8,128)(2,1)S(1)}, u32[]{:S(2)}, u32[]{:S(2)}) collective-permute-start(bf16[64,1024]{1,0:T(8,128)(2,1)S(1)} %get-tuple-element.58.refs_3_.own1), channel_id=1, source_target_pairs={{0,1},{1,0},{2,3},{3,2},{4,5},{5,4},{6,7},{7,6},{8,9},{9,8},{10,11... | collective-permute-start | bytes 393224 | tf_op jit(solution)/shard_map/ppermute | solution.py:282
  46.3 2.1 %collective-permute-start.10 = (bf16[64,1024]{1,0:T(8,128)(2,1)S(1)}, bf16[64,1024]{1,0:T(8,128)(2,1)S(1)}, u32[]{:S(2)}, u32[]{:S(2)}) collective-permute-start(bf16[64,1024]{1,0:T(8,128)(2,1)S(1)} %get-tuple-element.55.refs_0_), channel_id=1, source_target_pairs={{0,1},{1,0},{2,3},{3,2},{4,5},{5,4},{6,7},{7,6},{8,9},{9,8},{10,11... | collective-permute-start | bytes 393224 | tf_op jit(solution)/shard_map/ppermute | solution.py:282
  46.4 23.0 %copy-start.8 = (bf16[16,128]{1,0:T(8,128)(2,1)S(1)}, bf16[16,128]{1,0:T(8,128)(2,1)}, u32[]{:S(2)}) copy-start(bf16[16,128]{1,0:T(8,128)(2,1)} %up_act.1) | copy-start | bytes 12292
  46.4 23.0 %copy-start.9 = (bf16[16,128]{1,0:T(8,128)(2,1)S(1)}, bf16[16,128]{1,0:T(8,128)(2,1)}, u32[]{:S(2)}) copy-start(bf16[16,128]{1,0:T(8,128)(2,1)} %down_act.1) | copy-start | bytes 12292
  46.4 2.0 %collective-permute-start.11 = (bf16[64,1024]{1,0:T(8,128)(2,1)S(1)}, bf16[64,1024]{1,0:T(8,128)(2,1)S(1)}, u32[]{:S(2)}, u32[]{:S(2)}) collective-permute-start(bf16[64,1024]{1,0:T(8,128)(2,1)S(1)} %get-tuple-element.56.refs_1_), channel_id=1, source_target_pairs={{0,1},{1,0},{2,3},{3,2},{4,5},{5,4},{6,7},{7,6},{8,9},{9,8},{10,11... | collective-permute-start | bytes 393224 | tf_op jit(solution)/shard_map/ppermute | solution.py:282
  47.4 11.5 %collective-permute-start.15 = (bf16[32,4096]{1,0:T(8,128)(2,1)S(1)}, bf16[32,4096]{1,0:T(8,128)(2,1)S(1)}, u32[]{:S(2)}, u32[]{:S(2)}) collective-permute-start(bf16[32,4096]{1,0:T(8,128)(2,1)S(1)} %collective-permute-done.14.i2), channel_id=1, source_target_pairs={{0,4},{4,0},{8,12},{12,8},{1,5},{5,1},{9,13},{13,9},{2,6},{6,2},{1... | collective-permute-start | bytes 786440 | tf_op jit(solution)/shard_map/ppermute | solution.py:282
  54.2 13.8 %collective-permute-start.19 = (bf16[560,128]{1,0:T(8,128)(2,1)S(1)}, bf16[560,128]{1,0:T(8,128)(2,1)S(1)}, u32[]{:S(2)}, u32[]{:S(2)}) collective-permute-start(bf16[560,128]{1,0:T(8,128)(2,1)S(1)} %get-tuple-element.60), channel_id=1, source_target_pairs={{0,4},{4,0},{8,12},{12,8},{1,5},{5,1},{9,13},{13,9},{2,6},{6,2},{1... | collective-permute-start | bytes 430088 | tf_op jit(solution)/shard_map/ppermute | solution.py:282
  55.3 15.2 %collective-permute-start.20 = (bf16[560,128]{1,0:T(8,128)(2,1)S(1)}, bf16[560,128]{1,0:T(8,128)(2,1)S(1)}, u32[]{:S(2)}, u32[]{:S(2)}) collective-permute-start(bf16[560,128]{1,0:T(8,128)(2,1)S(1)} %get-tuple-element.61), channel_id=1, source_target_pairs={{0,8},{4,12},{8,0},{12,4},{1,9},{5,13},{9,1},{13,5},{2,10},{6,14},... | collective-permute-start | bytes 430088 | tf_op jit(solution)/shard_map/ppermute | solution.py:282
  57.5 13.1 %collective-permute-start.21 = (bf16[560,128]{1,0:T(8,128)(2,1)S(1)}, bf16[560,128]{1,0:T(8,128)(2,1)S(1)}, u32[]{:S(2)}, u32[]{:S(2)}) collective-permute-start(bf16[560,128]{1,0:T(8,128)(2,1)S(1)} %get-tuple-element.62), channel_id=1, source_target_pairs={{0,12},{4,8},{8,4},{12,0},{1,13},{5,9},{9,5},{13,1},{2,14},{6,10},... | collective-permute-start | bytes 430088 | tf_op jit(solution)/shard_map/ppermute | solution.py:282
  64.9 7.0 %collective-permute-start.16 = (bf16[512,128]{1,0:T(8,128)(2,1)S(1)}, bf16[512,128]{1,0:T(8,128)(2,1)S(1)}, u32[]{:S(2)}, u32[]{:S(2)}) collective-permute-start(bf16[512,128]{1,0:T(8,128)(2,1)S(1)} %get-tuple-element.67), channel_id=1, source_target_pairs={{0,4},{4,0},{8,12},{12,8},{1,5},{5,1},{9,13},{13,9},{2,6},{6,2},{1... | collective-permute-start | bytes 393224 | tf_op jit(solution)/shard_map/ppermute | solution.py:282
  65.5 15.0 %collective-permute-start.17 = (bf16[512,128]{1,0:T(8,128)(2,1)S(1)}, bf16[512,128]{1,0:T(8,128)(2,1)S(1)}, u32[]{:S(2)}, u32[]{:S(2)}) collective-permute-start(bf16[512,128]{1,0:T(8,128)(2,1)S(1)} %get-tuple-element.68), channel_id=1, source_target_pairs={{0,8},{4,12},{8,0},{12,4},{1,9},{5,13},{9,1},{13,5},{2,10},{6,14},... | collective-permute-start | bytes 393224 | tf_op jit(solution)/shard_map/ppermute | solution.py:282
  68.0 12.5 %collective-permute-start.18 = (bf16[512,128]{1,0:T(8,128)(2,1)S(1)}, bf16[512,128]{1,0:T(8,128)(2,1)S(1)}, u32[]{:S(2)}, u32[]{:S(2)}) collective-permute-start(bf16[512,128]{1,0:T(8,128)(2,1)S(1)} %get-tuple-element.69), channel_id=1, source_target_pairs={{0,12},{4,8},{8,4},{12,0},{1,13},{5,9},{9,5},{13,1},{2,14},{6,10},... | collective-permute-start | bytes 393224 | tf_op jit(solution)/shard_map/ppermute | solution.py:282

commit v6 on v5

--- a/solution.py
+++ b/solution.py
@@ -317,10 +317,10 @@
     gathered.append(swap(after(gathered[1], gate_v, up_v, near), "row", 1, 4))
     down_v = after(down_v, gate_v, up_v, near)
 
-    quarter = shape((tokens // 4, half + LANES), f32)
+    quarter = shape((tokens // 1, half + LANES), f32)
     *send, low_piece, full_gradient = call(
         functools.partial(send_kernel, half, 256),
-        (quarter,) * 4 + (shape((rank, tokens), f32), shape((tokens, width), bf16)),
+        (quarter,) * 1 + (shape((rank, tokens), f32), shape((tokens, width), bf16)),
         own_gradient,
         *gathered,
         in_vmem(down_v),

time: 81.4 us -> 80.8 us (level)
  starting transfers between devices: 25.8 us -> 24.9 us
    ppermute x22 -> x19, starting transfers between devices: 25.8 us -> 24.9 us  [swap(): return lax.ppermute(x, axis, [(i, i ^ distance) for i in range(n)])]
    ppermute x22 -> x19, waiting for transfers between devices: 11.3 us -> 11.6 us  [swap(): return lax.ppermute(x, axis, [(i, i ^ distance) for i in range(n)])]
  transfers between devices with their start and end apart: 22 -> 19, of which waited for: 4 -> 4; matrix products, arithmetic and copies ran while one was open for 0% -> 0% of each run, Pallas kernels for 47% -> 47%
where the time goes in v6:
time: 80.8 us; the launch traced here: 80.7 us
  Pallas kernels  43.2 us (53%)
  starting transfers between devices  24.9 us (31%)
  waiting for transfers between devices  11.6 us (14%)
  between operations  0.92 us (1%)
    pallas_call x17, Pallas kernels, call(): pl.pallas_call(kernel, out_shape=tuple(outs), in_specs=specs if specs is...  43.2 us
    ppermute x19, starting transfers between devices, swap(): return lax.ppermute(x, axis, [(i, i ^ distance) for i in range(n)])  24.9 us
    ppermute x19, waiting for transfers between devices, swap(): return lax.ppermute(x, axis, [(i, i ^ distance) for i in range(n)])  11.6 us
  transfers between devices with their start and end apart: 19, of which 4 were waited for; matrix products, arithmetic and copies ran while one was open for 0% of the time, Pallas kernels for 47%

profile of v6, /device:TPU:0, one launch (start us, length us, event | category | flops | bytes accessed | tf_op | source)
XLA Modules:
  0.0 80.7 jit_solution(5765518631595777312)
XLA Ops:
  0.6 3.1 %collective-permute-start.2 = (bf16[32,4096]{1,0:T(8,128)(2,1)}, bf16[32,4096]{1,0:T(8,128)(2,1)S(1)}, u32[]{:S(2)}, u32[]{:S(2)}) collective-permute-start(bf16[32,4096]{1,0:T(8,128)(2,1)} %i0.1), channel_id=1, source_target_pairs={{0,4},{4,0},{8,12},{12,8},{1,5},{5,1},{9,13},{13,9},{2,6},{6,2},{1... | collective-permute-start | bytes 786440 | tf_op jit(solution)/shard_map/ppermute | solution.py:282
  3.7 2.6 %collective-permute-start.1 = (bf16[32,4096]{1,0:T(8,128)(2,1)}, bf16[32,4096]{1,0:T(8,128)(2,1)S(1)}, u32[]{:S(2)}, u32[]{:S(2)}) collective-permute-start(bf16[32,4096]{1,0:T(8,128)(2,1)} %o0.1), channel_id=1, source_target_pairs={{0,8},{4,12},{8,0},{12,4},{1,9},{5,13},{9,1},{13,5},{2,10},{6,14},... | collective-permute-start | bytes 786440 | tf_op jit(solution)/shard_map/ppermute | solution.py:282
  6.8 3.5 %shard_map.165.refs_8_ = bf16[2048,2048]{1,0:T(8,128)(2,1)S(1)} custom-call(bf16[4096,2048]{1,0:T(8,128)(2,1)} %src.5), custom_call_target="tpu_custom_call" | custom-call | tf_op jit(solution)/shard_map/pallas_call | solution.py:46
  10.3 3.5 %shard_map.164.refs_8_ = bf16[2048,2048]{1,0:T(8,128)(2,1)S(1)} custom-call(bf16[4096,2048]{1,0:T(8,128)(2,1)} %src.5), custom_call_target="tpu_custom_call" | custom-call | tf_op jit(solution)/shard_map/pallas_call | solution.py:46
  13.8 3.5 %shard_map.166.refs_9_ = bf16[2048,2048]{1,0:T(8,128)(2,1)S(1)} custom-call(bf16[4096,2048]{1,0:T(8,128)(2,1)} %src.8), custom_call_target="tpu_custom_call" | custom-call | tf_op jit(solution)/shard_map/pallas_call | solution.py:46
  17.3 2.4 %collective-permute-start.3 = (bf16[32,4096]{1,0:T(8,128)(2,1)S(1)}, bf16[32,4096]{1,0:T(8,128)(2,1)S(1)}, u32[]{:S(2)}, u32[]{:S(2)}) collective-permute-start(bf16[32,4096]{1,0:T(8,128)(2,1)S(1)} %collective-permute-done.1.o2), channel_id=1, source_target_pairs={{0,4},{4,0},{8,12},{12,8},{1,5},{5,1},{9,13},{13,9},{2,6},{6,2},{1... | collective-permute-start | bytes 786440 | tf_op jit(solution)/shard_map/ppermute | solution.py:282
  19.8 5.9 %shard_map.167.w = bf16[2048,4096]{1,0:T(8,128)(2,1)S(1)} custom-call(bf16[2048,4096]{1,0:T(8,128)(2,1)} %src.7), custom_call_target="tpu_custom_call" | custom-call | tf_op jit(solution)/shard_map/pallas_call | solution.py:46
  25.7 1.4 %collective-permute-done.3.o3 = bf16[32,4096]{1,0:T(8,128)(2,1)S(1)} collective-permute-done((bf16[32,4096]{1,0:T(8,128)(2,1)S(1)}, bf16[32,4096]{1,0:T(8,128)(2,1)S(1)}, u32[]{:S(2)}, u32[]{:S(2)}) %collective-permute-start.3) | collective-permute-done | bytes 262176 | tf_op jit(solution)/shard_map/ppermute | solution.py:282
  27.1 4.2 %shard_map.168 = (f32[128,1152]{1,0:T(8,128)S(1)}, f32[16,128]{1,0:T(8,128)S(1)}, bf16[128,4096]{1,0:T(8,128)(2,1)S(1)}) custom-call(bf16[32,4096]{1,0:T(8,128)(2,1)S(1)} %copy-done.4, bf16[32,4096]{1,0:T(8,128)(2,1)S(1)} %collective-permute-done.o1, bf16[32,4096]{1,0:T(8,128)(2,1)S(1)} %collective-permute-done.1.o2, ...), custom_call_target="tpu_custom_call" | custom-call | tf_op jit(solution)/shard_map/pallas_call | solution.py:46
  31.4 2.9 %collective-permute-start.11 = (bf16[32,4096]{1,0:T(8,128)(2,1)S(1)}, bf16[32,4096]{1,0:T(8,128)(2,1)S(1)}, u32[]{:S(2)}, u32[]{:S(2)}) collective-permute-start(bf16[32,4096]{1,0:T(8,128)(2,1)S(1)} %copy-done.6), channel_id=1, source_target_pairs={{0,8},{4,12},{8,0},{12,4},{1,9},{5,13},{9,1},{13,5},{2,10},{6,14},... | collective-permute-start | bytes 786440 | tf_op jit(solution)/shard_map/ppermute | solution.py:282
  34.3 1.9 %shard_map.169.keep = f32[128,640]{1,0:T(8,128)S(1)} custom-call(bf16[128,4096]{1,0:T(8,128)(2,1)S(1)} %get-tuple-element.43.full, f32[16,128]{1,0:T(8,128)S(1)} %get-tuple-element.41.low, bf16[2048,4096]{1,0:T(8,128)(2,1)S(1)} %shard_map.167.w, bf16[16,2048]{1,0:T(8,128)(2,1)S(1)} %copy-done), custom_call_target="tpu_custom_call" | custom-call | tf_op jit(solution)/shard_map/pallas_call | solution.py:46
  36.2 1.6 %collective-permute-start.5 = (bf16[688,128]{1,0:T(8,128)(2,1)S(1)}, bf16[688,128]{1,0:T(8,128)(2,1)S(1)}, u32[]{:S(2)}, u32[]{:S(2)}) collective-permute-start(bf16[688,128]{1,0:T(8,128)(2,1)S(1)} %shard_map.170.mine0), channel_id=1, source_target_pairs={{0,2},{1,3},{2,0},{3,1},{4,6},{5,7},{6,4},{7,5},{8,10},{9,11},{10,... | collective-permute-start | bytes 528392 | tf_op jit(solution)/shard_map/ppermute | solution.py:282
  37.8 1.3 %shard_map.171.mine1 = bf16[384,128]{1,0:T(8,128)(2,1)S(1)} custom-call(bf16[128,4096]{1,0:T(8,128)(2,1)S(1)} %get-tuple-element.43.full, f32[16,128]{1,0:T(8,128)S(1)} %get-tuple-element.41.low, bf16[2048,4096]{1,0:T(8,128)(2,1)S(1)} %shard_map.167.w, bf16[16,2048]{1,0:T(8,128)(2,1)S(1)} %copy-done, f32[128,1152]{1,0:T(8,128)S(1)} %collective-permute-done.4.rest_0_), custom_call_target="tpu_custom_call" | custom-call | tf_op jit(solution)/shard_map/pallas_call | solution.py:46
  39.1 0.6 collective-permute-start.6
  39.7 3.5 %shard_map.173.refs_9_ = bf16[2048,2048]{1,0:T(8,128)(2,1)S(1)} custom-call(bf16[4096,2048]{1,0:T(8,128)(2,1)} %src.8), custom_call_target="tpu_custom_call" | custom-call | tf_op jit(solution)/shard_map/pallas_call | solution.py:46
  43.2 0.6 shard_map.172
  43.9 1.1 %collective-permute-done.6.other1 = bf16[384,128]{1,0:T(8,128)(2,1)S(1)} collective-permute-done((bf16[384,128]{1,0:T(8,128)(2,1)S(1)}, bf16[384,128]{1,0:T(8,128)(2,1)S(1)}, u32[]{:S(2)}, u32[]{:S(2)}) %collective-permute-start.6) | collective-permute-done | bytes 98336 | tf_op jit(solution)/shard_map/ppermute | solution.py:282
  45.2 0.5 collective-permute-start.8
  46.2 0.6 collective-permute-done.11.i2
  46.8 1.0 %collective-permute-start.12 = (bf16[32,4096]{1,0:T(8,128)(2,1)S(1)}, bf16[32,4096]{1,0:T(8,128)(2,1)S(1)}, u32[]{:S(2)}, u32[]{:S(2)}) collective-permute-start(bf16[32,4096]{1,0:T(8,128)(2,1)S(1)} %collective-permute-done.11.i2), channel_id=1, source_target_pairs={{0,4},{4,0},{8,12},{12,8},{1,5},{5,1},{9,13},{13,9},{2,6},{6,2},{1... | collective-permute-start | bytes 786440 | tf_op jit(solution)/shard_map/ppermute | solution.py:282
  47.8 5.8 %shard_map.175 = (f32[32,2048]{1,0:T(8,128)S(1)}, bf16[560,128]{1,0:T(8,128)(2,1)S(1)}, bf16[560,128]{1,0:T(8,128)(2,1)S(1)}, bf16[560,128]{1,0:T(8,128)(2,1)S(1)}, f32[16,128]{1,0:T(8,128)S(1)}) custom-call(bf16[64,1024]{1,0:T(8,128)(2,1)S(1)} %get-tuple-element.49.refs_0_, bf16[64,1024]{1,0:T(8,128)(2,1)S(1)} %get-tuple-element.50.refs_1_, ...), custom_call_target="tpu_custom_call" | custom-call | tf_op jit(solution)/shard_map/pallas_call | solution.py:46
  53.6 1.1 %collective-permute-start.16 = (bf16[560,128]{1,0:T(8,128)(2,1)S(1)}, bf16[560,128]{1,0:T(8,128)(2,1)S(1)}, u32[]{:S(2)}, u32[]{:S(2)}) collective-permute-start(bf16[560,128]{1,0:T(8,128)(2,1)S(1)} %get-tuple-element.54), channel_id=1, source_target_pairs={{0,4},{4,0},{8,12},{12,8},{1,5},{5,1},{9,13},{13,9},{2,6},{6,2},{1... | collective-permute-start | bytes 430088 | tf_op jit(solution)/shard_map/ppermute | solution.py:282
  54.7 2.2 %collective-permute-start.17 = (bf16[560,128]{1,0:T(8,128)(2,1)S(1)}, bf16[560,128]{1,0:T(8,128)(2,1)S(1)}, u32[]{:S(2)}, u32[]{:S(2)}) collective-permute-start(bf16[560,128]{1,0:T(8,128)(2,1)S(1)} %get-tuple-element.55), channel_id=1, source_target_pairs={{0,8},{4,12},{8,0},{12,4},{1,9},{5,13},{9,1},{13,5},{2,10},{6,14},... | collective-permute-start | bytes 430088 | tf_op jit(solution)/shard_map/ppermute | solution.py:282
  56.9 1.4 %collective-permute-start.18 = (bf16[560,128]{1,0:T(8,128)(2,1)S(1)}, bf16[560,128]{1,0:T(8,128)(2,1)S(1)}, u32[]{:S(2)}, u32[]{:S(2)}) collective-permute-start(bf16[560,128]{1,0:T(8,128)(2,1)S(1)} %get-tuple-element.56), channel_id=1, source_target_pairs={{0,12},{4,8},{8,4},{12,0},{1,13},{5,9},{9,5},{13,1},{2,14},{6,10},... | collective-permute-start | bytes 430088 | tf_op jit(solution)/shard_map/ppermute | solution.py:282
  58.3 6.0 %shard_map.176 = (f32[32,2048]{1,0:T(8,128)S(1)}, bf16[512,128]{1,0:T(8,128)(2,1)S(1)}, bf16[512,128]{1,0:T(8,128)(2,1)S(1)}, bf16[512,128]{1,0:T(8,128)(2,1)S(1)}) custom-call(bf16[64,1024]{1,0:T(8,128)(2,1)S(1)} %get-tuple-element.49.refs_0_, bf16[64,1024]{1,0:T(8,128)(2,1)S(1)} %get-tuple-element.50.refs_1_, ...), custom_call_target="tpu_custom_call" | custom-call | tf_op jit(solution)/shard_map/pallas_call | solution.py:46
  64.3 0.6 collective-permute-start.13
  64.9 2.4 %collective-permute-start.14 = (bf16[512,128]{1,0:T(8,128)(2,1)S(1)}, bf16[512,128]{1,0:T(8,128)(2,1)S(1)}, u32[]{:S(2)}, u32[]{:S(2)}) collective-permute-start(bf16[512,128]{1,0:T(8,128)(2,1)S(1)} %get-tuple-element.62), channel_id=1, source_target_pairs={{0,8},{4,12},{8,0},{12,4},{1,9},{5,13},{9,1},{13,5},{2,10},{6,14},... | collective-permute-start | bytes 393224 | tf_op jit(solution)/shard_map/ppermute | solution.py:282
  67.4 1.4 %collective-permute-start.15 = (bf16[512,128]{1,0:T(8,128)(2,1)S(1)}, bf16[512,128]{1,0:T(8,128)(2,1)S(1)}, u32[]{:S(2)}, u32[]{:S(2)}) collective-permute-start(bf16[512,128]{1,0:T(8,128)(2,1)S(1)} %get-tuple-element.63), channel_id=1, source_target_pairs={{0,12},{4,8},{8,4},{12,0},{1,13},{5,9},{9,5},{13,1},{2,14},{6,10},... | collective-permute-start | bytes 393224 | tf_op jit(solution)/shard_map/ppermute | solution.py:282
  68.8 1.2 %shard_map.180 = (f32[16,2048]{1,0:T(8,128)}, f32[16,2048]{1,0:T(8,128)}, f32[16,4096]{1,0:T(8,128)}) custom-call(bf16[64,1024]{1,0:T(8,128)(2,1)S(1)} %get-tuple-element.51.refs_2_.own0, bf16[64,1024]{1,0:T(8,128)(2,1)S(1)} %get-tuple-element.52.refs_3_.own1, bf16[64,1024]{1,0:T(8,128)(2,1)S(1)} %collective-permute-done.9.refs_6_.mate0, ...), custom_call_target="tpu_custom_call" | custom-call | tf_op jit(solution)/shard_map/pallas_call | solution.py:46
  70.0 1.3 %shard_map.179 = f32[16,4096]{1,0:T(8,128)} custom-call(f32[16,128]{1,0:T(8,128)S(1)} %get-tuple-element.65.low, bf16[560,128]{1,0:T(8,128)(2,1)S(1)} %collective-permute-done.16.r1, bf16[560,128]{1,0:T(8,128)(2,1)S(1)} %collective-permute-done.17.r2, bf16[560,128]{1,0:T(8,128)(2,1)S(1)} %collective-permute-done.18.r3, bf16[32,4096]{1,0:T(8,128)(2,1)S(1)} %copy-done.6, ...), custom_call_target="tpu_custom_call" | custom-call | tf_op jit(solution)/shard_map/pallas_call | solution.py:46
  71.4 8.6 %collective-permute-done.14.r2 = bf16[512,128]{1,0:T(8,128)(2,1)S(1)} collective-permute-done((bf16[512,128]{1,0:T(8,128)(2,1)S(1)}, bf16[512,128]{1,0:T(8,128)(2,1)S(1)}, u32[]{:S(2)}, u32[]{:S(2)}) %collective-permute-start.14) | collective-permute-done | bytes 131104 | tf_op jit(solution)/shard_map/ppermute | solution.py:282
  79.9 0.8 shard_map.178
  (43 shorter events, 1.5 us)
Async XLA Ops:
  0.6 16.7 %collective-permute-start.2 = (bf16[32,4096]{1,0:T(8,128)(2,1)}, bf16[32,4096]{1,0:T(8,128)(2,1)S(1)}, u32[]{:S(2)}, u32[]{:S(2)}) collective-permute-start(bf16[32,4096]{1,0:T(8,128)(2,1)} %i0.1), channel_id=1, source_target_pairs={{0,4},{4,0},{8,12},{12,8},{1,5},{5,1},{9,13},{13,9},{2,6},{6,2},{1... | collective-permute-start | bytes 786440 | tf_op jit(solution)/shard_map/ppermute | solution.py:282
  3.7 13.6 %collective-permute-start.1 = (bf16[32,4096]{1,0:T(8,128)(2,1)}, bf16[32,4096]{1,0:T(8,128)(2,1)S(1)}, u32[]{:S(2)}, u32[]{:S(2)}) collective-permute-start(bf16[32,4096]{1,0:T(8,128)(2,1)} %o0.1), channel_id=1, source_target_pairs={{0,8},{4,12},{8,0},{12,4},{1,9},{5,13},{9,1},{13,5},{2,10},{6,14},... | collective-permute-start | bytes 786440 | tf_op jit(solution)/shard_map/ppermute | solution.py:282
  6.3 19.4 %collective-permute-start = (bf16[32,4096]{1,0:T(8,128)(2,1)}, bf16[32,4096]{1,0:T(8,128)(2,1)S(1)}, u32[]{:S(2)}, u32[]{:S(2)}) collective-permute-start(bf16[32,4096]{1,0:T(8,128)(2,1)} %o0.1), channel_id=1, source_target_pairs={{0,4},{4,0},{8,12},{12,8},{1,5},{5,1},{9,13},{13,9},{2,6},{6,2},{1... | collective-permute-start | bytes 786440 | tf_op jit(solution)/shard_map/ppermute | solution.py:282
  17.3 9.8 %copy-start = (bf16[16,2048]{1,0:T(8,128)(2,1)S(1)}, bf16[16,2048]{1,0:T(8,128)(2,1)}, u32[]{:S(2)}) copy-start(bf16[16,2048]{1,0:T(8,128)(2,1)} %entry.5) | copy-start | bytes 196612
  17.3 9.8 %copy-start.4 = (bf16[32,4096]{1,0:T(8,128)(2,1)S(1)}, bf16[32,4096]{1,0:T(8,128)(2,1)}, u32[]{:S(2)}) copy-start(bf16[32,4096]{1,0:T(8,128)(2,1)} %o0.1) | copy-start | bytes 786436
  17.3 9.8 %copy-start.7 = (bf16[16,4096]{1,0:T(8,128)(2,1)S(1)}, bf16[16,4096]{1,0:T(8,128)(2,1)}, u32[]{:S(2)}) copy-start(bf16[16,4096]{1,0:T(8,128)(2,1)} %exit_ref.1) | copy-start | bytes 393220
  17.3 9.7 %collective-permute-start.3 = (bf16[32,4096]{1,0:T(8,128)(2,1)S(1)}, bf16[32,4096]{1,0:T(8,128)(2,1)S(1)}, u32[]{:S(2)}, u32[]{:S(2)}) collective-permute-start(bf16[32,4096]{1,0:T(8,128)(2,1)S(1)} %collective-permute-done.1.o2), channel_id=1, source_target_pairs={{0,4},{4,0},{8,12},{12,8},{1,5},{5,1},{9,13},{13,9},{2,6},{6,2},{1... | collective-permute-start | bytes 786440 | tf_op jit(solution)/shard_map/ppermute | solution.py:282
  25.7 5.7 %copy-start.6 = (bf16[32,4096]{1,0:T(8,128)(2,1)S(1)}, bf16[32,4096]{1,0:T(8,128)(2,1)}, u32[]{:S(2)}) copy-start(bf16[32,4096]{1,0:T(8,128)(2,1)} %i0.1) | copy-start | bytes 786436
  31.3 4.9 %collective-permute-start.4 = (f32[128,1152]{1,0:T(8,128)S(1)}, f32[128,1152]{1,0:T(8,128)S(1)}, u32[]{:S(2)}, u32[]{:S(2)}) collective-permute-start(f32[128,1152]{1,0:T(8,128)S(1)} %get-tuple-element.42), channel_id=1, source_target_pairs={{0,1},{1,0},{2,3},{3,2},{4,5},{5,4},{6,7},{7,6},{8,9},{9,8},{10,11... | collective-permute-start | bytes 1769480 | tf_op jit(solution)/shard_map/ppermute | solution.py:282
  31.4 15.4 %collective-permute-start.11 = (bf16[32,4096]{1,0:T(8,128)(2,1)S(1)}, bf16[32,4096]{1,0:T(8,128)(2,1)S(1)}, u32[]{:S(2)}, u32[]{:S(2)}) collective-permute-start(bf16[32,4096]{1,0:T(8,128)(2,1)S(1)} %copy-done.6), channel_id=1, source_target_pairs={{0,8},{4,12},{8,0},{12,4},{1,9},{5,13},{9,1},{13,5},{2,10},{6,14},... | collective-permute-start | bytes 786440 | tf_op jit(solution)/shard_map/ppermute | solution.py:282
  36.2 8.7 %collective-permute-start.5 = (bf16[688,128]{1,0:T(8,128)(2,1)S(1)}, bf16[688,128]{1,0:T(8,128)(2,1)S(1)}, u32[]{:S(2)}, u32[]{:S(2)}) collective-permute-start(bf16[688,128]{1,0:T(8,128)(2,1)S(1)} %shard_map.170.mine0), channel_id=1, source_target_pairs={{0,2},{1,3},{2,0},{3,1},{4,6},{5,7},{6,4},{7,5},{8,10},{9,11},{10,... | collective-permute-start | bytes 528392 | tf_op jit(solution)/shard_map/ppermute | solution.py:282
  39.1 4.1 %copy-start.2 = (bf16[128,2048]{1,0:T(8,128)(2,1)S(1)}, bf16[128,2048]{1,0:T(8,128)(2,1)}, u32[]{:S(2)}) copy-start(bf16[128,2048]{1,0:T(8,128)(2,1)} %g_ref) | copy-start | bytes 1572868
  39.1 4.1 %copy-start.3 = (bf16[128,2048]{1,0:T(8,128)(2,1)S(1)}, bf16[128,2048]{1,0:T(8,128)(2,1)}, u32[]{:S(2)}) copy-start(bf16[128,2048]{1,0:T(8,128)(2,1)} %u_ref.1) | copy-start | bytes 1572868
  39.1 8.7 %copy-start.1 = (bf16[16,4096]{1,0:T(8,128)(2,1)S(1)}, bf16[16,4096]{1,0:T(8,128)(2,1)}, u32[]{:S(2)}) copy-start(bf16[16,4096]{1,0:T(8,128)(2,1)} %refs_11_.3) | copy-start | bytes 393220
  39.1 8.7 %copy-start.5 = (bf16[16,2048]{1,0:T(8,128)(2,1)S(1)}, bf16[16,2048]{1,0:T(8,128)(2,1)}, u32[]{:S(2)}) copy-start(bf16[16,2048]{1,0:T(8,128)(2,1)} %refs_10_.3) | copy-start | bytes 196612
  39.1 5.8 %collective-permute-start.6 = (bf16[384,128]{1,0:T(8,128)(2,1)S(1)}, bf16[384,128]{1,0:T(8,128)(2,1)S(1)}, u32[]{:S(2)}, u32[]{:S(2)}) collective-permute-start(bf16[384,128]{1,0:T(8,128)(2,1)S(1)} %shard_map.171.mine1), channel_id=1, source_target_pairs={{0,2},{1,3},{2,0},{3,1},{4,6},{5,7},{6,4},{7,5},{8,10},{9,11},{10,... | collective-permute-start | bytes 294920 | tf_op jit(solution)/shard_map/ppermute | solution.py:282
  45.1 2.6 %collective-permute-start.7 = (bf16[64,1024]{1,0:T(8,128)(2,1)S(1)}, bf16[64,1024]{1,0:T(8,128)(2,1)S(1)}, u32[]{:S(2)}, u32[]{:S(2)}) collective-permute-start(bf16[64,1024]{1,0:T(8,128)(2,1)S(1)} %get-tuple-element.49.refs_0_), channel_id=1, source_target_pairs={{0,1},{1,0},{2,3},{3,2},{4,5},{5,4},{6,7},{7,6},{8,9},{9,8},{10,11... | collective-permute-start | bytes 393224 | tf_op jit(solution)/shard_map/ppermute | solution.py:282
  45.2 2.6 %collective-permute-start.8 = (bf16[64,1024]{1,0:T(8,128)(2,1)S(1)}, bf16[64,1024]{1,0:T(8,128)(2,1)S(1)}, u32[]{:S(2)}, u32[]{:S(2)}) collective-permute-start(bf16[64,1024]{1,0:T(8,128)(2,1)S(1)} %get-tuple-element.50.refs_1_), channel_id=1, source_target_pairs={{0,1},{1,0},{2,3},{3,2},{4,5},{5,4},{6,7},{7,6},{8,9},{9,8},{10,11... | collective-permute-start | bytes 393224 | tf_op jit(solution)/shard_map/ppermute | solution.py:282
  45.7 2.1 %collective-permute-start.9 = (bf16[64,1024]{1,0:T(8,128)(2,1)S(1)}, bf16[64,1024]{1,0:T(8,128)(2,1)S(1)}, u32[]{:S(2)}, u32[]{:S(2)}) collective-permute-start(bf16[64,1024]{1,0:T(8,128)(2,1)S(1)} %get-tuple-element.51.refs_2_.own0), channel_id=1, source_target_pairs={{0,1},{1,0},{2,3},{3,2},{4,5},{5,4},{6,7},{7,6},{8,9},{9,8},{10,11... | collective-permute-start | bytes 393224 | tf_op jit(solution)/shard_map/ppermute | solution.py:282
  45.8 23.0 %copy-start.8 = (bf16[16,128]{1,0:T(8,128)(2,1)S(1)}, bf16[16,128]{1,0:T(8,128)(2,1)}, u32[]{:S(2)}) copy-start(bf16[16,128]{1,0:T(8,128)(2,1)} %up_act.1) | copy-start | bytes 12292
  45.8 23.0 %copy-start.9 = (bf16[16,128]{1,0:T(8,128)(2,1)S(1)}, bf16[16,128]{1,0:T(8,128)(2,1)}, u32[]{:S(2)}) copy-start(bf16[16,128]{1,0:T(8,128)(2,1)} %down_act.1) | copy-start | bytes 12292
  45.8 2.0 %collective-permute-start.10 = (bf16[64,1024]{1,0:T(8,128)(2,1)S(1)}, bf16[64,1024]{1,0:T(8,128)(2,1)S(1)}, u32[]{:S(2)}, u32[]{:S(2)}) collective-permute-start(bf16[64,1024]{1,0:T(8,128)(2,1)S(1)} %get-tuple-element.52.refs_3_.own1), channel_id=1, source_target_pairs={{0,1},{1,0},{2,3},{3,2},{4,5},{5,4},{6,7},{7,6},{8,9},{9,8},{10,11... | collective-permute-start | bytes 393224 | tf_op jit(solution)/shard_map/ppermute | solution.py:282
  46.8 11.5 %collective-permute-start.12 = (bf16[32,4096]{1,0:T(8,128)(2,1)S(1)}, bf16[32,4096]{1,0:T(8,128)(2,1)S(1)}, u32[]{:S(2)}, u32[]{:S(2)}) collective-permute-start(bf16[32,4096]{1,0:T(8,128)(2,1)S(1)} %collective-permute-done.11.i2), channel_id=1, source_target_pairs={{0,4},{4,0},{8,12},{12,8},{1,5},{5,1},{9,13},{13,9},{2,6},{6,2},{1... | collective-permute-start | bytes 786440 | tf_op jit(solution)/shard_map/ppermute | solution.py:282
  53.6 13.8 %collective-permute-start.16 = (bf16[560,128]{1,0:T(8,128)(2,1)S(1)}, bf16[560,128]{1,0:T(8,128)(2,1)S(1)}, u32[]{:S(2)}, u32[]{:S(2)}) collective-permute-start(bf16[560,128]{1,0:T(8,128)(2,1)S(1)} %get-tuple-element.54), channel_id=1, source_target_pairs={{0,4},{4,0},{8,12},{12,8},{1,5},{5,1},{9,13},{13,9},{2,6},{6,2},{1... | collective-permute-start | bytes 430088 | tf_op jit(solution)/shard_map/ppermute | solution.py:282
  54.7 15.2 %collective-permute-start.17 = (bf16[560,128]{1,0:T(8,128)(2,1)S(1)}, bf16[560,128]{1,0:T(8,128)(2,1)S(1)}, u32[]{:S(2)}, u32[]{:S(2)}) collective-permute-start(bf16[560,128]{1,0:T(8,128)(2,1)S(1)} %get-tuple-element.55), channel_id=1, source_target_pairs={{0,8},{4,12},{8,0},{12,4},{1,9},{5,13},{9,1},{13,5},{2,10},{6,14},... | collective-permute-start | bytes 430088 | tf_op jit(solution)/shard_map/ppermute | solution.py:282
  56.9 13.0 %collective-permute-start.18 = (bf16[560,128]{1,0:T(8,128)(2,1)S(1)}, bf16[560,128]{1,0:T(8,128)(2,1)S(1)}, u32[]{:S(2)}, u32[]{:S(2)}) collective-permute-start(bf16[560,128]{1,0:T(8,128)(2,1)S(1)} %get-tuple-element.56), channel_id=1, source_target_pairs={{0,12},{4,8},{8,4},{12,0},{1,13},{5,9},{9,5},{13,1},{2,14},{6,10},... | collective-permute-start | bytes 430088 | tf_op jit(solution)/shard_map/ppermute | solution.py:282
  64.3 7.0 %collective-permute-start.13 = (bf16[512,128]{1,0:T(8,128)(2,1)S(1)}, bf16[512,128]{1,0:T(8,128)(2,1)S(1)}, u32[]{:S(2)}, u32[]{:S(2)}) collective-permute-start(bf16[512,128]{1,0:T(8,128)(2,1)S(1)} %get-tuple-element.61), channel_id=1, source_target_pairs={{0,4},{4,0},{8,12},{12,8},{1,5},{5,1},{9,13},{13,9},{2,6},{6,2},{1... | collective-permute-start | bytes 393224 | tf_op jit(solution)/shard_map/ppermute | solution.py:282
  64.9 15.0 %collective-permute-start.14 = (bf16[512,128]{1,0:T(8,128)(2,1)S(1)}, bf16[512,128]{1,0:T(8,128)(2,1)S(1)}, u32[]{:S(2)}, u32[]{:S(2)}) collective-permute-start(bf16[512,128]{1,0:T(8,128)(2,1)S(1)} %get-tuple-element.62), channel_id=1, source_target_pairs={{0,8},{4,12},{8,0},{12,4},{1,9},{5,13},{9,1},{13,5},{2,10},{6,14},... | collective-permute-start | bytes 393224 | tf_op jit(solution)/shard_map/ppermute | solution.py:282
  67.4 12.5 %collective-permute-start.15 = (bf16[512,128]{1,0:T(8,128)(2,1)S(1)}, bf16[512,128]{1,0:T(8,128)(2,1)S(1)}, u32[]{:S(2)}, u32[]{:S(2)}) collective-permute-start(bf16[512,128]{1,0:T(8,128)(2,1)S(1)} %get-tuple-element.63), channel_id=1, source_target_pairs={{0,12},{4,8},{8,4},{12,0},{1,13},{5,9},{9,5},{13,1},{2,14},{6,10},... | collective-permute-start | bytes 393224 | tf_op jit(solution)/shard_map/ppermute | solution.py:282
